TPU v7x, 32 devices: a whole 2x2x4 slice. The times are simulated.
32 devices in a mesh: dp: 16 (over z, y, core), tensor: 2 (over x).
Axes of the slice: x: 2, y: 2, z: 4, core: 2. Of those that a mesh axis runs over, the one named last changes fastest.
Arguments:
- tokens: bfloat16 [2048, 16, 1024], P('tensor', 'dp'), may hold values from -6 to 6
- lengths: int32 [16], P('dp'), may hold values from 512 to 2048, as said below
- cotangent: bfloat16 [2048, 16, 1024], P('tensor', 'dp'), may hold values from -16 to 16
- w_query: bfloat16 [1024, 1024], P(None, 'tensor'), may hold values from -0.1875 to 0.1875
- w_key: bfloat16 [1024, 1024], P(None, 'tensor'), may hold values from -0.1875 to 0.1875
- w_value: bfloat16 [1024, 1024], P(None, 'tensor'), may hold values from -0.1875 to 0.1875
- w_out: bfloat16 [1024, 1024], P('tensor'), may hold values from -0.1875 to 0.1875
- up_weight: bfloat16 [1024, 4096], P(None, 'tensor'), may hold values from -0.1875 to 0.1875
- bias_up: bfloat16 [4096], P('tensor'), may hold values from -3 to 3
- down_weight: bfloat16 [4096, 1024], P('tensor'), may hold values from -0.09375 to 0.09375
- bias_down: bfloat16 [1024], replicated, may hold values from -3 to 3
- norm_gains: float32 [4, 1024], replicated, may hold values from 0.1 to 1.9
- norm_shifts: float32 [4, 1024], replicated, may hold values from -3 to 3
Outputs:
- layer_out: bfloat16 [2048, 16, 1024], P('tensor', 'dp')
- grad_tokens: bfloat16 [2048, 16, 1024], P('tensor', 'dp')
- grad_query: float32 [1024, 1024], P(None, 'tensor')
- grad_key: float32 [1024, 1024], P(None, 'tensor')
- grad_value: float32 [1024, 1024], P(None, 'tensor')
- grad_out: float32 [1024, 1024], P('tensor')
- grad_up: float32 [1024, 4096], P(None, 'tensor')
- grad_bias_up: float32 [4096], P('tensor')
- down_weight_gradient: float32 [4096, 1024], P('tensor')
- grad_bias_down: float32 [1024], replicated
- grad_gains: float32 [4, 1024], replicated
- grad_shifts: float32 [4, 1024], replicated
Inputs may be any that keep to these rules, and one draw needn't show every extreme that they name: Row b's valid tokens are its first lengths[b] slots; in every draw some row has exactly 2048 and some row exactly 512.
All inputs are finite; a program needn't handle non-finite values.
Results may differ from a plain program's by a relative error of at most 0.02.
Values may be sent and summed in bfloat16 or wider, within the bound.
A program may use at most 320 MiB of HBM per device.

v0:
```python
import functools
import jax
import jax.numpy as jnp
from jax import lax
from jax.experimental import pallas as pl
from jax.experimental.pallas import tpu as pltpu
from jax.sharding import PartitionSpec as P

HD = 64
EPSILON = 1e-05
BF = jnp.bfloat16
F32 = jnp.float32
NT = (((1,), (1,)), ((), ()))
NN = (((1,), (0,)), ((), ()))
TN = (((0,), (0,)), ((), ()))
MIB = 1 << 20


def dotg(a, b, dims=NN):
    return lax.dot_general(a, b, dims, preferred_element_type=F32)


def rotate(x, cos, sin):
    first = lax.broadcasted_iota(jnp.int32, (x.shape[0], 128), 1) % HD < HD // 2
    parts = []
    for a in range(0, x.shape[1], 128):
        v = x[:, a : a + 128]
        swapped = jnp.where(first, pltpu.roll(v, 96, 1), pltpu.roll(v, 32, 1))
        parts.append(v * cos + swapped * sin)
    return jnp.concatenate(parts, axis=1) if len(parts) > 1 else parts[0]


def qkv_kernel(x_ref, wq_ref, wk_ref, wv_ref, cos_ref, sin_ref, o_ref):
    width = wq_ref.shape[1]
    x, cos, sin = x_ref[...], cos_ref[...], sin_ref[...]
    o_ref[:, :width] = rotate(dotg(x, wq_ref[...]), cos, sin).astype(BF)
    o_ref[:, width : 2 * width] = rotate(dotg(x, wk_ref[...]), cos, sin).astype(BF)
    o_ref[:, 2 * width :] = dotg(x, wv_ref[...]).astype(BF)


def project(where, x, w_query, w_key, w_value, cos, sin, joint=None, blk=256):
    rows, depth = x.shape
    width, slots = w_query.shape[1], cos.shape[0]
    blk = min(blk, rows)
    count = rows // blk
    weight = pl.BlockSpec((depth, width), lambda i, at: (0, 0))
    angle = pl.BlockSpec((blk, 128), lambda i, at: (at[0] * count + i, 0))
    kernel = lambda at, *refs: qkv_kernel(*refs[:6], refs[-1])
    held = [] if joint is None else [joint]
    return pl.pallas_call(
        kernel,
        grid_spec=pltpu.PrefetchScalarGridSpec(
            num_scalar_prefetch=1,
            grid=(count,),
            in_specs=[pl.BlockSpec((blk, depth), lambda i, at: (i, 0)), weight, weight, weight, angle, angle]
            + [pl.BlockSpec(memory_space=pl.ANY)] * len(held),
            out_specs=pl.BlockSpec((blk, 3 * width), lambda i, at: (at[0] * count + i, 0)),
        ),
        out_shape=jax.ShapeDtypeStruct((slots, 3 * width), BF),
        input_output_aliases={7: 0} if held else {},
        compiler_params=pltpu.CompilerParams(vmem_limit_bytes=60 * MIB),
        cost_estimate=pl.CostEstimate(flops=rows * depth, bytes_accessed=rows * depth, transcendentals=0),
        name="project",
    )(where, x, w_query, w_key, w_value, cos, sin, *held)


def attend_kernel(at_ref, len_ref, q_ref, k_ref, v_ref, w_ref, *refs, blk):
    o_ref, lse_ref, share_ref, vt, low_ref = refs[-5:]
    pair = pl.program_id(0)
    i = at_ref[0]
    length = len_ref[0]
    def turn(j, _):
        part = pl.ds(pl.multiple_of(j * blk, blk), blk)
        vt[:, part] = jnp.transpose(v_ref[part, :])
        return 0

    lax.fori_loop(0, i + 1, turn, 0)
    lane = lax.broadcasted_iota(jnp.int32, (blk, 128), 1)
    q = q_ref[...] * jnp.asarray(0.125, BF)
    zero = jnp.zeros_like(q)
    qs = (jnp.where(lane < HD, q, zero), jnp.where(lane < HD, zero, q))

    def step(j, carry, diag):
        start = pl.multiple_of(j * blk, blk)
        kb = k_ref[pl.ds(start, blk), :]
        out = []
        for h in range(2):
            m, l, acc = carry[h]
            s = dotg(kb, qs[h], NT)
            if diag:
                key = lax.broadcasted_iota(jnp.int32, (blk, blk), 0)
                qry = lax.broadcasted_iota(jnp.int32, (blk, blk), 1)
                s = jnp.where((key <= qry) & (key + start < length), s, -1e30)
            mn = jnp.maximum(m, jnp.max(s, axis=0, keepdims=True))
            p = jnp.exp(s - mn)
            al = jnp.exp(m - mn)
            l = l * al + jnp.sum(p, axis=0, keepdims=True)
            vb = vt[HD * h : HD * h + HD, pl.ds(start, blk)]
            acc = acc * al + dotg(vb, p.astype(BF))
            out.append((mn, l, acc))
        return tuple(out)

    init = tuple(
        (jnp.full((1, blk), -1e30, F32), jnp.zeros((1, blk), F32), jnp.zeros((HD, blk), F32))
        for _ in range(2)
    )
    c = lax.fori_loop(0, i, lambda j, c: step(j, c, False), init)
    c = step(i, c, True)
    ot = jnp.concatenate([c[h][2] / c[h][1] for h in range(2)], axis=0)
    low = jnp.transpose(ot).astype(BF)
    o_ref[...] = low
    lse_ref[0] = jnp.concatenate([c[h][0] + jnp.log(c[h][1]) for h in range(2)], axis=0)
    low_ref[pair] = low

    @pl.when(pair == pl.num_programs(0) - 1)
    def _():
        pairs = low_ref.shape[0]
        low = jnp.concatenate([low_ref[p] for p in range(pairs)], axis=1)
        share_ref[...] = dotg(low, w_ref[...]).astype(share_ref.dtype)


def attend(at, length, joint, w_out, held, kind, blk):
    rows, width, depth = joint.shape[0], w_out.shape[0], w_out.shape[1]
    pairs = width // 128
    return pl.pallas_call(
        functools.partial(attend_kernel, blk=blk),
        grid_spec=pltpu.PrefetchScalarGridSpec(
            num_scalar_prefetch=2,
            grid=(pairs,),
            in_specs=[
                pl.BlockSpec((blk, 128), lambda p, at, *_: (at[0], p)),
                pl.BlockSpec((rows, 128), lambda p, *_: (0, pairs + p)),
                pl.BlockSpec((rows, 128), lambda p, *_: (0, 2 * pairs + p)),
                pl.BlockSpec((width, depth), lambda p, *_: (0, 0), pipeline_mode=pl.Buffered(1)),
            ]
            + [pl.BlockSpec(memory_space=pl.ANY)] * len(held),
            out_specs=[
                pl.BlockSpec((blk, 128), lambda p, at, *_: (at[0], p)),
                pl.BlockSpec((1, 2, blk), lambda p, at, *_: (p, 0, at[0])),
                pl.BlockSpec((blk, depth), lambda p, *_: (0, 0)),
            ],
            scratch_shapes=[pltpu.VMEM((128, rows), BF), pltpu.VMEM((pairs, blk, 128), BF)],
        ),
        out_shape=[
            jax.ShapeDtypeStruct((rows, width), BF),
            jax.ShapeDtypeStruct((pairs, 2, rows), F32),
            jax.ShapeDtypeStruct((blk, depth), kind),
        ],
        input_output_aliases={6: 0, 7: 1} if held else {},
        compiler_params=pltpu.CompilerParams(vmem_limit_bytes=60 * MIB),
        cost_estimate=pl.CostEstimate(flops=rows * width, bytes_accessed=rows * width, transcendentals=0),
        name="attend",
    )(at, length, joint, joint, joint, w_out, *held)


def attend_back_kernel(
    len_ref, q_ref, k_ref, v_ref, o_ref, do_ref, lse_ref, cos_ref, sin_ref,
    dq_ref, dk_ref, dv_ref, kt, dlt, dqt, *, blk, blocks,
):
    j = pl.program_id(1)
    length = len_ref[0]

    @pl.when(j == 0)
    def _():
        kt[...] = jnp.transpose(k_ref[...])
        dqt[...] = jnp.zeros_like(dqt)

        def body(i, _):
            at = pl.ds(pl.multiple_of(i * blk, blk), blk)
            both = jnp.transpose(do_ref[at, :].astype(F32) * o_ref[at, :].astype(F32))
            for h in range(2):
                dlt[h : h + 1, at] = jnp.sum(both[HD * h : HD * h + HD], axis=0, keepdims=True)
            return 0

        lax.fori_loop(0, blocks, body, 0)

    js = pl.multiple_of(j * blk, blk)
    lane = lax.broadcasted_iota(jnp.int32, (blk, 128), 1)
    kb = k_ref[pl.ds(js, blk), :] * jnp.asarray(0.125, BF)
    vb = v_ref[pl.ds(js, blk), :]
    zero = jnp.zeros_like(kb)
    ks = (jnp.where(lane < HD, kb, zero), jnp.where(lane < HD, zero, kb))
    vs = (jnp.where(lane < HD, vb, zero), jnp.where(lane < HD, zero, vb))

    def step(i, carry, diag):
        at = pl.ds(pl.multiple_of(i * blk, blk), blk)
        qb, dob = q_ref[at, :], do_ref[at, :]
        out = []
        for h in range(2):
            dk, dv = carry[h]
            s = dotg(ks[h], qb, NT)
            if diag:
                key = lax.broadcasted_iota(jnp.int32, (blk, blk), 0)
                qry = lax.broadcasted_iota(jnp.int32, (blk, blk), 1)
                s = jnp.where((key <= qry) & (key + js < length), s, -1e30)
            p = jnp.exp(s - lse_ref[0, h : h + 1, at])
            dp = dotg(vs[h], dob, NT)
            ds = (p * (dp - dlt[h : h + 1, at])).astype(BF)
            dv = dv + dotg(p.astype(BF), dob)
            dk = dk + dotg(ds, qb)
            dqt[HD * h : HD * h + HD, at] += dotg(kt[HD * h : HD * h + HD, pl.ds(js, blk)], ds)
            out.append((dk, dv))
        return tuple(out)

    z = jnp.zeros((blk, 128), F32)
    c = step(j, ((z, z), (z, z)), True)
    c = lax.fori_loop(j + 1, blocks, lambda i, c: step(i, c, False), c)
    grad = jnp.where(lane < HD, c[0][0], c[1][0]) * 0.125
    dk_ref[...] = rotate(grad, cos_ref[pl.ds(js, blk), :], -sin_ref[pl.ds(js, blk), :]).astype(BF)
    dv_ref[...] = jnp.where(lane < HD, c[0][1], c[1][1]).astype(BF)

    @pl.when(j == blocks - 1)
    def _():
        def body(i, _):
            at = pl.ds(pl.multiple_of(i * blk, blk), blk)
            grad = jnp.transpose(dqt[:, at]) * 0.125
            dq_ref[at, :] = rotate(grad, cos_ref[at, :], -sin_ref[at, :]).astype(BF)
            return 0

        lax.fori_loop(0, blocks, body, 0)


def attend_back(length, joint, mixed, dmixed, lse, cos, sin, width, blk=512):
    rows = joint.shape[0]
    pairs, blocks = width // 128, rows // blk
    full = lambda off: pl.BlockSpec((rows, 128), lambda p, j, *_: (0, off * pairs + p))
    angle = pl.BlockSpec((rows, 128), lambda p, j, *_: (0, 0))
    block = pl.BlockSpec((blk, 128), lambda p, j, *_: (j, p))
    return pl.pallas_call(
        functools.partial(attend_back_kernel, blk=blk, blocks=blocks),
        grid_spec=pltpu.PrefetchScalarGridSpec(
            num_scalar_prefetch=1,
            grid=(pairs, blocks),
            in_specs=[full(0), full(1), full(2), full(0), full(0)]
            + [pl.BlockSpec((1, 2, rows), lambda p, j, *_: (p, 0, 0)), angle, angle],
            out_specs=[full(0), block, block],
            scratch_shapes=[
                pltpu.VMEM((128, rows), BF),
                pltpu.VMEM((2, rows), F32),
                pltpu.VMEM((128, rows), F32),
            ],
        ),
        out_shape=[jax.ShapeDtypeStruct((rows, width), BF)] * 3,
        compiler_params=pltpu.CompilerParams(vmem_limit_bytes=60 * MIB),
        cost_estimate=pl.CostEstimate(
            flops=rows * width, bytes_accessed=rows * width, transcendentals=0
        ),
        name="attend_back",
    )(length, joint, joint, joint, mixed, dmixed, lse, cos, sin)


def gelu_parts(v):
    c = 0.7978845608028654
    return c, jnp.tanh(c * (v + 0.044715 * v * v * v))


def gelu_both(v):
    c, t = gelu_parts(v)
    half = 0.5 * (1.0 + t)
    return v * half, half + 0.5 * v * (1.0 - t * t) * c * (1.0 + 3 * 0.044715 * v * v)


def norm_parts(values):
    average = jnp.mean(values, axis=-1, keepdims=True)
    centred = values - average
    scale = lax.rsqrt(jnp.mean(centred * centred, axis=-1, keepdims=True) + EPSILON)
    return centred * scale, scale


def norm_back(grad, hat, scale, gain):
    g = grad * gain
    return scale * (
        g - jnp.mean(g, axis=-1, keepdims=True) - hat * jnp.mean(g * hat, axis=-1, keepdims=True)
    )


def column_sum(v):
    return jnp.sum(v, axis=0, keepdims=True)


def valid_rows(info_ref, start, count):
    at = info_ref[1] + start + lax.broadcasted_iota(jnp.int32, (count, 1), 0)
    return (at < info_ref[0]).astype(F32)


def loop_rows(rows, blk, body):
    def step(i, _):
        body(pl.multiple_of(i * blk, blk))
        return 0

    lax.fori_loop(0, rows // blk, step, 0)


def feed_kernel(info_ref, *refs, groups, chunks, sub):
    x_ref, bias_ref, resid_hbm, cot_hbm, bd_ref, gain_ref, shift_ref = refs[:7]
    ups, downs = refs[7 : 7 + groups], refs[7 + groups : 7 + 2 * groups]
    slope_ref, act_ref, out_ref, gb_ref, sums_ref, acc, resid_ref, cot_ref, sems = refs[7 + 2 * groups :]
    step = pl.program_id(0)
    rows = x_ref.shape[0]
    late = [
        pltpu.make_async_copy(resid_hbm, resid_ref, sems.at[0]),
        pltpu.make_async_copy(cot_hbm, cot_ref, sems.at[1]),
    ]

    @pl.when(step == 0)
    def _():
        for c in late:
            c.start()
        acc[...] = jnp.zeros_like(acc) + bd_ref[...].astype(F32)

    for g in range(groups):

        @pl.when(step // chunks == g)
        def _():
            for r in range(0, rows, sub):
                act, slope = gelu_both(dotg(x_ref[r : r + sub], ups[g][...]) + bias_ref[0])
                slope_ref[r : r + sub] = slope.astype(BF)
                act = act.astype(BF)
                if g == 0:
                    act_ref[r : r + sub] = act
                acc[r : r + sub] += dotg(act, downs[g][...])

    @pl.when(step == groups * chunks - 1)
    def _():
        for c in late:
            c.wait()
        sums_ref[...] = jnp.zeros_like(sums_ref)
        gain, shift = gain_ref[3:4], shift_ref[3:4]
        blk = min(256, rows)

        def body(r):
            at = pl.ds(r, blk)
            valid = valid_rows(info_ref, r, blk)
            hat, scale = norm_parts(acc[at])
            out_ref[at] = (valid * (resid_ref[at] + hat * gain + shift)).astype(BF)
            g_out = valid * cot_ref[at].astype(F32)
            low = norm_back(g_out, hat, scale, gain).astype(BF)
            gb_ref[at] = low
            sums_ref[0:1] += column_sum(g_out * hat)
            sums_ref[1:2] += column_sum(g_out)
            sums_ref[2:3] += column_sum(low.astype(F32))

        loop_rows(rows, blk, body)


def feed(info, x, biases, ups, downs, resid, cot, bias_down, gains, shifts, cols=512):
    rows, depth = x.shape
    groups, hidden = len(ups), ups[0].shape[1]
    chunks = hidden // cols
    once = lambda shape: pl.BlockSpec(shape, lambda s, *_: (0, 0), pipeline_mode=pl.Buffered(1))
    anyspace = pl.BlockSpec(memory_space=pl.ANY)
    own = lambda g: (lambda s, *_: (0, jnp.clip(s - g * chunks, 0, chunks - 1)))
    own_t = lambda g: (lambda s, *_: (jnp.clip(s - g * chunks, 0, chunks - 1), 0))
    return pl.pallas_call(
        functools.partial(feed_kernel, groups=groups, chunks=chunks, sub=min(512, rows)),
        grid_spec=pltpu.PrefetchScalarGridSpec(
            num_scalar_prefetch=1,
            grid=(groups * chunks,),
            in_specs=[
                once((rows, depth)),
                pl.BlockSpec((1, 1, cols), lambda s, *_: (s, 0, 0)),
                anyspace,
                anyspace,
                once((1, depth)),
                once(gains.shape),
                once(gains.shape),
            ]
            + [pl.BlockSpec((depth, cols), own(g)) for g in range(groups)]
            + [pl.BlockSpec((cols, depth), own_t(g)) for g in range(groups)],
            out_specs=[
                pl.BlockSpec((rows, cols), lambda s, *_: (0, s)),
                pl.BlockSpec((rows, cols), own(0)),
                once((rows, depth)),
                once((rows, depth)),
                once((8, depth)),
            ],
            scratch_shapes=[
                pltpu.VMEM((rows, depth), F32),
                pltpu.VMEM((rows, depth), F32),
                pltpu.VMEM((rows, depth), BF),
                pltpu.SemaphoreType.DMA((2,)),
            ],
        ),
        out_shape=[
            jax.ShapeDtypeStruct((rows, groups * hidden), BF),
            jax.ShapeDtypeStruct((rows, hidden), BF),
            jax.ShapeDtypeStruct((rows, depth), BF),
            jax.ShapeDtypeStruct((rows, depth), BF),
            jax.ShapeDtypeStruct((8, depth), F32),
        ],
        compiler_params=pltpu.CompilerParams(vmem_limit_bytes=60 * MIB),
        cost_estimate=pl.CostEstimate(flops=rows * depth, bytes_accessed=rows * depth, transcendentals=0),
        name="feed",
    )(info, x, biases.reshape(-1, 1, cols), resid, cot, bias_down, gains, shifts, *ups, *downs)


def feed_back_kernel(info_ref, *refs, groups, chunks, sub):
    gb_ref, slope_ref, resid_hbm, attn_hbm, cot_hbm, gain_ref = refs[:6]
    ups, downs = refs[6 : 6 + groups], refs[6 + groups : 6 + 2 * groups]
    gp_ref, gr_ref, ga_ref, sums_ref, acc, resid_ref, attn_ref, cot_ref, sems = refs[6 + 2 * groups :]
    step = pl.program_id(0)
    rows = gb_ref.shape[0]
    late = [
        pltpu.make_async_copy(src, dst, sems.at[i])
        for i, (src, dst) in enumerate(((resid_hbm, resid_ref), (attn_hbm, attn_ref), (cot_hbm, cot_ref)))
    ]

    @pl.when(step == 0)
    def _():
        for c in late:
            c.start()
        acc[...] = jnp.zeros_like(acc)

    for g in range(groups):

        @pl.when(step // chunks == g)
        def _():
            for r in range(0, rows, sub):
                grad = dotg(gb_ref[r : r + sub], downs[g][...], NT)
                low = (grad * slope_ref[r : r + sub].astype(F32)).astype(BF)
                if g == 0:
                    gp_ref[r : r + sub] = low
                acc[r : r + sub] += dotg(low, ups[g][...], NT)

    @pl.when(step == groups * chunks - 1)
    def _():
        for c in late:
            c.wait()
        sums_ref[...] = jnp.zeros_like(sums_ref)
        blk = min(256, rows)

        def body(r):
            at = pl.ds(r, blk)
            g_out = valid_rows(info_ref, r, blk) * cot_ref[at].astype(F32)
            hat, scale = norm_parts(resid_ref[at])
            g_two = acc[at]
            g_resid = g_out + norm_back(g_two, hat, scale, gain_ref[2:3])
            gr_ref[at] = g_resid
            sums_ref[0:1] += column_sum(g_two * hat)
            sums_ref[1:2] += column_sum(g_two)
            hat, scale = norm_parts(attn_ref[at])
            ga_ref[at] = norm_back(g_resid, hat, scale, gain_ref[1:2]).astype(BF)
            sums_ref[2:3] += column_sum(g_resid * hat)
            sums_ref[3:4] += column_sum(g_resid)

        loop_rows(rows, blk, body)


def feed_back(info, gb, slope, ups, downs, resid, attn_sum, cot, gains, cols=512):
    rows, depth = gb.shape
    groups, hidden = len(ups), ups[0].shape[1]
    chunks = hidden // cols
    once = lambda shape: pl.BlockSpec(shape, lambda s, *_: (0, 0), pipeline_mode=pl.Buffered(1))
    anyspace = pl.BlockSpec(memory_space=pl.ANY)
    own = lambda g: (lambda s, *_: (0, jnp.clip(s - g * chunks, 0, chunks - 1)))
    own_t = lambda g: (lambda s, *_: (jnp.clip(s - g * chunks, 0, chunks - 1), 0))
    return pl.pallas_call(
        functools.partial(feed_back_kernel, groups=groups, chunks=chunks, sub=min(512, rows)),
        grid_spec=pltpu.PrefetchScalarGridSpec(
            num_scalar_prefetch=1,
            grid=(groups * chunks,),
            in_specs=[
                once((rows, depth)),
                pl.BlockSpec((rows, cols), lambda s, *_: (0, s)),
                anyspace,
                anyspace,
                anyspace,
                once(gains.shape),
            ]
            + [pl.BlockSpec((depth, cols), own(g)) for g in range(groups)]
            + [pl.BlockSpec((cols, depth), own_t(g)) for g in range(groups)],
            out_specs=[
                pl.BlockSpec((rows, cols), own(0)),
                once((rows, depth)),
                once((rows, depth)),
                once((8, depth)),
            ],
            scratch_shapes=[
                pltpu.VMEM((rows, depth), F32),
                pltpu.VMEM((rows, depth), F32),
                pltpu.VMEM((rows, depth), F32),
                pltpu.VMEM((rows, depth), BF),
                pltpu.SemaphoreType.DMA((3,)),
            ],
        ),
        out_shape=[
            jax.ShapeDtypeStruct((rows, hidden), BF),
            jax.ShapeDtypeStruct((rows, depth), F32),
            jax.ShapeDtypeStruct((rows, depth), BF),
            jax.ShapeDtypeStruct((8, depth), F32),
        ],
        compiler_params=pltpu.CompilerParams(vmem_limit_bytes=60 * MIB),
        cost_estimate=pl.CostEstimate(flops=rows * depth, bytes_accessed=rows * depth, transcendentals=0),
        name="feed_back",
    )(info, gb, slope, resid, attn_sum, cot, gains, *ups, *downs)


def feed_grad_kernel(*refs, groups):
    up_ref, down_ref, bias_ref, act_ref, gp_ref = refs[:5]
    n2s, gbs = refs[5 : 5 + groups], refs[5 + groups : 5 + 2 * groups]
    grad_ref, sum_ref = refs[5 + 2 * groups :]
    act, gp = act_ref[...], gp_ref[...]
    dup = dotg(gp, n2s[0][...], TN)
    ddown = dotg(act, gbs[0][...], TN)
    sums = column_sum(gp.astype(F32))
    for g in range(1, groups):
        pre = dotg(n2s[g][...], up_ref[...]) + bias_ref[0]
        act, slope = gelu_both(pre)
        act = act.astype(BF)
        gp = (dotg(gbs[g][...], down_ref[...], NT) * slope).astype(BF)
        dup += dotg(gp, n2s[g][...], TN)
        ddown += dotg(act, gbs[g][...], TN)
        sums += column_sum(gp.astype(F32))
    grad_ref[0] = dup.astype(BF)
    grad_ref[1] = ddown.astype(BF)
    sum_ref[0] = sums


def feed_grad(up, down, bias, act, gp, n2s, gbs, cols=512):
    rows, depth = n2s[0].shape
    groups, hidden = len(n2s), up.shape[1]
    once = lambda shape: pl.BlockSpec(shape, lambda s: (0, 0), pipeline_mode=pl.Buffered(1))
    wide = lambda count: pl.BlockSpec((count, cols), lambda s: (0, s))
    tall = pl.BlockSpec((cols, depth), lambda s: (s, 0))
    flat = pl.BlockSpec((1, 1, cols), lambda s: (s, 0, 0))
    return pl.pallas_call(
        functools.partial(feed_grad_kernel, groups=groups),
        grid=(hidden // cols,),
        in_specs=[wide(depth), tall, flat, wide(rows), wide(rows)] + [once((rows, depth))] * (2 * groups),
        out_specs=[pl.BlockSpec((2, cols, depth), lambda s: (0, s, 0)), flat],
        out_shape=[
            jax.ShapeDtypeStruct((2, hidden, depth), BF),
            jax.ShapeDtypeStruct((hidden // cols, 1, cols), F32),
        ],
        compiler_params=pltpu.CompilerParams(vmem_limit_bytes=60 * MIB),
        cost_estimate=pl.CostEstimate(
            flops=(8 * groups - 4) * rows * depth * hidden, bytes_accessed=20 * rows * depth, transcendentals=0
        ),
        name="feed_grad",
    )(up, down, bias.reshape(-1, 1, cols), act, gp, *n2s, *gbs)


def norm_kernel(x_ref, gain_ref, shift_ref, o_ref):
    hat, _ = norm_parts(x_ref[...].astype(F32))
    o_ref[...] = (hat * gain_ref[0:1] + shift_ref[0:1]).astype(BF)


def first_norm(x, gains, shifts, blk=512):
    rows, depth = x.shape
    blk = min(blk, rows)
    whole = pl.BlockSpec(gains.shape, lambda i: (0, 0))
    block = pl.BlockSpec((blk, depth), lambda i: (i, 0))
    return pl.pallas_call(
        norm_kernel,
        grid=(rows // blk,),
        in_specs=[block, whole, whole],
        out_specs=block,
        out_shape=jax.ShapeDtypeStruct((rows, depth), BF),
        compiler_params=pltpu.CompilerParams(vmem_limit_bytes=60 * MIB),
        name="first_norm",
    )(x, gains, shifts)


def join_kernel(pick_ref, x_ref, gain_ref, shift_ref, *refs, blocks, each):
    parts, (attn_ref, resid_ref, low_ref) = refs[:-3], refs[-3:]
    block = pl.program_id(0) // each
    total = None
    for g in range(len(parts) // blocks):
        wanted = pick_ref[g * blocks + block]
        part = parts[g * blocks][...]
        for b in range(1, blocks):
            part = jnp.where(wanted == b, parts[g * blocks + b][...], part)
        total = part if total is None else total + part.astype(F32)
    attn_ref[...] = total
    hat, _ = norm_parts(total)
    resid = x_ref[...].astype(F32) + hat * gain_ref[1:2] + shift_ref[1:2]
    resid_ref[...] = resid
    hat, _ = norm_parts(resid)
    low_ref[...] = (hat * gain_ref[2:3] + shift_ref[2:3]).astype(BF)


def join(x, gains, shifts, shares, picks, blk=256):
    rows, depth = x.shape
    blocks = len(shares[0])
    blk = min(blk, rows // blocks)
    each = rows // blocks // blk
    whole = pl.BlockSpec(gains.shape, lambda i, *_: (0, 0))
    block = pl.BlockSpec((blk, depth), lambda i, *_: (i, 0))
    part = pl.BlockSpec((blk, depth), lambda i, *_: (lax.rem(i, each), 0))
    return pl.pallas_call(
        functools.partial(join_kernel, blocks=blocks, each=each),
        grid_spec=pltpu.PrefetchScalarGridSpec(
            num_scalar_prefetch=1,
            grid=(rows // blk,),
            in_specs=[block, whole, whole] + [part] * (len(shares) * blocks),
            out_specs=[block, block, block],
        ),
        out_shape=[
            jax.ShapeDtypeStruct((rows, depth), F32),
            jax.ShapeDtypeStruct((rows, depth), F32),
            jax.ShapeDtypeStruct((rows, depth), BF),
        ],
        compiler_params=pltpu.CompilerParams(vmem_limit_bytes=60 * MIB),
        name="join",
    )(picks, x, gains, shifts, *[v for share in shares for v in share])


def widen_kernel(up_ref, down_ref, dup_ref, ddown_ref):
    dup_ref[...] = jnp.transpose(up_ref[...]).astype(F32)
    ddown_ref[...] = down_ref[...].astype(F32)


def widen(grads, blk=256):
    hidden, depth = grads.shape[0] // 2, grads.shape[1]
    blk = min(blk, hidden)
    count = hidden // blk
    return pl.pallas_call(
        widen_kernel,
        grid=(count,),
        in_specs=[
            pl.BlockSpec((blk, depth), lambda i: (i, 0)),
            pl.BlockSpec((blk, depth), lambda i: (count + i, 0)),
        ],
        out_specs=[
            pl.BlockSpec((depth, blk), lambda i: (0, i)),
            pl.BlockSpec((blk, depth), lambda i: (i, 0)),
        ],
        out_shape=[
            jax.ShapeDtypeStruct((depth, hidden), F32),
            jax.ShapeDtypeStruct((hidden, depth), F32),
        ],
        compiler_params=pltpu.CompilerParams(vmem_limit_bytes=60 * MIB),
        name="widen",
    )(grads, grads)

MESH = pl.DeviceIdType.MESH


def exchange(src, dst, sems, slot, bit):
    peer = lax.axis_index("dp") ^ (1 << bit)
    return pltpu.make_async_remote_copy(
        src_ref=src,
        dst_ref=dst,
        send_sem=sems[0].at[slot],
        recv_sem=sems[1].at[slot],
        device_id={"dp": peer},
        device_id_type=MESH,
    )


def tail_kernel(
    gq_ref, gk_ref, gv_ref, mixed_ref, wq_ref, wk_ref, wv_ref, x_ref, gr_ref, gain_ref, vec_ref, *refs,
    bits, groups, steps,
):
    lefts, refs = refs[: 2 * groups], refs[2 * groups :]
    sum_ref, out_ref, total_ref = refs[:3]
    right, left, weight, x, g_resid, packed, acc, core_buf, buf, sent, came, own_share, vec_buf = refs[3:16]
    send, recv, vec_send, vec_recv, x_send, x_recv, local = refs[16:]
    sems = (send, recv)
    place, me = lax.axis_index("tensor"), lax.axis_index("dp")
    bit = lambda b: lax.rem(lax.div(me, 1 << b), 2)
    core = bit(0)
    order = list(range(1, bits))
    rows, depth = x.shape
    width = weight.shape[2]
    half = 2 * depth
    base = pl.multiple_of(core * half, half)
    part = min(512, depth)
    chunks = half // part
    slots, fetched = iter(range(send.shape[0])), iter(range(local.shape[0]))

    def fetch(src, dst):
        c = pltpu.make_async_copy(src, dst, local.at[next(fetched)])
        c.start()
        return c

    def wait_all(copies):
        for c in copies:
            c.wait()

    second = [fetch(r, right.at[i]) for i, r in enumerate((gq_ref, gk_ref, gv_ref))]
    second += [fetch(r, weight.at[i]) for i, r in enumerate((wq_ref, wk_ref, wv_ref))]
    third = [fetch(r, left.at[i]) for i, r in enumerate(lefts)] + [fetch(mixed_ref, right.at[3])]
    fourth = [fetch(x_ref, x), fetch(gr_ref, g_resid)]

    greeted = [{"dp": me ^ (1 << b)} for b in range(bits)]
    greeted += [{"tensor": lax.rem(place + r, groups)} for r in range(1, groups)]
    known = {frozenset([("dp", b)]) for b in range(bits)} | {
        frozenset([("tensor", b)]) for b in range((groups - 1).bit_length())
    }
    for bits_of in steps:
        for mask in range(1, 1 << len(bits_of)):
            chosen = [bits_of[i] for i in range(len(bits_of)) if mask >> i & 1]
            if frozenset(chosen) not in known and any(axis == "dp" for axis, _ in chosen):
                known.add(frozenset(chosen))
                peer = {}
                for axis, b in chosen:
                    peer[axis] = peer.get(axis, lax.axis_index(axis)) ^ (1 << b)
                greeted.append(peer)
    barrier = pltpu.get_barrier_semaphore()
    for peer in greeted:
        pl.semaphore_signal(barrier, inc=1, device_id=peer, device_id_type=MESH)
    pl.semaphore_wait(barrier, len(greeted))

    def copy(src, dst, b):
        c = exchange(src, dst, sems, next(slots), b)
        c.start()
        return c

    forwards = []
    cores = {}

    def reduce(chunk):
        cores[chunk].wait()

        def join(i, _):
            at = pl.ds(pl.multiple_of(chunk * part + i * 64, 64), 64)
            own = packed[pl.ds(pl.multiple_of(base + chunk * part + i * 64, 64), 64)].astype(F32)
            acc[at] = (own + core_buf[at].astype(F32)).astype(BF)
            return 0

        lax.fori_loop(0, part // 64, join, 0)
        start, size = chunk * part, part
        landing = chunk * (part - part // (1 << (bits - 1)))
        for b in order:
            size //= 2
            away = pl.multiple_of(start + (1 - bit(b)) * size, size)
            c = copy(acc.at[pl.ds(away, size)], buf.at[pl.ds(landing, size)], b)
            start = start + bit(b) * size
            yield
            c.wait()
            step = min(size, 64)

            def body(i, _, start=start, landing=landing, step=step):
                at = pl.ds(pl.multiple_of(start + i * step, step), step)
                got = buf[pl.ds(pl.multiple_of(landing + i * step, step), step)].astype(F32)
                acc[at] = (acc[at].astype(F32) + got).astype(BF)
                return 0

            lax.fori_loop(0, size // step, body, 0)
            landing += size
        start = base + start
        sum_ref[pl.ds(pl.multiple_of(start, size), size)] = acc[pl.ds(pl.multiple_of(start - base, size), size)]
        for b in reversed(order):
            have = sum_ref.at[pl.ds(pl.multiple_of(start, size), size)]
            c = copy(have, have, b)
            yield
            c.wait()
            start = start - bit(b) * size
            size *= 2
        have = sum_ref.at[pl.ds(pl.multiple_of(start, size), size)]
        forwards.append(copy(have, have, 0))

    def share(r, store):
        at = lax.rem(place + r, groups) * rows
        blk = min(256, rows)

        def body(i, _):
            g = pl.ds(pl.multiple_of(at + i * blk, blk), blk)
            value = dotg(right[0, g, :], weight[0], NT)
            value += dotg(right[1, g, :], weight[1], NT)
            value += dotg(right[2, g, :], weight[2], NT)
            store(pl.ds(pl.multiple_of(i * blk, blk), blk), value)
            return 0

        lax.fori_loop(0, rows // blk, body, 0)

    shares = []

    def share_away(r):
        def store(at, value):
            sent[r - 1, at, :] = value.astype(BF)

        share(r, store)
        c = pltpu.make_async_remote_copy(
            src_ref=sent.at[r - 1],
            dst_ref=came.at[r - 1],
            send_sem=x_send.at[r - 1],
            recv_sem=x_recv.at[r - 1],
            device_id={"tensor": lax.rem(place + r, groups)},
            device_id_type=MESH,
        )
        c.start()
        shares.append(c)

    def store_own(at, value):
        own_share[at, :] = value

    def weight_grad(side, some):
        cols = min(256, part)
        each = part // cols

        def body(i, _):
            first = pl.multiple_of(lax.rem(core + side, 2) * half + i * cols, cols)
            number = lax.div(first, depth)
            kind = lax.div(number, 3) * groups
            lanes = pl.ds(pl.multiple_of(lax.rem(first, depth), cols), cols)
            value = None
            for r in range(groups):
                at = pl.ds(pl.multiple_of(lax.rem(place + r, groups) * rows, rows), rows)
                term = dotg(left[kind + r, :, lanes], right[number, at, :], TN)
                value = term if value is None else value + term
            packed[pl.ds(first, cols), :] = value.astype(BF)
            return 0

        lax.fori_loop(some[0] * each, (some[-1] + 1) * each, body, 0)
        if side:
            for c in some:
                at = pl.ds(pl.multiple_of((1 - core) * half + c * part, part), part)
                cores[c] = copy(packed.at[at], core_buf.at[pl.ds(c * part, part)], 0)

    def last_norm():
        blk = min(64, rows)

        def body(i, _):
            at = pl.ds(pl.multiple_of(i * blk, blk), blk)
            value = own_share[at, :]
            for r in range(groups - 1):
                value += came[r, at, :].astype(F32)
            hat, scale = norm_parts(x[at, :].astype(F32))
            out_ref[at, :] = (g_resid[at, :] + norm_back(value, hat, scale, gain_ref[0:1])).astype(BF)
            total_ref[0:1] += column_sum(value * hat)
            total_ref[1:2] += column_sum(value)
            return 0

        lax.fori_loop(0, rows // blk, body, 0)

    def vectors():
        slot = 0
        for bits_of in steps:
            sends = []
            for mask in range(1, 1 << len(bits_of)):
                peer = {}
                for i, (axis, b) in enumerate(bits_of):
                    if mask >> i & 1:
                        peer[axis] = peer.get(axis, lax.axis_index(axis)) ^ (1 << b)
                sends.append(
                    pltpu.make_async_remote_copy(
                        src_ref=total_ref,
                        dst_ref=vec_buf.at[slot],
                        send_sem=vec_send.at[slot],
                        recv_sem=vec_recv.at[slot],
                        device_id=peer,
                        device_id_type=MESH,
                    )
                )
                sends[-1].start()
                slot += 1
            yield
            wait_all(sends)
            total = total_ref[...]
            for i in range(len(sends)):
                total += vec_buf[slot - len(sends) + i]
            total_ref[...] = total

    def turn(chains):
        still = []
        for chain in chains:
            try:
                next(chain)
                still.append(chain)
            except StopIteration:
                pass
        return still

    wait_all(second)
    for r in range(1, groups):
        share_away(r)
    wait_all(third)
    all_chunks = list(range(chunks))
    for some in (all_chunks[: chunks // 2], all_chunks[chunks // 2 :]):
        weight_grad(1, some)
    reduces = []
    for chunk in all_chunks:
        weight_grad(0, [chunk])
        reduces = turn(reduces + [reduce(chunk)])
    share(0, store_own)
    reduces = turn(reduces)
    wait_all(fourth)
    wait_all(shares)
    total_ref[...] = vec_ref[...]
    last_norm()
    chain = turn([vectors()])
    while reduces or chain:
        reduces, chain = turn(reduces), turn(chain)
    wait_all(forwards)


def tail(grads, mixed, weights, x, g_resid, gains, vectors, n1s, gas, bits, steps):
    (slots, width), (rows, depth), groups = mixed.shape, x.shape, len(n1s)
    half = 2 * depth
    landing = half - half // (1 << (bits - 1))
    count = half // min(512, depth) * (2 * bits + 1)
    vecs = sum((1 << len(b)) - 1 for b in steps)
    vmem = pl.BlockSpec(memory_space=pltpu.VMEM)
    anyspace = pl.BlockSpec(memory_space=pl.ANY)
    dma = pltpu.SemaphoreType.DMA
    peers = max(groups - 1, 1)
    return pl.pallas_call(
        functools.partial(tail_kernel, bits=bits, groups=groups, steps=steps),
        in_specs=[anyspace] * 9 + [vmem] * 2 + [anyspace] * (2 * groups),
        out_specs=[vmem, vmem, vmem],
        out_shape=[
            jax.ShapeDtypeStruct((4 * depth, width), BF),
            jax.ShapeDtypeStruct((rows, depth), BF),
            jax.ShapeDtypeStruct(vectors.shape, F32),
        ],
        scratch_shapes=[
            pltpu.VMEM((4, slots, width), BF),
            pltpu.VMEM((2 * groups, rows, depth), BF),
            pltpu.VMEM((3, depth, width), BF),
            pltpu.VMEM((rows, depth), BF),
            pltpu.VMEM((rows, depth), F32),
            pltpu.VMEM((4 * depth, width), BF),
            pltpu.VMEM((half, width), BF),
            pltpu.VMEM((half, width), BF),
            pltpu.VMEM((landing, width), BF),
            pltpu.VMEM((peers, rows, depth), BF),
            pltpu.VMEM((peers, rows, depth), BF),
            pltpu.VMEM((rows, depth), F32),
            pltpu.VMEM((vecs,) + vectors.shape, F32),
            dma((count,)),
            dma((count,)),
            dma((vecs,)),
            dma((vecs,)),
            dma((peers,)),
            dma((peers,)),
            dma((9 + 2 * groups,)),
        ],
        compiler_params=pltpu.CompilerParams(
            collective_id=1, has_side_effects=True, vmem_limit_bytes=60 * MIB
        ),
        cost_estimate=pl.CostEstimate(flops=rows * width, bytes_accessed=rows * width, transcendentals=0),
        name="tail",
    )(*grads, mixed, *weights, x, g_resid, gains, vectors, *n1s, *gas)


def mixed_back_kernel(at_ref, x_ref, w_ref, *refs):
    refs[-1][...] = dotg(x_ref[...], w_ref[...], NT).astype(BF)


def mixed_back(where, x, w_out, slots, held, blk=256):
    rows, depth = x.shape
    width = w_out.shape[0]
    blk = min(blk, rows)
    count = rows // blk
    return pl.pallas_call(
        mixed_back_kernel,
        grid_spec=pltpu.PrefetchScalarGridSpec(
            num_scalar_prefetch=1,
            grid=(count,),
            in_specs=[
                pl.BlockSpec((blk, depth), lambda i, at: (i, 0)),
                pl.BlockSpec((width, depth), lambda i, at: (0, 0)),
            ]
            + [pl.BlockSpec(memory_space=pl.ANY)] * len(held),
            out_specs=pl.BlockSpec((blk, width), lambda i, at: (at[0] * count + i, 0)),
        ),
        out_shape=jax.ShapeDtypeStruct((slots, width), BF),
        input_output_aliases={3: 0} if held else {},
        compiler_params=pltpu.CompilerParams(vmem_limit_bytes=60 * MIB),
        cost_estimate=pl.CostEstimate(flops=rows * depth, bytes_accessed=rows * depth, transcendentals=0),
        name="mixed_back",
    )(where, x, w_out, *held)


def shift(x, axis, count, step):
    return lax.ppermute(x, axis, [((i + step) % count, i) for i in range(count)])


def shards(
    tokens,
    lengths,
    cotangent,
    w_query,
    w_key,
    w_value,
    w_out,
    up_weight,
    bias_up,
    down_weight,
    bias_down,
    norm_gains,
    norm_shifts,
):
    rows, _, depth = tokens.shape
    groups, replicas = lax.axis_size("tensor"), lax.axis_size("dp")
    me, replica = lax.axis_index("tensor"), lax.axis_index("dp")
    slots = rows * groups
    width = w_query.shape[1]
    hidden = up_weight.shape[1]
    x = tokens.reshape(rows, depth)
    here = me.reshape(1).astype(jnp.int32)
    place = lambda r: (here + r) % groups

    def others(v):
        return [shift(v, "tensor", groups, r) for r in range(1, groups)]

    def to_owner(v, r):
        return shift(v, "tensor", groups, groups - r)

    up_piece = lax.dynamic_slice_in_dim(up_weight, replica * (depth // replicas), depth // replicas, 0)
    down_piece = lax.dynamic_slice_in_dim(
        down_weight, replica * (hidden // replicas), hidden // replicas, 0
    )
    up_pieces, down_pieces, bias_rest = others(up_piece), others(down_piece), others(bias_up)
    gather = lambda v: lax.all_gather(v, "dp", axis=0, tiled=True)

    freqs = 10000.0 ** (-jnp.arange(HD // 2).astype(F32) * 2.0 / HD)
    angles = jnp.arange(slots).astype(F32)[:, None] * freqs[None, :]
    cosine, sine = jnp.cos(angles), jnp.sin(angles)
    cosine = jnp.concatenate([cosine] * 4, axis=1)
    sine = jnp.concatenate([-sine, sine] * 2, axis=1)
    normed_one = first_norm(x, norm_gains, norm_shifts)
    normed_one_rest = others(normed_one)
    weights = (w_query, w_key, w_value)
    own, up_pieces = lax.optimization_barrier((normed_one, up_pieces))
    joint = project(here, own, *weights, cosine, sine)
    joint, normed_one_rest, down_pieces, bias_rest = lax.optimization_barrier(
        (joint, normed_one_rest, down_pieces, bias_rest)
    )
    for r, n in enumerate(normed_one_rest):
        joint = project(place(r + 1), n, *weights, cosine, sine, joint)
    blk = min(512, rows)
    each = rows // blk
    odd = lambda r: lax.rem(place(r), 2)
    ranks = lambda r, k: jnp.where(odd(r) == 1, each - 1 - k, k)
    held, shares, arrived = (), [], [[] for _ in range(1, groups)]
    for k in range(each):
        for r in range(1, groups):
            *held, share = attend(place(r) * each + ranks(0, k), lengths, joint, w_out, held, BF, blk)
            arrived[r - 1].append(to_owner(share, r))
        if k == each - 1 and k > 0:
            joint, arrived = lax.optimization_barrier((joint, [v[:k] for v in arrived])), arrived
            joint, early = joint
            arrived = [list(e) + v[k:] for e, v in zip(early, arrived)]
        *held, share = attend(here * each + ranks(0, k), lengths, joint, w_out, held, F32, blk)
        shares.append(share)
    mixed, lse = held
    shares = [shares] + arrived
    picks = jnp.concatenate([ranks(groups - r, k) for r in range(groups) for k in range(each)])
    up_rest, down_rest = [gather(p) for p in up_pieces], [gather(p) for p in down_pieces]
    shares, up_rest, down_rest = lax.optimization_barrier((shares, up_rest, down_rest))
    ups, downs = [up_weight] + up_rest, [down_weight] + down_rest
    biases = jnp.concatenate([bias_up] + bias_rest).astype(F32)

    info = jnp.stack([lengths[0], me * rows]).astype(jnp.int32)
    cot = cotangent.reshape(rows, depth)
    attn_sum, resid, normed_two = join(x, norm_gains, norm_shifts, shares, picks)
    normed_two_rest = others(normed_two)
    slope, act, layer_out, g_branch, sums3 = feed(
        info, normed_two, biases, ups, downs, resid, cot, bias_down.reshape(1, depth), norm_gains, norm_shifts
    )
    g_branch_rest = others(g_branch)
    g_pre, g_resid, g_attn, sums21 = feed_back(
        info, g_branch, slope, ups, downs, resid, attn_sum, cot, norm_gains
    )
    g_attn_rest = others(g_attn)
    g_pre, normed_two_rest = lax.optimization_barrier((g_pre, normed_two_rest))
    grad_feed, bias_up_sum = feed_grad(
        up_weight, down_weight, biases[:hidden], act, g_pre,
        [normed_two] + normed_two_rest, [g_branch] + g_branch_rest,
    )
    grad_feed = grad_feed.reshape(2 * hidden, depth)
    g_attn, g_attn_rest, grad_feed = lax.optimization_barrier((g_attn, g_attn_rest, grad_feed))
    grad_feed = lax.psum(grad_feed, "dp")
    g_mixed = mixed_back(here, g_attn, w_out, slots, [])
    for r, g in enumerate(g_attn_rest):
        g_mixed = mixed_back(place(r + 1), g, w_out, slots, [g_mixed])

    grads = attend_back(lengths, joint, mixed, g_mixed, lse, cosine, sine, width)
    placed = lax.dynamic_update_slice(
        jnp.zeros((groups * hidden,), F32), bias_up_sum.reshape(-1), (me * hidden,)
    ).reshape(-1, depth)
    bits = (replicas - 1).bit_length()
    steps = [("tensor", b) for b in range((groups - 1).bit_length())] + [("dp", b) for b in range(bits)]
    steps = [tuple(steps[i : i + 2]) for i in range(0, len(steps), 2)]
    vectors = jnp.concatenate([jnp.zeros((2, depth), F32), sums3[:3], sums21[:4], placed])
    vectors = jnp.pad(vectors, ((0, -len(vectors) % 8), (0, 0)))
    packed, grad_tokens, sums = tail(
        grads, mixed, weights, x, g_resid, norm_gains, vectors,
        [normed_one] + normed_one_rest, [g_attn] + g_attn_rest, bits, steps,
    )
    grad_up, grad_down = widen(grad_feed)
    grad_query, grad_key, grad_value = (packed[i * depth : (i + 1) * depth].astype(F32) for i in range(3))
    grad_out = jnp.transpose(packed[3 * depth :]).astype(F32)
    grad_gains = jnp.stack([sums[0], sums[7], sums[5], sums[2]])
    grad_shifts = jnp.stack([sums[1], sums[8], sums[6], sums[3]])
    grad_bias_up = lax.dynamic_slice_in_dim(sums[9 : 9 + groups * hidden // depth].reshape(-1), me * hidden, hidden, 0)
    whole = (rows, 1, depth)
    return (
        layer_out.reshape(whole),
        grad_tokens.reshape(whole),
        grad_query,
        grad_key,
        grad_value,
        grad_out,
        grad_up,
        grad_bias_up,
        grad_down,
        sums[4],
        grad_gains,
        grad_shifts,
    )


def solution(mesh):
    wide, tall = P(None, "tensor"), P("tensor", None)
    acts = P("tensor", "dp", None)
    return jax.shard_map(
        shards,
        mesh=mesh,
        in_specs=(acts, P("dp"), acts, wide, wide, wide, tall, wide, P("tensor"), tall, P(), P(), P()),
        out_specs=(acts, acts, wide, wide, wide, tall, wide, P("tensor"), tall, P(), P(), P()),
        check_vma=False,
    )
```

profile of v0, /device:TPU:0, one launch (start us, length us, event | category | flops | bytes accessed | tf_op | source)
XLA Modules:
  0.0 542.8 jit_solution(2402001181618050109)
XLA Ops:
  8.2 3.0 collective-permute-start
  11.2 3.7 first_norm.1.refs_0_
  23.2 3.7 fusion
  26.9 3.0 pad_maximum_fusion
  29.9 7.5 %project.2.refs_6_ = bf16[2048,1536]{1,0:T(8,128)(2,1)} custom-call(s32[1]{0:T(128)} %bitcast.1.at.at_ref, bf16[1024,1024]{1,0:T(8,128)(2,1)} %first_norm.1.refs_0_, bf16[1024,512]{1,0:T(8,128)(2,1)} %wq_ref.1, bf16[1024,512]{1,0:T(8,128)(2,1)} %wk_ref.1, bf16[1024,512]{1,0:T(8,128)(2,1)} %wv_ref.1, f32[2048,128]{1,0:T(8,128)} %get-tuple-element.170.refs_4_.cos_ref, ...), custom_call_target="tpu_custom_call" | custom-call | flops 1048576 | bytes 1048576 | tf_op jit(solution)/shard_map/project/pallas_call | solution.py:50
  37.5 33.6 %collective-permute-done.3 = bf16[2048]{0:T(1024)(128)(2,1)S(1)} collective-permute-done((bf16[2048]{0:T(1024)(128)(2,1)S(1)}, bf16[2048]{0:T(1024)(128)(2,1)S(1)}, u32[]{:S(2)}, u32[]{:S(2)}) %collective-permute-start.3) | collective-permute-done | bytes 4128 | tf_op jit(solution)/shard_map/ppermute | solution.py:968
  72.6 8.0 %project.3.q_ref.k_ref.v_ref = bf16[2048,1536]{1,0:T(8,128)(2,1)} custom-call(s32[1]{0:T(128)S(6)} %select_n.67.at.at_ref, bf16[1024,1024]{1,0:T(8,128)(2,1)} %copy-done.1, bf16[1024,512]{1,0:T(8,128)(2,1)} %wq_ref.1, bf16[1024,512]{1,0:T(8,128)(2,1)} %wk_ref.1, bf16[1024,512]{1,0:T(8,128)(2,1)} %wv_ref.1, ...), custom_call_target="tpu_custom_call", output_to_operand_aliasing={{}: (7, {})} | custom-call | flops 1048576 | bytes 1048576 | tf_op jit(solution)/shard_map/project/pallas_call | solution.py:50
  80.6 19.5 %attend.4 = (bf16[2048,512]{1,0:T(8,128)(2,1)}, f32[4,2,2048]{2,1,0:T(2,128)}, bf16[512,1024]{1,0:T(8,128)(2,1)}) custom-call(s32[1]{0:T(128)S(6)} %add.78.at_ref, s32[1]{0:T(128)S(6)} %copy.55.len_ref, bf16[2048,1536]{1,0:T(8,128)(2,1)} %project.3.q_ref.k_ref.v_ref, bf16[2048,1536]{1,0:T(8,128)(2,1)} %project.3.q_ref.k_ref.v_ref, ...), custom_call_target="tpu_custom_call" | custom-call | flops 1048576 | bytes 1048576 | tf_op jit(solution)/shard_map/attend/pallas_call | solution.py:125
  100.2 9.1 %attend.5 = (bf16[2048,512]{1,0:T(8,128)(2,1)}, f32[4,2,2048]{2,1,0:T(2,128)}, f32[512,1024]{1,0:T(8,128)}) custom-call(s32[1]{0:T(128)S(6)} %add.75.at_ref, s32[1]{0:T(128)S(6)} %copy.55.len_ref, bf16[2048,1536]{1,0:T(8,128)(2,1)} %project.3.q_ref.k_ref.v_ref, ...), custom_call_target="tpu_custom_call", output_to_operand_aliasing={{0}: (6, {}), {1}: (7, {})} | custom-call | flops 1048576 | bytes 1048576 | tf_op jit(solution)/shard_map/attend/pallas_call | solution.py:125
  109.3 24.6 %attend.6 = (bf16[2048,512]{1,0:T(8,128)(2,1)}, f32[4,2,2048]{2,1,0:T(2,128)}, bf16[512,1024]{1,0:T(8,128)(2,1)}) custom-call(s32[1]{0:T(128)S(6)} %add.80.at_ref, s32[1]{0:T(128)S(6)} %copy.55.len_ref, bf16[2048,1536]{1,0:T(8,128)(2,1)} %project.3.q_ref.k_ref.v_ref, ...), custom_call_target="tpu_custom_call", output_to_operand_aliasing={{0}: (6, {}), {1}: (7, {})} | custom-call | flops 1048576 | bytes 1048576 | tf_op jit(solution)/shard_map/attend/pallas_call | solution.py:125
  138.4 14.8 %attend.7 = (bf16[2048,512]{1,0:T(8,128)(2,1)}, f32[4,2,2048]{2,1,0:T(2,128)}, f32[512,1024]{1,0:T(8,128)}) custom-call(s32[1]{0:T(128)S(6)} %add.79.at_ref, s32[1]{0:T(128)S(6)} %copy.55.len_ref, bf16[2048,1536]{1,0:T(8,128)(2,1)} %project.3.q_ref.k_ref.v_ref, ...), custom_call_target="tpu_custom_call", output_to_operand_aliasing={{0}: (6, {}), {1}: (7, {})} | custom-call | flops 1048576 | bytes 1048576 | tf_op jit(solution)/shard_map/attend/pallas_call | solution.py:125
  153.2 4.4 collective-permute-done.5.refs_3_
  158.6 10.5 %join.1 = (f32[1024,1024]{1,0:T(8,128)}, f32[1024,1024]{1,0:T(8,128)}, bf16[1024,1024]{1,0:T(8,128)(2,1)}) custom-call(s32[4]{0:T(128)} %pad_add_fusion.1.pick_ref, bf16[1024,1024]{1,0:T(8,128)(2,1)} %bitcast.17, f32[4,1024]{1,0:T(4,128)} %gain_ref.5, f32[4,1024]{1,0:T(4,128)} %refs_6_.2, f32[512,1024]{1,0:T(8,128)} %get-tuple-element.82.refs_0_, ...), custom_call_target="tpu_custom_call" | custom-call | tf_op jit(solution)/shard_map/join/pallas_call | solution.py:590
  170.8 40.0 %feed.1 = (bf16[1024,4096]{1,0:T(8,128)(2,1)}, bf16[1024,2048]{1,0:T(8,128)(2,1)}, bf16[1024,1024]{1,0:T(8,128)(2,1)}, bf16[1024,1024]{1,0:T(8,128)(2,1)}, f32[8,1024]{1,0:T(8,128)}) custom-call(s32[2]{0:T(128)} %pad_add_fusion.info_ref, bf16[1024,1024]{1,0:T(8,128)(2,1)} %get-tuple-element.86.refs_0_.refs_5_, f32[8,1,512]{2,1,0:T(1,128)} %maximum_convert_fusion.refs_1_, ...), custom_call_target="tpu_custom_call" | custom-call | flops 1048576 | bytes 1048576 | tf_op jit(solution)/shard_map/feed/pallas_call | solution.py:354
  211.9 34.1 %feed_back.1 = (bf16[1024,2048]{1,0:T(8,128)(2,1)}, f32[1024,1024]{1,0:T(8,128)}, bf16[1024,1024]{1,0:T(8,128)(2,1)}, f32[8,1024]{1,0:T(8,128)}) custom-call(s32[2]{0:T(128)} %pad_add_fusion.info_ref, bf16[1024,1024]{1,0:T(8,128)(2,1)} %get-tuple-element.93.refs_0_.refs_7_, bf16[1024,4096]{1,0:T(8,128)(2,1)} %get-tuple-element.94.refs_1_, ...), custom_call_target="tpu_custom_call" | custom-call | flops 1048576 | bytes 1048576 | tf_op jit(solution)/shard_map/feed_back/pallas_call | solution.py:457
  247.7 15.0 %collective-permute-done.8.refs_8_ = bf16[1024,1024]{1,0:T(8,128)(2,1)} collective-permute-done((bf16[1024,1024]{1,0:T(8,128)(2,1)}, bf16[1024,1024]{1,0:T(8,128)(2,1)}, u32[]{:S(2)}, u32[]{:S(2)}) %collective-permute-start.8) | collective-permute-done | bytes 2097184 | tf_op jit(solution)/shard_map/ppermute | solution.py:968
  262.7 33.6 %feed_grad.1 = (bf16[2,2048,1024]{2,1,0:T(8,128)(2,1)}, f32[4,1,512]{2,1,0:T(1,128)}) custom-call(bf16[1024,2048]{1,0:T(8,128)(2,1)} %refs_0_.1, bf16[2048,1024]{1,0:T(8,128)(2,1)} %refs_1_.5, f32[4,1,512]{2,1,0:T(1,128)} %slice.69.refs_2_, bf16[1024,2048]{1,0:T(8,128)(2,1)} %get-tuple-element.97.refs_3_, bf16[1024,2048]{1,0:T(8,128)(2,1)} %get-tuple-element.99.refs_4_, ...), custom_call_target="tpu_custom_call" | custom-call | flops 25769803776 | bytes 20971520 | tf_op jit(solution)/shard_map/feed_grad/pallas_call | solution.py:526
  296.4 7.8 %collective-permute-done.6.x_ref.refs_3_ = bf16[1024,1024]{1,0:T(8,128)(2,1)S(1)} collective-permute-done((bf16[1024,1024]{1,0:T(8,128)(2,1)}, bf16[1024,1024]{1,0:T(8,128)(2,1)S(1)}, u32[]{:S(2)}, u32[]{:S(2)}) %collective-permute-start.6) | collective-permute-done | bytes 2097184 | tf_op jit(solution)/shard_map/ppermute | solution.py:968
  306.6 4.8 mixed_back.2.refs_0_
  311.4 5.1 mixed_back.3.do_ref
  316.5 79.8 %attend_back.1 = (bf16[2048,512]{1,0:T(8,128)(2,1)}, bf16[2048,512]{1,0:T(8,128)(2,1)}, bf16[2048,512]{1,0:T(8,128)(2,1)}) custom-call(s32[1]{0:T(128)S(6)} %copy.55.len_ref, bf16[2048,1536]{1,0:T(8,128)(2,1)} %project.3.q_ref.k_ref.v_ref, bf16[2048,1536]{1,0:T(8,128)(2,1)} %project.3.q_ref.k_ref.v_ref, bf16[2048,1536]{1,0:T(8,128)(2,1)} %project.3.q_ref.k_ref.v_ref, ...), custom_call_target="tpu_custom_call" | custom-call | flops 1048576 | bytes 1048576 | tf_op jit(solution)/shard_map/attend_back/pallas_call | solution.py:229
  396.4 117.8 %tail.1 = (bf16[4096,512]{1,0:T(8,128)(2,1)}, bf16[1024,1024]{1,0:T(8,128)(2,1)}, f32[16,1024]{1,0:T(8,128)}) custom-call(bf16[2048,512]{1,0:T(8,128)(2,1)} %get-tuple-element.105.gq_ref, bf16[2048,512]{1,0:T(8,128)(2,1)} %get-tuple-element.106.gk_ref, bf16[2048,512]{1,0:T(8,128)(2,1)} %get-tuple-element.107.gv_ref, ...), custom_call_target="tpu_custom_call" | custom-call | flops 524288 | bytes 524288 | tf_op jit(solution)/shard_map/tail/pallas_call | solution.py:899
  514.2 5.4 convert_bitcast_fusion
  523.9 10.6 %widen.1 = (f32[1024,2048]{1,0:T(8,128)}, f32[2048,1024]{1,0:T(8,128)}) custom-call(bf16[4096,1024]{1,0:T(8,128)(2,1)} %all-reduce.3.cloned.1.call-done.up_ref.down_ref, bf16[4096,1024]{1,0:T(8,128)(2,1)} %all-reduce.3.cloned.1.call-done.up_ref.down_ref), custom_call_target="tpu_custom_call" | custom-call | tf_op jit(solution)/shard_map/widen/pallas_call | solution.py:617
  (78 shorter events, 27.9 us)
Async XLA Ops:
  7.2 150.4 %all-gather.3.cloned.1.call-start = ((), (), s32[]{:S(2)}) async-start(), calls=%async_computation | async-start | bytes 4456448 | tf_op jit(solution)/shard_map/all_gather | solution.py:1007
  8.2 9.3 %collective-permute-start = (bf16[64,2048]{1,0:T(8,128)(2,1)S(1)}, bf16[64,2048]{1,0:T(8,128)(2,1)S(1)}, u32[]{:S(2)}, u32[]{:S(2)}) collective-permute-start(bf16[64,2048]{1,0:T(8,128)(2,1)S(1)} %constant_dynamic-slice_fusion.1), channel_id=1, source_target_pairs={{1,0},{0,1},{3,2},{2,3},{5,4},{4,5},{7,6},{6,7},{9,8},{8,9},{11,10... | collective-permute-start | bytes 786440 | tf_op jit(solution)/shard_map/ppermute | solution.py:968
  11.2 10.2 %copy-start.12 = (bf16[2048]{0:T(1024)(128)(2,1)S(1)}, bf16[2048]{0:T(1024)(128)(2,1)}, u32[]{:S(2)}) copy-start(bf16[2048]{0:T(1024)(128)(2,1)} %param.21) | copy-start | bytes 12292
  18.2 139.4 %all-gather.5.cloned.1.call-start = ((), (), s32[]{:S(2)}) async-start(), calls=%async_computation.1 | async-start | bytes 4456448 | tf_op jit(solution)/shard_map/all_gather | solution.py:1007
  18.3 52.8 %collective-permute-start.1 = (bf16[1024,1024]{1,0:T(8,128)(2,1)}, bf16[1024,1024]{1,0:T(8,128)(2,1)S(1)}, u32[]{:S(2)}, u32[]{:S(2)}) collective-permute-start(bf16[1024,1024]{1,0:T(8,128)(2,1)} %first_norm.1.refs_0_), channel_id=1, source_target_pairs={{1,0},{0,1},{3,2},{2,3},{5,4},{4,5},{7,6},{6,7},{9,8},{8,9},{11,10... | collective-permute-start | bytes 6291464 | tf_op jit(solution)/shard_map/ppermute | solution.py:968
  21.1 50.0 %collective-permute-start.2 = (bf16[128,1024]{1,0:T(8,128)(2,1)S(1)}, bf16[128,1024]{1,0:T(8,128)(2,1)S(1)}, u32[]{:S(2)}, u32[]{:S(2)}) collective-permute-start(bf16[128,1024]{1,0:T(8,128)(2,1)S(1)} %constant_dynamic-slice_fusion), channel_id=1, source_target_pairs={{1,0},{0,1},{3,2},{2,3},{5,4},{4,5},{7,6},{6,7},{9,8},{8,9},{11,10... | collective-permute-start | bytes 786440 | tf_op jit(solution)/shard_map/ppermute | solution.py:968
  21.4 49.7 %collective-permute-start.3 = (bf16[2048]{0:T(1024)(128)(2,1)S(1)}, bf16[2048]{0:T(1024)(128)(2,1)S(1)}, u32[]{:S(2)}, u32[]{:S(2)}) collective-permute-start(bf16[2048]{0:T(1024)(128)(2,1)S(1)} %copy-done.12), channel_id=1, source_target_pairs={{1,0},{0,1},{3,2},{2,3},{5,4},{4,5},{7,6},{6,7},{9,8},{8,9},{11,10... | collective-permute-start | bytes 12296 | tf_op jit(solution)/shard_map/ppermute | solution.py:968
  71.1 1.5 copy-start.1
  71.8 452.1 %all-reduce.3.cloned.1.call-start = ((), (), s32[]{:S(2)}) async-start(), calls=%async_computation.2 | async-start | bytes 16777216 | tf_op jit(solution)/shard_map/psum | solution.py:1066
  100.1 38.3 %collective-permute-start.4 = (bf16[512,1024]{1,0:T(8,128)(2,1)}, bf16[512,1024]{1,0:T(8,128)(2,1)S(1)}, u32[]{:S(2)}, u32[]{:S(2)}) collective-permute-start(bf16[512,1024]{1,0:T(8,128)(2,1)} %get-tuple-element.71), channel_id=1, source_target_pairs={{1,0},{0,1},{3,2},{2,3},{5,4},{4,5},{7,6},{6,7},{9,8},{8,9},{11,10... | collective-permute-start | bytes 3145736 | tf_op jit(solution)/shard_map/ppermute | solution.py:968
  109.3 26.7 %copy-start.13 = (bf16[1024]{0:T(1024)(128)(2,1)S(1)}, bf16[1024]{0:T(1024)(128)(2,1)}, u32[]{:S(2)}) copy-start(bf16[1024]{0:T(1024)(128)(2,1)} %param.23) | copy-start | bytes 6148
  133.9 23.7 %collective-permute-start.5 = (bf16[512,1024]{1,0:T(8,128)(2,1)}, bf16[512,1024]{1,0:T(8,128)(2,1)S(1)}, u32[]{:S(2)}, u32[]{:S(2)}) collective-permute-start(bf16[512,1024]{1,0:T(8,128)(2,1)} %get-tuple-element.79), channel_id=1, source_target_pairs={{1,0},{0,1},{3,2},{2,3},{5,4},{4,5},{7,6},{6,7},{9,8},{8,9},{11,10... | collective-permute-start | bytes 3145736 | tf_op jit(solution)/shard_map/ppermute | solution.py:968
  138.4 14.8 %copy-start.3 = (bf16[512,1024]{1,0:T(8,128)(2,1)}, bf16[512,1024]{1,0:T(8,128)(2,1)S(1)}, u32[]{:S(2)}) copy-start(bf16[512,1024]{1,0:T(8,128)(2,1)S(1)} %collective-permute-done.4.refs_2_) | copy-start | bytes 3145732
  157.6 1.0 copy-start.4
  169.1 78.6 %collective-permute-start.7 = (bf16[1024,1024]{1,0:T(8,128)(2,1)}, bf16[1024,1024]{1,0:T(8,128)(2,1)}, u32[]{:S(2)}, u32[]{:S(2)}) collective-permute-start(bf16[1024,1024]{1,0:T(8,128)(2,1)} %get-tuple-element.86.refs_0_.refs_5_), channel_id=1, source_target_pairs={{1,0},{0,1},{3,2},{2,3},{5,4},{4,5},{7,6},{6,7},{9,8},{8,9},{11,10... | collective-permute-start | bytes 6291464 | tf_op jit(solution)/shard_map/ppermute | solution.py:968
  170.8 40.5 %copy-start.7 = (f32[8,1,512]{2,1,0:T(1,128)S(1)}, f32[8,1,512]{2,1,0:T(1,128)}, u32[]{:S(2)}) copy-start(f32[8,1,512]{2,1,0:T(1,128)} %maximum_convert_fusion.refs_1_) | copy-start | bytes 49156
  210.8 51.9 %collective-permute-start.8 = (bf16[1024,1024]{1,0:T(8,128)(2,1)}, bf16[1024,1024]{1,0:T(8,128)(2,1)}, u32[]{:S(2)}, u32[]{:S(2)}) collective-permute-start(bf16[1024,1024]{1,0:T(8,128)(2,1)} %get-tuple-element.93.refs_0_.refs_7_), channel_id=1, source_target_pairs={{1,0},{0,1},{3,2},{2,3},{5,4},{4,5},{7,6},{6,7},{9,8},{8,9},{11,10... | collective-permute-start | bytes 6291464 | tf_op jit(solution)/shard_map/ppermute | solution.py:968
  246.0 58.1 %collective-permute-start.6 = (bf16[1024,1024]{1,0:T(8,128)(2,1)}, bf16[1024,1024]{1,0:T(8,128)(2,1)S(1)}, u32[]{:S(2)}, u32[]{:S(2)}) collective-permute-start(bf16[1024,1024]{1,0:T(8,128)(2,1)} %get-tuple-element.103.x_ref.refs_2_), channel_id=1, source_target_pairs={{1,0},{0,1},{3,2},{2,3},{5,4},{4,5},{7,6},{6,7},{9,8},{8,9},{11,10... | collective-permute-start | bytes 6291464 | tf_op jit(solution)/shard_map/ppermute | solution.py:968
  304.1 1.3 copy-start
  304.1 1.3 copy-start.10
  304.1 1.3 copy-start.9
  304.1 1.4 copy-start.11
  519.6 1.8 copy-start.8
  523.9 10.6 %copy-start.2 = (bf16[1024,1024]{1,0:T(8,128)(2,1)S(1)}, bf16[1024,1024]{1,0:T(8,128)(2,1)}, u32[]{:S(2)}) copy-start(bf16[1024,1024]{1,0:T(8,128)(2,1)} %get-tuple-element.112) | copy-start | bytes 6291460
  (2 other events, 1.4 us)
Sparse Core Ops, SparseCore 0:
  18.4 52.0 all-gather.2
  72.6 51.2 all-gather.4
  304.3 207.3 all-reduce.2
where the time goes:
time: 549 us; the launch traced here: 543 us
  Pallas kernels  424 us (77%)
  waiting for transfers between devices  63.4 us (12%)
  other arithmetic  15.3 us (3%)
  between operations  15.1 us (3%)
  starting transfers between devices  12.9 us (2%)
  local copies, waits for them, and re-layouts  12.2 us (2%)
    pallas_call x1, Pallas kernels, tail(): pl.pallas_call(functools.partial(tail_kernel, bits=bits, groups=groups, s...  118 us
    pallas_call x1, Pallas kernels, attend_back(): pl.pallas_call(functools.partial(attend_back_kernel, blk=blk, blocks=bloc...  79.8 us
    pallas_call x4, Pallas kernels, attend(): pl.pallas_call(functools.partial(attend_kernel, blk=blk), grid_spec=pltpu...  68.1 us
    ppermute x9, waiting for transfers between devices, shift(): lax.ppermute(x, axis, [((i + step) % count, i) for i in range(count)])  63.4 us
    pallas_call x1, Pallas kernels, feed(): pl.pallas_call(functools.partial(feed_kernel, groups=groups, chunks=chunk...  40 us
    pallas_call x1, Pallas kernels, feed_back(): pl.pallas_call(functools.partial(feed_back_kernel, groups=groups, chunks=...  34.1 us
    pallas_call x1, Pallas kernels, feed_grad(): pl.pallas_call(functools.partial(feed_grad_kernel, groups=groups), grid=(...  33.6 us
    pallas_call x2, Pallas kernels, project(): pl.pallas_call(kernel, grid_spec=pltpu.PrefetchScalarGridSpec(num_scalar_...  15.5 us
  transfers between devices with their start and end apart: 12, of which 5 were waited for; matrix products, arithmetic and copies ran while one was open for 4% of the time, Pallas kernels for 74%

commit v1 on v0

--- a/solution.py
+++ b/solution.py
@@ -1003,7 +1003,6 @@
     down_piece = lax.dynamic_slice_in_dim(
         down_weight, replica * (hidden // replicas), hidden // replicas, 0
     )
-    up_pieces, down_pieces, bias_rest = others(up_piece), others(down_piece), others(bias_up)
     gather = lambda v: lax.all_gather(v, "dp", axis=0, tiled=True)
 
     freqs = 10000.0 ** (-jnp.arange(HD // 2).astype(F32) * 2.0 / HD)
@@ -1011,14 +1010,15 @@
     cosine, sine = jnp.cos(angles), jnp.sin(angles)
     cosine = jnp.concatenate([cosine] * 4, axis=1)
     sine = jnp.concatenate([-sine, sine] * 2, axis=1)
+    x_rest = others(x)
     normed_one = first_norm(x, norm_gains, norm_shifts)
-    normed_one_rest = others(normed_one)
     weights = (w_query, w_key, w_value)
-    own, up_pieces = lax.optimization_barrier((normed_one, up_pieces))
-    joint = project(here, own, *weights, cosine, sine)
-    joint, normed_one_rest, down_pieces, bias_rest = lax.optimization_barrier(
-        (joint, normed_one_rest, down_pieces, bias_rest)
+    up_pieces, down_pieces, bias_rest = others(up_piece), others(down_piece), others(bias_up)
+    joint = project(here, normed_one, *weights, cosine, sine)
+    joint, x_rest, up_pieces, down_pieces, bias_rest = lax.optimization_barrier(
+        (joint, x_rest, up_pieces, down_pieces, bias_rest)
     )
+    normed_one_rest = [first_norm(v, norm_gains, norm_shifts) for v in x_rest]
     for r, n in enumerate(normed_one_rest):
         joint = project(place(r + 1), n, *weights, cosine, sine, joint)
     blk = min(512, rows)
@@ -1040,14 +1040,14 @@
     shares = [shares] + arrived
     picks = jnp.concatenate([ranks(groups - r, k) for r in range(groups) for k in range(each)])
     up_rest, down_rest = [gather(p) for p in up_pieces], [gather(p) for p in down_pieces]
-    shares, up_rest, down_rest = lax.optimization_barrier((shares, up_rest, down_rest))
-    ups, downs = [up_weight] + up_rest, [down_weight] + down_rest
     biases = jnp.concatenate([bias_up] + bias_rest).astype(F32)
 
     info = jnp.stack([lengths[0], me * rows]).astype(jnp.int32)
     cot = cotangent.reshape(rows, depth)
     attn_sum, resid, normed_two = join(x, norm_gains, norm_shifts, shares, picks)
+    normed_two, up_rest, down_rest = lax.optimization_barrier((normed_two, up_rest, down_rest))
     normed_two_rest = others(normed_two)
+    ups, downs = [up_weight] + up_rest, [down_weight] + down_rest
     slope, act, layer_out, g_branch, sums3 = feed(
         info, normed_two, biases, ups, downs, resid, cot, bias_down.reshape(1, depth), norm_gains, norm_shifts
     )
@@ -1057,14 +1057,15 @@
     )
     g_attn_rest = others(g_attn)
     g_pre, normed_two_rest = lax.optimization_barrier((g_pre, normed_two_rest))
+    g_mixed = mixed_back(here, g_attn, w_out, slots, [])
+    g_pre, g_mixed = lax.optimization_barrier((g_pre, g_mixed))
     grad_feed, bias_up_sum = feed_grad(
         up_weight, down_weight, biases[:hidden], act, g_pre,
         [normed_two] + normed_two_rest, [g_branch] + g_branch_rest,
     )
     grad_feed = grad_feed.reshape(2 * hidden, depth)
-    g_attn, g_attn_rest, grad_feed = lax.optimization_barrier((g_attn, g_attn_rest, grad_feed))
+    g_mixed, g_attn_rest, grad_feed = lax.optimization_barrier((g_mixed, g_attn_rest, grad_feed))
     grad_feed = lax.psum(grad_feed, "dp")
-    g_mixed = mixed_back(here, g_attn, w_out, slots, [])
     for r, g in enumerate(g_attn_rest):
         g_mixed = mixed_back(place(r + 1), g, w_out, slots, [g_mixed])
 

time: 549 us -> 547 us (level)
  transfers between devices with their start and end apart: 12 -> 12, of which waited for: 5 -> 5; matrix products, arithmetic and copies ran while one was open for 4% -> 4% of each run, Pallas kernels for 74% -> 77%
where the time goes in v1:
time: 547 us; the launch traced here: 540 us
  Pallas kernels  424 us (78%)
  waiting for transfers between devices  63 us (12%)
  other arithmetic  15.3 us (3%)
  between operations  15.1 us (3%)
  local copies, waits for them, and re-layouts  11.5 us (2%)
  starting transfers between devices  11.1 us (2%)
    pallas_call x1, Pallas kernels, tail(): pl.pallas_call(functools.partial(tail_kernel, bits=bits, groups=groups, s...  114 us
    pallas_call x1, Pallas kernels, attend_back(): pl.pallas_call(functools.partial(attend_back_kernel, blk=blk, blocks=bloc...  79.8 us
    pallas_call x4, Pallas kernels, attend(): pl.pallas_call(functools.partial(attend_kernel, blk=blk), grid_spec=pltpu...  68.1 us
    ppermute x9, waiting for transfers between devices, shift(): lax.ppermute(x, axis, [((i + step) % count, i) for i in range(count)])  61.8 us
    pallas_call x1, Pallas kernels, feed(): pl.pallas_call(functools.partial(feed_kernel, groups=groups, chunks=chunk...  39.9 us
    pallas_call x1, Pallas kernels, feed_back(): pl.pallas_call(functools.partial(feed_back_kernel, groups=groups, chunks=...  34.2 us
    pallas_call x1, Pallas kernels, feed_grad(): pl.pallas_call(functools.partial(feed_grad_kernel, groups=groups), grid=(...  33.6 us
    pallas_call x2, Pallas kernels, project(): pl.pallas_call(kernel, grid_spec=pltpu.PrefetchScalarGridSpec(num_scalar_...  15 us
  transfers between devices with their start and end apart: 12, of which 5 were waited for; matrix products, arithmetic and copies ran while one was open for 4% of the time, Pallas kernels for 77%

profile of v1, /device:TPU:0, one launch (start us, length us, event | category | flops | bytes accessed | tf_op | source)
XLA Modules:
  0.0 539.7 jit_solution(12583755699856533810)
XLA Ops:
  14.4 3.7 fusion
  18.1 3.0 pad_maximum_fusion
  21.2 3.7 first_norm.2.refs_0_
  24.9 7.5 %project.2.refs_6_ = bf16[2048,1536]{1,0:T(8,128)(2,1)} custom-call(s32[1]{0:T(128)} %bitcast.1.at.at_ref, bf16[1024,1024]{1,0:T(8,128)(2,1)} %first_norm.2.refs_0_, bf16[1024,512]{1,0:T(8,128)(2,1)} %wq_ref.1, bf16[1024,512]{1,0:T(8,128)(2,1)} %wk_ref.1, bf16[1024,512]{1,0:T(8,128)(2,1)} %wv_ref.1, f32[2048,128]{1,0:T(8,128)} %get-tuple-element.166.refs_4_.cos_ref, ...), custom_call_target="tpu_custom_call" | custom-call | flops 1048576 | bytes 1048576 | tf_op jit(solution)/shard_map/project/pallas_call | solution.py:50
  32.4 35.0 %collective-permute-done.3 = bf16[2048]{0:T(1024)(128)(2,1)S(1)} collective-permute-done((bf16[2048]{0:T(1024)(128)(2,1)}, bf16[2048]{0:T(1024)(128)(2,1)S(1)}, u32[]{:S(2)}, u32[]{:S(2)}) %collective-permute-start.3) | collective-permute-done | bytes 4128 | tf_op jit(solution)/shard_map/ppermute | solution.py:968
  70.1 3.7 first_norm.3.refs_0_.refs_1_
  73.8 7.5 %project.3.q_ref.k_ref.v_ref = bf16[2048,1536]{1,0:T(8,128)(2,1)} custom-call(s32[1]{0:T(128)S(6)} %select_n.67.at.at_ref, bf16[1024,1024]{1,0:T(8,128)(2,1)} %first_norm.3.refs_0_.refs_1_, bf16[1024,512]{1,0:T(8,128)(2,1)} %wq_ref.1, bf16[1024,512]{1,0:T(8,128)(2,1)} %wk_ref.1, bf16[1024,512]{1,0:T(8,128)(2,1)} %wv_ref.1, ...), custom_call_target="tpu_custom_call", output_to_operand_aliasing={{}: (7, {})} | custom-call | flops 1048576 | bytes 1048576 | tf_op jit(solution)/shard_map/project/pallas_call | solution.py:50
  81.3 19.4 %attend.4 = (bf16[2048,512]{1,0:T(8,128)(2,1)}, f32[4,2,2048]{2,1,0:T(2,128)}, bf16[512,1024]{1,0:T(8,128)(2,1)}) custom-call(s32[1]{0:T(128)S(6)} %add.78.at_ref, s32[1]{0:T(128)S(6)} %copy.55.len_ref, bf16[2048,1536]{1,0:T(8,128)(2,1)} %project.3.q_ref.k_ref.v_ref, bf16[2048,1536]{1,0:T(8,128)(2,1)} %project.3.q_ref.k_ref.v_ref, ...), custom_call_target="tpu_custom_call" | custom-call | flops 1048576 | bytes 1048576 | tf_op jit(solution)/shard_map/attend/pallas_call | solution.py:125
  100.8 9.2 %attend.5 = (bf16[2048,512]{1,0:T(8,128)(2,1)}, f32[4,2,2048]{2,1,0:T(2,128)}, f32[512,1024]{1,0:T(8,128)}) custom-call(s32[1]{0:T(128)S(6)} %add.75.at_ref, s32[1]{0:T(128)S(6)} %copy.55.len_ref, bf16[2048,1536]{1,0:T(8,128)(2,1)} %project.3.q_ref.k_ref.v_ref, ...), custom_call_target="tpu_custom_call", output_to_operand_aliasing={{0}: (6, {}), {1}: (7, {})} | custom-call | flops 1048576 | bytes 1048576 | tf_op jit(solution)/shard_map/attend/pallas_call | solution.py:125
  110.0 24.8 %attend.6 = (bf16[2048,512]{1,0:T(8,128)(2,1)}, f32[4,2,2048]{2,1,0:T(2,128)}, bf16[512,1024]{1,0:T(8,128)(2,1)}) custom-call(s32[1]{0:T(128)S(6)} %add.80.at_ref, s32[1]{0:T(128)S(6)} %copy.55.len_ref, bf16[2048,1536]{1,0:T(8,128)(2,1)} %project.3.q_ref.k_ref.v_ref, ...), custom_call_target="tpu_custom_call", output_to_operand_aliasing={{0}: (6, {}), {1}: (7, {})} | custom-call | flops 1048576 | bytes 1048576 | tf_op jit(solution)/shard_map/attend/pallas_call | solution.py:125
  139.1 14.8 %attend.7 = (bf16[2048,512]{1,0:T(8,128)(2,1)}, f32[4,2,2048]{2,1,0:T(2,128)}, f32[512,1024]{1,0:T(8,128)}) custom-call(s32[1]{0:T(128)S(6)} %add.79.at_ref, s32[1]{0:T(128)S(6)} %copy.55.len_ref, bf16[2048,1536]{1,0:T(8,128)(2,1)} %project.3.q_ref.k_ref.v_ref, ...), custom_call_target="tpu_custom_call", output_to_operand_aliasing={{0}: (6, {}), {1}: (7, {})} | custom-call | flops 1048576 | bytes 1048576 | tf_op jit(solution)/shard_map/attend/pallas_call | solution.py:125
  153.9 5.3 collective-permute-done.5.refs_3_
  160.2 10.9 %join.1 = (f32[1024,1024]{1,0:T(8,128)}, f32[1024,1024]{1,0:T(8,128)}, bf16[1024,1024]{1,0:T(8,128)(2,1)}) custom-call(s32[4]{0:T(128)} %pad_add_fusion.1.pick_ref, bf16[1024,1024]{1,0:T(8,128)(2,1)} %bitcast.18, f32[4,1024]{1,0:T(4,128)} %gain_ref.7, f32[4,1024]{1,0:T(4,128)} %refs_6_.2, f32[512,1024]{1,0:T(8,128)} %get-tuple-element.67.refs_0_, ...), custom_call_target="tpu_custom_call" | custom-call | tf_op jit(solution)/shard_map/join/pallas_call | solution.py:590
  172.9 39.9 %feed.1 = (bf16[1024,4096]{1,0:T(8,128)(2,1)}, bf16[1024,2048]{1,0:T(8,128)(2,1)}, bf16[1024,1024]{1,0:T(8,128)(2,1)}, bf16[1024,1024]{1,0:T(8,128)(2,1)}, f32[8,1024]{1,0:T(8,128)}) custom-call(s32[2]{0:T(128)} %pad_add_fusion.info_ref, bf16[1024,1024]{1,0:T(8,128)(2,1)} %get-tuple-element.80.refs_0_.refs_5_, f32[8,1,512]{2,1,0:T(1,128)} %maximum_convert_fusion.refs_1_, ...), custom_call_target="tpu_custom_call" | custom-call | flops 1048576 | bytes 1048576 | tf_op jit(solution)/shard_map/feed/pallas_call | solution.py:354
  214.3 34.2 %feed_back.1 = (bf16[1024,2048]{1,0:T(8,128)(2,1)}, f32[1024,1024]{1,0:T(8,128)}, bf16[1024,1024]{1,0:T(8,128)(2,1)}, f32[8,1024]{1,0:T(8,128)}) custom-call(s32[2]{0:T(128)} %pad_add_fusion.info_ref, bf16[1024,1024]{1,0:T(8,128)(2,1)} %get-tuple-element.87.refs_0_.refs_7_, bf16[1024,4096]{1,0:T(8,128)(2,1)} %get-tuple-element.88.refs_1_, ...), custom_call_target="tpu_custom_call" | custom-call | flops 1048576 | bytes 1048576 | tf_op jit(solution)/shard_map/feed_back/pallas_call | solution.py:457
  249.7 4.8 mixed_back.2.refs_0_
  254.5 10.9 %collective-permute-done.8.refs_8_ = bf16[1024,1024]{1,0:T(8,128)(2,1)} collective-permute-done((bf16[1024,1024]{1,0:T(8,128)(2,1)}, bf16[1024,1024]{1,0:T(8,128)(2,1)}, u32[]{:S(2)}, u32[]{:S(2)}) %collective-permute-start.8) | collective-permute-done | bytes 2097184 | tf_op jit(solution)/shard_map/ppermute | solution.py:968
  265.4 33.6 %feed_grad.1 = (bf16[2,2048,1024]{2,1,0:T(8,128)(2,1)}, f32[4,1,512]{2,1,0:T(1,128)}) custom-call(bf16[1024,2048]{1,0:T(8,128)(2,1)} %refs_0_.1, bf16[2048,1024]{1,0:T(8,128)(2,1)} %refs_1_.5, f32[4,1,512]{2,1,0:T(1,128)} %slice.69.refs_2_, bf16[1024,2048]{1,0:T(8,128)(2,1)} %get-tuple-element.94.refs_3_, bf16[1024,2048]{1,0:T(8,128)(2,1)} %get-tuple-element.95.refs_4_, ...), custom_call_target="tpu_custom_call" | custom-call | flops 25769803776 | bytes 20971520 | tf_op jit(solution)/shard_map/feed_grad/pallas_call | solution.py:526
  299.0 10.6 %collective-permute-done.7.x_ref.refs_3_ = bf16[1024,1024]{1,0:T(8,128)(2,1)S(1)} collective-permute-done((bf16[1024,1024]{1,0:T(8,128)(2,1)}, bf16[1024,1024]{1,0:T(8,128)(2,1)S(1)}, u32[]{:S(2)}, u32[]{:S(2)}) %collective-permute-start.7) | collective-permute-done | bytes 2097184 | tf_op jit(solution)/shard_map/ppermute | solution.py:968
  312.0 5.1 mixed_back.3.do_ref
  317.1 79.8 %attend_back.1 = (bf16[2048,512]{1,0:T(8,128)(2,1)}, bf16[2048,512]{1,0:T(8,128)(2,1)}, bf16[2048,512]{1,0:T(8,128)(2,1)}) custom-call(s32[1]{0:T(128)S(6)} %copy.55.len_ref, bf16[2048,1536]{1,0:T(8,128)(2,1)} %project.3.q_ref.k_ref.v_ref, bf16[2048,1536]{1,0:T(8,128)(2,1)} %project.3.q_ref.k_ref.v_ref, bf16[2048,1536]{1,0:T(8,128)(2,1)} %project.3.q_ref.k_ref.v_ref, ...), custom_call_target="tpu_custom_call" | custom-call | flops 1048576 | bytes 1048576 | tf_op jit(solution)/shard_map/attend_back/pallas_call | solution.py:229
  396.9 114.2 %tail.1 = (bf16[4096,512]{1,0:T(8,128)(2,1)}, bf16[1024,1024]{1,0:T(8,128)(2,1)}, f32[16,1024]{1,0:T(8,128)}) custom-call(bf16[2048,512]{1,0:T(8,128)(2,1)} %get-tuple-element.101.gq_ref, bf16[2048,512]{1,0:T(8,128)(2,1)} %get-tuple-element.102.gk_ref, bf16[2048,512]{1,0:T(8,128)(2,1)} %get-tuple-element.103.gv_ref, ...), custom_call_target="tpu_custom_call" | custom-call | flops 524288 | bytes 524288 | tf_op jit(solution)/shard_map/tail/pallas_call | solution.py:899
  511.1 5.4 convert_bitcast_fusion
  520.8 10.6 %widen.1 = (f32[1024,2048]{1,0:T(8,128)}, f32[2048,1024]{1,0:T(8,128)}) custom-call(bf16[4096,1024]{1,0:T(8,128)(2,1)} %all-reduce.3.cloned.1.call-done.up_ref.down_ref, bf16[4096,1024]{1,0:T(8,128)(2,1)} %all-reduce.3.cloned.1.call-done.up_ref.down_ref), custom_call_target="tpu_custom_call" | custom-call | tf_op jit(solution)/shard_map/widen/pallas_call | solution.py:617
  (79 shorter events, 27.0 us)
Async XLA Ops:
  7.2 164.0 %all-gather.3.cloned.1.call-start = ((), (), s32[]{:S(2)}) async-start(), calls=%async_computation | async-start | bytes 4456448 | tf_op jit(solution)/shard_map/all_gather | solution.py:1006
  7.2 60.2 %collective-permute-start = (bf16[1024,1024]{1,0:T(8,128)(2,1)}, bf16[1024,1024]{1,0:T(8,128)(2,1)S(1)}, u32[]{:S(2)}, u32[]{:S(2)}) collective-permute-start(bf16[1024,1024]{1,0:T(8,128)(2,1)} %bitcast.16), channel_id=1, source_target_pairs={{1,0},{0,1},{3,2},{2,3},{5,4},{4,5},{7,6},{6,7},{9,8},{8,9},{11,10... | collective-permute-start | bytes 6291464 | tf_op jit(solution)/shard_map/ppermute | solution.py:968
  11.2 56.2 %collective-permute-start.1 = (bf16[64,2048]{1,0:T(8,128)(2,1)S(1)}, bf16[64,2048]{1,0:T(8,128)(2,1)S(1)}, u32[]{:S(2)}, u32[]{:S(2)}) collective-permute-start(bf16[64,2048]{1,0:T(8,128)(2,1)S(1)} %constant_dynamic-slice_fusion.1), channel_id=1, source_target_pairs={{1,0},{0,1},{3,2},{2,3},{5,4},{4,5},{7,6},{6,7},{9,8},{8,9},{11,10... | collective-permute-start | bytes 786440 | tf_op jit(solution)/shard_map/ppermute | solution.py:968
  12.3 55.1 %collective-permute-start.2 = (bf16[128,1024]{1,0:T(8,128)(2,1)S(1)}, bf16[128,1024]{1,0:T(8,128)(2,1)S(1)}, u32[]{:S(2)}, u32[]{:S(2)}) collective-permute-start(bf16[128,1024]{1,0:T(8,128)(2,1)S(1)} %constant_dynamic-slice_fusion), channel_id=1, source_target_pairs={{1,0},{0,1},{3,2},{2,3},{5,4},{4,5},{7,6},{6,7},{9,8},{8,9},{11,10... | collective-permute-start | bytes 786440 | tf_op jit(solution)/shard_map/ppermute | solution.py:968
  14.3 53.1 %collective-permute-start.3 = (bf16[2048]{0:T(1024)(128)(2,1)}, bf16[2048]{0:T(1024)(128)(2,1)S(1)}, u32[]{:S(2)}, u32[]{:S(2)}) collective-permute-start(bf16[2048]{0:T(1024)(128)(2,1)} %param.21), channel_id=1, source_target_pairs={{1,0},{0,1},{3,2},{2,3},{5,4},{4,5},{7,6},{6,7},{9,8},{8,9},{11,10... | collective-permute-start | bytes 12296 | tf_op jit(solution)/shard_map/ppermute | solution.py:968
  67.4 2.7 copy-start.1
  68.1 103.6 %all-gather.5.cloned.1.call-start = ((), (), s32[]{:S(2)}) async-start(), calls=%async_computation.1 | async-start | bytes 4456448 | tf_op jit(solution)/shard_map/all_gather | solution.py:1006
  68.9 451.9 %all-reduce.3.cloned.1.call-start = ((), (), s32[]{:S(2)}) async-start(), calls=%async_computation.2 | async-start | bytes 16777216 | tf_op jit(solution)/shard_map/psum | solution.py:1068
  100.7 38.3 %collective-permute-start.4 = (bf16[512,1024]{1,0:T(8,128)(2,1)}, bf16[512,1024]{1,0:T(8,128)(2,1)S(1)}, u32[]{:S(2)}, u32[]{:S(2)}) collective-permute-start(bf16[512,1024]{1,0:T(8,128)(2,1)} %get-tuple-element.68), channel_id=1, source_target_pairs={{1,0},{0,1},{3,2},{2,3},{5,4},{4,5},{7,6},{6,7},{9,8},{8,9},{11,10... | collective-permute-start | bytes 3145736 | tf_op jit(solution)/shard_map/ppermute | solution.py:968
  110.0 26.7 %copy-start.12 = (bf16[2048]{0:T(1024)(128)(2,1)S(1)}, bf16[2048]{0:T(1024)(128)(2,1)}, u32[]{:S(2)}) copy-start(bf16[2048]{0:T(1024)(128)(2,1)} %param.21) | copy-start | bytes 12292
  110.0 26.7 %copy-start.13 = (bf16[1024]{0:T(1024)(128)(2,1)S(1)}, bf16[1024]{0:T(1024)(128)(2,1)}, u32[]{:S(2)}) copy-start(bf16[1024]{0:T(1024)(128)(2,1)} %param.23) | copy-start | bytes 6148
  134.7 24.5 %collective-permute-start.5 = (bf16[512,1024]{1,0:T(8,128)(2,1)}, bf16[512,1024]{1,0:T(8,128)(2,1)S(1)}, u32[]{:S(2)}, u32[]{:S(2)}) collective-permute-start(bf16[512,1024]{1,0:T(8,128)(2,1)} %get-tuple-element.76), channel_id=1, source_target_pairs={{1,0},{0,1},{3,2},{2,3},{5,4},{4,5},{7,6},{6,7},{9,8},{8,9},{11,10... | collective-permute-start | bytes 3145736 | tf_op jit(solution)/shard_map/ppermute | solution.py:968
  139.1 14.9 %copy-start.3 = (bf16[512,1024]{1,0:T(8,128)(2,1)}, bf16[512,1024]{1,0:T(8,128)(2,1)S(1)}, u32[]{:S(2)}) copy-start(bf16[512,1024]{1,0:T(8,128)(2,1)S(1)} %collective-permute-done.4.refs_2_) | copy-start | bytes 3145732
  159.3 1.0 copy-start.4
  171.7 82.8 %collective-permute-start.6 = (bf16[1024,1024]{1,0:T(8,128)(2,1)}, bf16[1024,1024]{1,0:T(8,128)(2,1)}, u32[]{:S(2)}, u32[]{:S(2)}) collective-permute-start(bf16[1024,1024]{1,0:T(8,128)(2,1)} %get-tuple-element.80.refs_0_.refs_5_), channel_id=1, source_target_pairs={{1,0},{0,1},{3,2},{2,3},{5,4},{4,5},{7,6},{6,7},{9,8},{8,9},{11,10... | collective-permute-start | bytes 6291464 | tf_op jit(solution)/shard_map/ppermute | solution.py:968
  172.9 40.8 %copy-start.7 = (f32[8,1,512]{2,1,0:T(1,128)S(1)}, f32[8,1,512]{2,1,0:T(1,128)}, u32[]{:S(2)}) copy-start(f32[8,1,512]{2,1,0:T(1,128)} %maximum_convert_fusion.refs_1_) | copy-start | bytes 49156
  212.8 52.7 %collective-permute-start.8 = (bf16[1024,1024]{1,0:T(8,128)(2,1)}, bf16[1024,1024]{1,0:T(8,128)(2,1)}, u32[]{:S(2)}, u32[]{:S(2)}) collective-permute-start(bf16[1024,1024]{1,0:T(8,128)(2,1)} %get-tuple-element.87.refs_0_.refs_7_), channel_id=1, source_target_pairs={{1,0},{0,1},{3,2},{2,3},{5,4},{4,5},{7,6},{6,7},{9,8},{8,9},{11,10... | collective-permute-start | bytes 6291464 | tf_op jit(solution)/shard_map/ppermute | solution.py:968
  248.4 61.1 %collective-permute-start.7 = (bf16[1024,1024]{1,0:T(8,128)(2,1)}, bf16[1024,1024]{1,0:T(8,128)(2,1)S(1)}, u32[]{:S(2)}, u32[]{:S(2)}) collective-permute-start(bf16[1024,1024]{1,0:T(8,128)(2,1)} %get-tuple-element.92.x_ref.refs_2_), channel_id=1, source_target_pairs={{1,0},{0,1},{3,2},{2,3},{5,4},{4,5},{7,6},{6,7},{9,8},{8,9},{11,10... | collective-permute-start | bytes 6291464 | tf_op jit(solution)/shard_map/ppermute | solution.py:968
  309.6 1.3 copy-start
  309.6 1.3 copy-start.10
  309.6 1.3 copy-start.9
  309.6 1.4 copy-start.11
  516.5 1.8 copy-start.8
  520.8 10.6 %copy-start.2 = (bf16[1024,1024]{1,0:T(8,128)(2,1)S(1)}, bf16[1024,1024]{1,0:T(8,128)(2,1)}, u32[]{:S(2)}) copy-start(bf16[1024,1024]{1,0:T(8,128)(2,1)} %get-tuple-element.108) | copy-start | bytes 6291460
  (2 other events, 1.5 us)
Sparse Core Ops, SparseCore 0:
  68.2 52.1 all-gather.2
  122.6 49.0 all-gather.4
  309.7 202.9 all-reduce.2

commit v2 on v1

--- a/solution.py
+++ b/solution.py
@@ -83,22 +83,44 @@
     def step(j, carry, diag):
         start = pl.multiple_of(j * blk, blk)
         kb = k_ref[pl.ds(start, blk), :]
-        out = []
-        for h in range(2):
-            m, l, acc = carry[h]
-            s = dotg(kb, qs[h], NT)
+        sub = min(256, blk)
+        n = blk // sub
+        if diag:
+            key = lax.broadcasted_iota(jnp.int32, (sub, blk), 0)
+            qry = lax.broadcasted_iota(jnp.int32, (sub, blk), 1)
+        state = [carry[h] for h in range(2)]
+        chains = [(h, t) for t in range(n) for h in range(2)]
+        live = {}
+
+        def first(c):
+            h, t = chains[c]
+            live[c] = dotg(kb[t * sub : t * sub + sub], qs[h], NT)
+
+        def middle(c):
+            h, t = chains[c]
+            s = live[c]
             if diag:
-                key = lax.broadcasted_iota(jnp.int32, (blk, blk), 0)
-                qry = lax.broadcasted_iota(jnp.int32, (blk, blk), 1)
-                s = jnp.where((key <= qry) & (key + start < length), s, -1e30)
+                s = jnp.where((key + t * sub <= qry) & (key + t * sub + start < length), s, -1e30)
+            m, l, acc = state[h]
             mn = jnp.maximum(m, jnp.max(s, axis=0, keepdims=True))
             p = jnp.exp(s - mn)
             al = jnp.exp(m - mn)
-            l = l * al + jnp.sum(p, axis=0, keepdims=True)
-            vb = vt[HD * h : HD * h + HD, pl.ds(start, blk)]
-            acc = acc * al + dotg(vb, p.astype(BF))
-            out.append((mn, l, acc))
-        return tuple(out)
+            state[h] = (mn, l * al + jnp.sum(p, axis=0, keepdims=True), acc)
+            live[c] = (p.astype(BF), al)
+
+        def last(c):
+            h, t = chains[c]
+            p, al = live.pop(c)
+            m, l, acc = state[h]
+            state[h] = (m, l, acc * al + dotg(vt[HD * h : HD * h + HD, pl.ds(start + t * sub, sub)], p))
+
+        stages = (first, middle, last)
+        for i in range(len(chains) + 4):
+            for k in range(3):
+                c = i - 2 * k
+                if 0 <= c < len(chains):
+                    stages[k](c)
+        return tuple(state)
 
     init = tuple(
         (jnp.full((1, blk), -1e30, F32), jnp.zeros((1, blk), F32), jnp.zeros((HD, blk), F32))
@@ -291,22 +313,32 @@
     lax.fori_loop(0, rows // blk, step, 0)
 
 
-def feed_kernel(info_ref, *refs, groups, chunks, sub):
-    x_ref, bias_ref, resid_hbm, cot_hbm, bd_ref, gain_ref, shift_ref = refs[:7]
-    ups, downs = refs[7 : 7 + groups], refs[7 + groups : 7 + 2 * groups]
-    slope_ref, act_ref, out_ref, gb_ref, sums_ref, acc, resid_ref, cot_ref, sems = refs[7 + 2 * groups :]
+def feed_kernel(info_ref, *refs, groups, chunks, sub, own):
+    x_ref, bias_ref = refs[:2]
+    ups, downs, refs = refs[2 : 2 + groups], refs[2 + groups : 2 + 2 * groups], refs[2 + 2 * groups :]
     step = pl.program_id(0)
     rows = x_ref.shape[0]
-    late = [
-        pltpu.make_async_copy(resid_hbm, resid_ref, sems.at[0]),
-        pltpu.make_async_copy(cot_hbm, cot_ref, sems.at[1]),
-    ]
+    if own:
+        bd_ref, slope_ref, act_ref, acc = refs
+        late = []
+    else:
+        resid_hbm, cot_hbm, before_hbm, gain_ref, shift_ref = refs[:5]
+        slope_ref, out_ref, gb_ref, sums_ref, acc, resid_ref, cot_ref, sems = refs[5:]
+        late = [
+            pltpu.make_async_copy(resid_hbm, resid_ref, sems.at[0]),
+            pltpu.make_async_copy(cot_hbm, cot_ref, sems.at[1]),
+        ]
 
     @pl.when(step == 0)
     def _():
+        if own:
+            acc[...] = jnp.zeros_like(acc) + bd_ref[...].astype(F32)
+        else:
+            before = pltpu.make_async_copy(before_hbm, acc, sems.at[2])
+            before.start()
+            before.wait()
         for c in late:
             c.start()
-        acc[...] = jnp.zeros_like(acc) + bd_ref[...].astype(F32)
 
     for g in range(groups):
 
@@ -316,9 +348,12 @@
                 act, slope = gelu_both(dotg(x_ref[r : r + sub], ups[g][...]) + bias_ref[0])
                 slope_ref[r : r + sub] = slope.astype(BF)
                 act = act.astype(BF)
-                if g == 0:
+                if own:
                     act_ref[r : r + sub] = act
                 acc[r : r + sub] += dotg(act, downs[g][...])
+
+    if own:
+        return
 
     @pl.when(step == groups * chunks - 1)
     def _():
@@ -343,61 +378,56 @@
         loop_rows(rows, blk, body)
 
 
-def feed(info, x, biases, ups, downs, resid, cot, bias_down, gains, shifts, cols=512):
+def feed(info, x, biases, ups, downs, own=None, rest=None, cols=512):
     rows, depth = x.shape
     groups, hidden = len(ups), ups[0].shape[1]
     chunks = hidden // cols
     once = lambda shape: pl.BlockSpec(shape, lambda s, *_: (0, 0), pipeline_mode=pl.Buffered(1))
     anyspace = pl.BlockSpec(memory_space=pl.ANY)
-    own = lambda g: (lambda s, *_: (0, jnp.clip(s - g * chunks, 0, chunks - 1)))
-    own_t = lambda g: (lambda s, *_: (jnp.clip(s - g * chunks, 0, chunks - 1), 0))
+    part = lambda g: (lambda s, *_: (0, jnp.clip(s - g * chunks, 0, chunks - 1)))
+    part_t = lambda g: (lambda s, *_: (jnp.clip(s - g * chunks, 0, chunks - 1), 0))
+    wide = pl.BlockSpec((rows, cols), lambda s, *_: (0, s))
+    low = jax.ShapeDtypeStruct((rows, depth), BF)
+    slope = jax.ShapeDtypeStruct((rows, groups * hidden), BF)
+    if rest is None:
+        more, args = [once((1, depth))], [own]
+        out_specs = [wide, wide, once((rows, depth))]
+        out_shape = [slope, slope, jax.ShapeDtypeStruct((rows, depth), F32)]
+        scratch = []
+    else:
+        before, resid, cot, gains, shifts = rest
+        more, args = [anyspace] * 3 + [once(gains.shape)] * 2, [resid, cot, before, gains, shifts]
+        out_specs = [wide, once((rows, depth)), once((rows, depth)), once((8, depth))]
+        out_shape = [slope, low, low, jax.ShapeDtypeStruct((8, depth), F32)]
+        scratch = [
+            pltpu.VMEM((rows, depth), F32),
+            pltpu.VMEM((rows, depth), F32),
+            pltpu.VMEM((rows, depth), BF),
+            pltpu.SemaphoreType.DMA((3,)),
+        ]
     return pl.pallas_call(
-        functools.partial(feed_kernel, groups=groups, chunks=chunks, sub=min(512, rows)),
+        functools.partial(feed_kernel, groups=groups, chunks=chunks, sub=min(512, rows), own=rest is None),
         grid_spec=pltpu.PrefetchScalarGridSpec(
             num_scalar_prefetch=1,
             grid=(groups * chunks,),
-            in_specs=[
-                once((rows, depth)),
-                pl.BlockSpec((1, 1, cols), lambda s, *_: (s, 0, 0)),
-                anyspace,
-                anyspace,
-                once((1, depth)),
-                once(gains.shape),
-                once(gains.shape),
-            ]
-            + [pl.BlockSpec((depth, cols), own(g)) for g in range(groups)]
-            + [pl.BlockSpec((cols, depth), own_t(g)) for g in range(groups)],
-            out_specs=[
-                pl.BlockSpec((rows, cols), lambda s, *_: (0, s)),
-                pl.BlockSpec((rows, cols), own(0)),
-                once((rows, depth)),
-                once((rows, depth)),
-                once((8, depth)),
-            ],
-            scratch_shapes=[
-                pltpu.VMEM((rows, depth), F32),
-                pltpu.VMEM((rows, depth), F32),
-                pltpu.VMEM((rows, depth), BF),
-                pltpu.SemaphoreType.DMA((2,)),
-            ],
+            in_specs=[once((rows, depth)), pl.BlockSpec((1, 1, cols), lambda s, *_: (s, 0, 0))]
+            + [pl.BlockSpec((depth, cols), part(g)) for g in range(groups)]
+            + [pl.BlockSpec((cols, depth), part_t(g)) for g in range(groups)]
+            + more,
+            out_specs=out_specs,
+            scratch_shapes=scratch,
         ),
-        out_shape=[
-            jax.ShapeDtypeStruct((rows, groups * hidden), BF),
-            jax.ShapeDtypeStruct((rows, hidden), BF),
-            jax.ShapeDtypeStruct((rows, depth), BF),
-            jax.ShapeDtypeStruct((rows, depth), BF),
-            jax.ShapeDtypeStruct((8, depth), F32),
-        ],
+        out_shape=out_shape,
         compiler_params=pltpu.CompilerParams(vmem_limit_bytes=60 * MIB),
         cost_estimate=pl.CostEstimate(flops=rows * depth, bytes_accessed=rows * depth, transcendentals=0),
         name="feed",
-    )(info, x, biases.reshape(-1, 1, cols), resid, cot, bias_down, gains, shifts, *ups, *downs)
+    )(info, x, biases.reshape(-1, 1, cols), *ups, *downs, *args)
 
 
 def feed_back_kernel(info_ref, *refs, groups, chunks, sub):
-    gb_ref, slope_ref, resid_hbm, attn_hbm, cot_hbm, gain_ref = refs[:6]
-    ups, downs = refs[6 : 6 + groups], refs[6 + groups : 6 + 2 * groups]
-    gp_ref, gr_ref, ga_ref, sums_ref, acc, resid_ref, attn_ref, cot_ref, sems = refs[6 + 2 * groups :]
+    gb_ref, own_slope, rest_slope, resid_hbm, attn_hbm, cot_hbm, gain_ref = refs[:7]
+    ups, downs = refs[7 : 7 + groups], refs[7 + groups : 7 + 2 * groups]
+    gp_ref, gr_ref, ga_ref, sums_ref, acc, resid_ref, attn_ref, cot_ref, sems = refs[7 + 2 * groups :]
     step = pl.program_id(0)
     rows = gb_ref.shape[0]
     late = [
@@ -417,6 +447,7 @@
         def _():
             for r in range(0, rows, sub):
                 grad = dotg(gb_ref[r : r + sub], downs[g][...], NT)
+                slope_ref = rest_slope if g else own_slope
                 low = (grad * slope_ref[r : r + sub].astype(F32)).astype(BF)
                 if g == 0:
                     gp_ref[r : r + sub] = low
@@ -446,7 +477,7 @@
         loop_rows(rows, blk, body)
 
 
-def feed_back(info, gb, slope, ups, downs, resid, attn_sum, cot, gains, cols=512):
+def feed_back(info, gb, own_slope, rest_slope, ups, downs, resid, attn_sum, cot, gains, cols=512):
     rows, depth = gb.shape
     groups, hidden = len(ups), ups[0].shape[1]
     chunks = hidden // cols
@@ -461,7 +492,8 @@
             grid=(groups * chunks,),
             in_specs=[
                 once((rows, depth)),
-                pl.BlockSpec((rows, cols), lambda s, *_: (0, s)),
+                pl.BlockSpec((rows, cols), own(0)),
+                pl.BlockSpec((rows, cols), lambda s, *_: (0, jnp.maximum(s - chunks, 0))),
                 anyspace,
                 anyspace,
                 anyspace,
@@ -492,7 +524,7 @@
         compiler_params=pltpu.CompilerParams(vmem_limit_bytes=60 * MIB),
         cost_estimate=pl.CostEstimate(flops=rows * depth, bytes_accessed=rows * depth, transcendentals=0),
         name="feed_back",
-    )(info, gb, slope, resid, attn_sum, cot, gains, *ups, *downs)
+    )(info, gb, own_slope, rest_slope, resid, attn_sum, cot, gains, *ups, *downs)
 
 
 def feed_grad_kernel(*refs, groups):
@@ -1013,14 +1045,13 @@
     x_rest = others(x)
     normed_one = first_norm(x, norm_gains, norm_shifts)
     weights = (w_query, w_key, w_value)
-    up_pieces, down_pieces, bias_rest = others(up_piece), others(down_piece), others(bias_up)
     joint = project(here, normed_one, *weights, cosine, sine)
-    joint, x_rest, up_pieces, down_pieces, bias_rest = lax.optimization_barrier(
-        (joint, x_rest, up_pieces, down_pieces, bias_rest)
-    )
+    joint, x_rest, up_piece, down_piece, bias = lax.optimization_barrier((joint, x_rest, up_piece, down_piece, bias_up))
+    up_pieces, down_pieces, bias_rest = others(up_piece), others(down_piece), others(bias)
     normed_one_rest = [first_norm(v, norm_gains, norm_shifts) for v in x_rest]
     for r, n in enumerate(normed_one_rest):
         joint = project(place(r + 1), n, *weights, cosine, sine, joint)
+    joint, up_pieces, down_pieces, bias_rest = lax.optimization_barrier((joint, up_pieces, down_pieces, bias_rest))
     blk = min(512, rows)
     each = rows // blk
     odd = lambda r: lax.rem(place(r), 2)
@@ -1045,15 +1076,17 @@
     info = jnp.stack([lengths[0], me * rows]).astype(jnp.int32)
     cot = cotangent.reshape(rows, depth)
     attn_sum, resid, normed_two = join(x, norm_gains, norm_shifts, shares, picks)
-    normed_two, up_rest, down_rest = lax.optimization_barrier((normed_two, up_rest, down_rest))
     normed_two_rest = others(normed_two)
+    slope, act, branch = feed(
+        info, normed_two, biases[:hidden], [up_weight], [down_weight], own=bias_down.reshape(1, depth)
+    )
+    slope_rest, layer_out, g_branch, sums3 = feed(
+        info, normed_two, biases[hidden:], up_rest, down_rest, rest=(branch, resid, cot, norm_gains, norm_shifts)
+    )
     ups, downs = [up_weight] + up_rest, [down_weight] + down_rest
-    slope, act, layer_out, g_branch, sums3 = feed(
-        info, normed_two, biases, ups, downs, resid, cot, bias_down.reshape(1, depth), norm_gains, norm_shifts
-    )
     g_branch_rest = others(g_branch)
     g_pre, g_resid, g_attn, sums21 = feed_back(
-        info, g_branch, slope, ups, downs, resid, attn_sum, cot, norm_gains
+        info, g_branch, slope, slope_rest, ups, downs, resid, attn_sum, cot, norm_gains
     )
     g_attn_rest = others(g_attn)
     g_pre, normed_two_rest = lax.optimization_barrier((g_pre, normed_two_rest))

time: 547 us -> 529 us (0.967)
  waiting for transfers between devices: 63 us -> 47.1 us
  Pallas kernels: 424 us -> 418 us
    ppermute x9, waiting for transfers between devices: 61.8 us -> 46.3 us  [shift(): lax.ppermute(x, axis, [((i + step) % count, i) for i in range(count)])]
    pallas_call x4, Pallas kernels: 68.1 us -> 58.1 us  [attend(): pl.pallas_call(functools.partial(attend_kernel, blk=blk), grid_spec=pltpu...]
    pallas_call x1 -> x2, Pallas kernels: 39.9 us -> 46.5 us  [feed(): pl.pallas_call(functools.partial(feed_kernel, groups=groups, chunks=chunk...]
  transfers between devices with their start and end apart: 12 -> 12, of which waited for: 5 -> 4; matrix products, arithmetic and copies ran while one was open for 4% -> 4% of each run, Pallas kernels for 77% -> 78%
where the time goes in v2:
time: 529 us; the launch traced here: 522 us
  Pallas kernels  418 us (79%)
  waiting for transfers between devices  47.1 us (9%)
  between operations  15.1 us (3%)
  other arithmetic  14.7 us (3%)
  starting transfers between devices  13.4 us (3%)
  local copies, waits for them, and re-layouts  12.9 us (2%)
    pallas_call x1, Pallas kernels, tail(): pl.pallas_call(functools.partial(tail_kernel, bits=bits, groups=groups, s...  112 us
    pallas_call x1, Pallas kernels, attend_back(): pl.pallas_call(functools.partial(attend_back_kernel, blk=blk, blocks=bloc...  79.8 us
    pallas_call x4, Pallas kernels, attend(): pl.pallas_call(functools.partial(attend_kernel, blk=blk), grid_spec=pltpu...  58.1 us
    pallas_call x2, Pallas kernels, feed(): pl.pallas_call(functools.partial(feed_kernel, groups=groups, chunks=chunk...  46.5 us
    ppermute x9, waiting for transfers between devices, shift(): lax.ppermute(x, axis, [((i + step) % count, i) for i in range(count)])  46.3 us
    pallas_call x1, Pallas kernels, feed_back(): pl.pallas_call(functools.partial(feed_back_kernel, groups=groups, chunks=...  33.9 us
    pallas_call x1, Pallas kernels, feed_grad(): pl.pallas_call(functools.partial(feed_grad_kernel, groups=groups), grid=(...  33.6 us
    pallas_call x2, Pallas kernels, project(): pl.pallas_call(kernel, grid_spec=pltpu.PrefetchScalarGridSpec(num_scalar_...  15 us
  transfers between devices with their start and end apart: 12, of which 4 were waited for; matrix products, arithmetic and copies ran while one was open for 4% of the time, Pallas kernels for 78%

profile of v2, /device:TPU:0, one launch (start us, length us, event | category | flops | bytes accessed | tf_op | source)
XLA Modules:
  0.0 521.5 jit_solution(8666510220089805286)
XLA Ops:
  10.2 3.7 first_norm.2.refs_0_
  14.0 3.7 fusion
  20.7 7.5 %project.2.refs_6_ = bf16[2048,1536]{1,0:T(8,128)(2,1)} custom-call(s32[1]{0:T(128)} %bitcast.1.at.at_ref, bf16[1024,1024]{1,0:T(8,128)(2,1)} %first_norm.2.refs_0_, bf16[1024,512]{1,0:T(8,128)(2,1)} %wq_ref.1, bf16[1024,512]{1,0:T(8,128)(2,1)} %wk_ref.1, bf16[1024,512]{1,0:T(8,128)(2,1)} %wv_ref.1, f32[2048,128]{1,0:T(8,128)} %get-tuple-element.174.refs_4_.cos_ref, ...), custom_call_target="tpu_custom_call" | custom-call | flops 1048576 | bytes 1048576 | tf_op jit(solution)/shard_map/project/pallas_call | solution.py:50
  30.2 25.9 %collective-permute-done.x_ref = bf16[1024,1024]{1,0:T(8,128)(2,1)S(1)} collective-permute-done((bf16[1024,1024]{1,0:T(8,128)(2,1)}, bf16[1024,1024]{1,0:T(8,128)(2,1)S(1)}, u32[]{:S(2)}, u32[]{:S(2)}) %collective-permute-start) | collective-permute-done | bytes 2097184 | tf_op jit(solution)/shard_map/ppermute | solution.py:1000
  59.8 3.7 first_norm.3.refs_0_.refs_1_
  63.6 7.5 %project.3.q_ref.k_ref.v_ref = bf16[2048,1536]{1,0:T(8,128)(2,1)} custom-call(s32[1]{0:T(128)S(6)} %select_n.67.at.at_ref, bf16[1024,1024]{1,0:T(8,128)(2,1)} %first_norm.3.refs_0_.refs_1_, bf16[1024,512]{1,0:T(8,128)(2,1)} %wq_ref.1, bf16[1024,512]{1,0:T(8,128)(2,1)} %wk_ref.1, bf16[1024,512]{1,0:T(8,128)(2,1)} %wv_ref.1, ...), custom_call_target="tpu_custom_call", output_to_operand_aliasing={{}: (7, {})} | custom-call | flops 1048576 | bytes 1048576 | tf_op jit(solution)/shard_map/project/pallas_call | solution.py:50
  73.8 16.2 %attend.4 = (bf16[2048,512]{1,0:T(8,128)(2,1)}, f32[4,2,2048]{2,1,0:T(2,128)}, bf16[512,1024]{1,0:T(8,128)(2,1)}) custom-call(s32[1]{0:T(128)S(6)} %add.78.at_ref, s32[1]{0:T(128)S(6)} %copy.55.len_ref, bf16[2048,1536]{1,0:T(8,128)(2,1)} %project.3.q_ref.k_ref.v_ref, bf16[2048,1536]{1,0:T(8,128)(2,1)} %project.3.q_ref.k_ref.v_ref, ...), custom_call_target="tpu_custom_call" | custom-call | flops 1048576 | bytes 1048576 | tf_op jit(solution)/shard_map/attend/pallas_call | solution.py:147
  90.1 8.5 %attend.5 = (bf16[2048,512]{1,0:T(8,128)(2,1)}, f32[4,2,2048]{2,1,0:T(2,128)}, f32[512,1024]{1,0:T(8,128)}) custom-call(s32[1]{0:T(128)S(6)} %add.75.at_ref, s32[1]{0:T(128)S(6)} %copy.55.len_ref, bf16[2048,1536]{1,0:T(8,128)(2,1)} %project.3.q_ref.k_ref.v_ref, ...), custom_call_target="tpu_custom_call", output_to_operand_aliasing={{0}: (6, {}), {1}: (7, {})} | custom-call | flops 1048576 | bytes 1048576 | tf_op jit(solution)/shard_map/attend/pallas_call | solution.py:147
  98.6 20.5 %attend.6 = (bf16[2048,512]{1,0:T(8,128)(2,1)}, f32[4,2,2048]{2,1,0:T(2,128)}, bf16[512,1024]{1,0:T(8,128)(2,1)}) custom-call(s32[1]{0:T(128)S(6)} %add.80.at_ref, s32[1]{0:T(128)S(6)} %copy.55.len_ref, bf16[2048,1536]{1,0:T(8,128)(2,1)} %project.3.q_ref.k_ref.v_ref, ...), custom_call_target="tpu_custom_call", output_to_operand_aliasing={{0}: (6, {}), {1}: (7, {})} | custom-call | flops 1048576 | bytes 1048576 | tf_op jit(solution)/shard_map/attend/pallas_call | solution.py:147
  123.5 12.9 %attend.7 = (bf16[2048,512]{1,0:T(8,128)(2,1)}, f32[4,2,2048]{2,1,0:T(2,128)}, f32[512,1024]{1,0:T(8,128)}) custom-call(s32[1]{0:T(128)S(6)} %add.79.at_ref, s32[1]{0:T(128)S(6)} %copy.55.len_ref, bf16[2048,1536]{1,0:T(8,128)(2,1)} %project.3.q_ref.k_ref.v_ref, ...), custom_call_target="tpu_custom_call", output_to_operand_aliasing={{0}: (6, {}), {1}: (7, {})} | custom-call | flops 1048576 | bytes 1048576 | tf_op jit(solution)/shard_map/attend/pallas_call | solution.py:147
  136.4 6.0 %collective-permute-done.5.refs_3_ = bf16[512,1024]{1,0:T(8,128)(2,1)S(1)} collective-permute-done((bf16[512,1024]{1,0:T(8,128)(2,1)}, bf16[512,1024]{1,0:T(8,128)(2,1)S(1)}, u32[]{:S(2)}, u32[]{:S(2)}) %collective-permute-start.5) | collective-permute-done | bytes 1048608 | tf_op jit(solution)/shard_map/ppermute | solution.py:1000
  143.4 11.2 %join.1 = (f32[1024,1024]{1,0:T(8,128)}, f32[1024,1024]{1,0:T(8,128)}, bf16[1024,1024]{1,0:T(8,128)(2,1)}) custom-call(s32[4]{0:T(128)} %pad_add_fusion.1.pick_ref, bf16[1024,1024]{1,0:T(8,128)(2,1)} %bitcast.18, f32[4,1024]{1,0:T(4,128)} %gain_ref.7, f32[4,1024]{1,0:T(4,128)} %refs_8_.1, f32[512,1024]{1,0:T(8,128)} %get-tuple-element.74.refs_0_, ...), custom_call_target="tpu_custom_call" | custom-call | tf_op jit(solution)/shard_map/join/pallas_call | solution.py:622
  156.6 20.5 %feed.2 = (bf16[1024,2048]{1,0:T(8,128)(2,1)}, bf16[1024,2048]{1,0:T(8,128)(2,1)}, f32[1024,1024]{1,0:T(8,128)}) custom-call(s32[2]{0:T(128)} %pad_add_fusion.info_ref, bf16[1024,1024]{1,0:T(8,128)(2,1)} %get-tuple-element.84.refs_0_.refs_5_, f32[4,1,512]{2,1,0:T(1,128)} %get-tuple-element.169.refs_1_.refs_2_, bf16[1024,2048]{1,0:T(8,128)(2,1)} %refs_0_.1, ...), custom_call_target="tpu_custom_call" | custom-call | flops 1048576 | bytes 1048576 | tf_op jit(solution)/shard_map/feed/pallas_call | solution.py:408
  177.2 25.9 %feed.3 = (bf16[1024,2048]{1,0:T(8,128)(2,1)}, bf16[1024,1024]{1,0:T(8,128)(2,1)}, bf16[1024,1024]{1,0:T(8,128)(2,1)}, f32[8,1024]{1,0:T(8,128)}) custom-call(s32[2]{0:T(128)} %pad_add_fusion.info_ref, bf16[1024,1024]{1,0:T(8,128)(2,1)} %get-tuple-element.84.refs_0_.refs_5_, f32[4,1,512]{2,1,0:T(1,128)} %get-tuple-element.170.refs_1_, ...), custom_call_target="tpu_custom_call" | custom-call | flops 1048576 | bytes 1048576 | tf_op jit(solution)/shard_map/feed/pallas_call | solution.py:408
  203.2 33.9 %feed_back.1 = (bf16[1024,2048]{1,0:T(8,128)(2,1)}, f32[1024,1024]{1,0:T(8,128)}, bf16[1024,1024]{1,0:T(8,128)(2,1)}, f32[8,1024]{1,0:T(8,128)}) custom-call(s32[2]{0:T(128)} %pad_add_fusion.info_ref, bf16[1024,1024]{1,0:T(8,128)(2,1)} %get-tuple-element.92.refs_0_.refs_7_, bf16[1024,2048]{1,0:T(8,128)(2,1)} %get-tuple-element.93.refs_1_, ...), custom_call_target="tpu_custom_call" | custom-call | flops 1048576 | bytes 1048576 | tf_op jit(solution)/shard_map/feed_back/pallas_call | solution.py:488
  240.5 4.8 mixed_back.2.refs_0_
  245.3 6.7 %collective-permute-done.8.refs_8_ = bf16[1024,1024]{1,0:T(8,128)(2,1)} collective-permute-done((bf16[1024,1024]{1,0:T(8,128)(2,1)}, bf16[1024,1024]{1,0:T(8,128)(2,1)}, u32[]{:S(2)}, u32[]{:S(2)}) %collective-permute-start.8) | collective-permute-done | bytes 2097184 | tf_op jit(solution)/shard_map/ppermute | solution.py:1000
  252.0 33.6 %feed_grad.1 = (bf16[2,2048,1024]{2,1,0:T(8,128)(2,1)}, f32[4,1,512]{2,1,0:T(1,128)}) custom-call(bf16[1024,2048]{1,0:T(8,128)(2,1)} %refs_0_.1, bf16[2048,1024]{1,0:T(8,128)(2,1)} %refs_1_.5, f32[4,1,512]{2,1,0:T(1,128)} %get-tuple-element.169.refs_1_.refs_2_, bf16[1024,2048]{1,0:T(8,128)(2,1)} %get-tuple-element.100.refs_3_, ...), custom_call_target="tpu_custom_call" | custom-call | flops 25769803776 | bytes 20971520 | tf_op jit(solution)/shard_map/feed_grad/pallas_call | solution.py:558
  285.6 7.7 %collective-permute-done.7.x_ref.refs_3_ = bf16[1024,1024]{1,0:T(8,128)(2,1)S(1)} collective-permute-done((bf16[1024,1024]{1,0:T(8,128)(2,1)}, bf16[1024,1024]{1,0:T(8,128)(2,1)S(1)}, u32[]{:S(2)}, u32[]{:S(2)}) %collective-permute-start.7) | collective-permute-done | bytes 2097184 | tf_op jit(solution)/shard_map/ppermute | solution.py:1000
  295.8 5.2 mixed_back.3.do_ref
  301.0 79.8 %attend_back.1 = (bf16[2048,512]{1,0:T(8,128)(2,1)}, bf16[2048,512]{1,0:T(8,128)(2,1)}, bf16[2048,512]{1,0:T(8,128)(2,1)}) custom-call(s32[1]{0:T(128)S(6)} %copy.55.len_ref, bf16[2048,1536]{1,0:T(8,128)(2,1)} %project.3.q_ref.k_ref.v_ref, bf16[2048,1536]{1,0:T(8,128)(2,1)} %project.3.q_ref.k_ref.v_ref, bf16[2048,1536]{1,0:T(8,128)(2,1)} %project.3.q_ref.k_ref.v_ref, ...), custom_call_target="tpu_custom_call" | custom-call | flops 1048576 | bytes 1048576 | tf_op jit(solution)/shard_map/attend_back/pallas_call | solution.py:251
  380.8 112.2 %tail.1 = (bf16[4096,512]{1,0:T(8,128)(2,1)}, bf16[1024,1024]{1,0:T(8,128)(2,1)}, f32[16,1024]{1,0:T(8,128)}) custom-call(bf16[2048,512]{1,0:T(8,128)(2,1)} %get-tuple-element.107.gq_ref, bf16[2048,512]{1,0:T(8,128)(2,1)} %get-tuple-element.108.gk_ref, bf16[2048,512]{1,0:T(8,128)(2,1)} %get-tuple-element.109.gv_ref, ...), custom_call_target="tpu_custom_call" | custom-call | flops 524288 | bytes 524288 | tf_op jit(solution)/shard_map/tail/pallas_call | solution.py:931
  493.0 5.4 %convert_bitcast_fusion = (f32[512,1024]{0,1:T(8,128)S(1)}, f32[1024,512]{1,0:T(8,128)}, f32[1024,512]{1,0:T(8,128)}, f32[1024,512]{1,0:T(8,128)}) fusion(bf16[4096,512]{1,0:T(8,128)(2,1)} %get-tuple-element.115), kind=kLoop, calls=%fused_computation | loop fusion | flops 2097152 | bytes 12582912 | tf_op jit(solution)/shard_map/convert_element_type | solution.py:1120
  502.7 10.6 %widen.1 = (f32[1024,2048]{1,0:T(8,128)}, f32[2048,1024]{1,0:T(8,128)}) custom-call(bf16[4096,1024]{1,0:T(8,128)(2,1)} %all-reduce.3.cloned.1.call-done.up_ref.down_ref, bf16[4096,1024]{1,0:T(8,128)(2,1)} %all-reduce.3.cloned.1.call-done.up_ref.down_ref), custom_call_target="tpu_custom_call" | custom-call | tf_op jit(solution)/shard_map/widen/pallas_call | solution.py:649
  (80 shorter events, 32.7 us)
Async XLA Ops:
  7.2 169.9 %all-gather.3.cloned.1.call-start = ((), (), s32[]{:S(2)}) async-start(), calls=%async_computation | async-start | bytes 4456448 | tf_op jit(solution)/shard_map/all_gather | solution.py:1038
  7.2 48.8 %collective-permute-start = (bf16[1024,1024]{1,0:T(8,128)(2,1)}, bf16[1024,1024]{1,0:T(8,128)(2,1)S(1)}, u32[]{:S(2)}, u32[]{:S(2)}) collective-permute-start(bf16[1024,1024]{1,0:T(8,128)(2,1)} %bitcast.16), channel_id=1, source_target_pairs={{1,0},{0,1},{3,2},{2,3},{5,4},{4,5},{7,6},{6,7},{9,8},{8,9},{11,10... | collective-permute-start | bytes 6291464 | tf_op jit(solution)/shard_map/ppermute | solution.py:1000
  20.7 37.4 %copy-start.11 = (bf16[2048]{0:T(1024)(128)(2,1)S(1)}, bf16[2048]{0:T(1024)(128)(2,1)}, u32[]{:S(2)}) copy-start(bf16[2048]{0:T(1024)(128)(2,1)} %param.21) | copy-start | bytes 12292
  56.1 3.8 copy-start.1
  56.1 15.0 %collective-permute-start.1 = (bf16[64,2048]{1,0:T(8,128)(2,1)S(1)}, bf16[64,2048]{1,0:T(8,128)(2,1)S(1)}, u32[]{:S(2)}, u32[]{:S(2)}) collective-permute-start(bf16[64,2048]{1,0:T(8,128)(2,1)S(1)} %constant_dynamic-slice_fusion.1), channel_id=1, source_target_pairs={{1,0},{0,1},{3,2},{2,3},{5,4},{4,5},{7,6},{6,7},{9,8},{8,9},{11,10... | collective-permute-start | bytes 786440 | tf_op jit(solution)/shard_map/ppermute | solution.py:1000
  57.8 13.3 %collective-permute-start.2 = (bf16[128,1024]{1,0:T(8,128)(2,1)S(1)}, bf16[128,1024]{1,0:T(8,128)(2,1)S(1)}, u32[]{:S(2)}, u32[]{:S(2)}) collective-permute-start(bf16[128,1024]{1,0:T(8,128)(2,1)S(1)} %constant_dynamic-slice_fusion), channel_id=1, source_target_pairs={{1,0},{0,1},{3,2},{2,3},{5,4},{4,5},{7,6},{6,7},{9,8},{8,9},{11,10... | collective-permute-start | bytes 786440 | tf_op jit(solution)/shard_map/ppermute | solution.py:1000
  58.1 13.0 %collective-permute-start.3 = (bf16[2048]{0:T(1024)(128)(2,1)S(1)}, bf16[2048]{0:T(1024)(128)(2,1)S(1)}, u32[]{:S(2)}, u32[]{:S(2)}) collective-permute-start(bf16[2048]{0:T(1024)(128)(2,1)S(1)} %copy-done.11), channel_id=1, source_target_pairs={{1,0},{0,1},{3,2},{2,3},{5,4},{4,5},{7,6},{6,7},{9,8},{8,9},{11,10... | collective-permute-start | bytes 12296 | tf_op jit(solution)/shard_map/ppermute | solution.py:1000
  71.8 105.3 %all-gather.5.cloned.1.call-start = ((), (), s32[]{:S(2)}) async-start(), calls=%async_computation.1 | async-start | bytes 4456448 | tf_op jit(solution)/shard_map/all_gather | solution.py:1038
  72.6 430.1 %all-reduce.3.cloned.1.call-start = ((), (), s32[]{:S(2)}) async-start(), calls=%async_computation.2 | async-start | bytes 16777216 | tf_op jit(solution)/shard_map/psum | solution.py:1101
  90.0 33.5 %collective-permute-start.4 = (bf16[512,1024]{1,0:T(8,128)(2,1)}, bf16[512,1024]{1,0:T(8,128)(2,1)S(1)}, u32[]{:S(2)}, u32[]{:S(2)}) collective-permute-start(bf16[512,1024]{1,0:T(8,128)(2,1)} %get-tuple-element.75), channel_id=1, source_target_pairs={{1,0},{0,1},{3,2},{2,3},{5,4},{4,5},{7,6},{6,7},{9,8},{8,9},{11,10... | collective-permute-start | bytes 3145736 | tf_op jit(solution)/shard_map/ppermute | solution.py:1000
  98.6 22.4 %copy-start.12 = (bf16[1024]{0:T(1024)(128)(2,1)S(1)}, bf16[1024]{0:T(1024)(128)(2,1)}, u32[]{:S(2)}) copy-start(bf16[1024]{0:T(1024)(128)(2,1)} %param.23) | copy-start | bytes 6148
  119.1 23.3 %collective-permute-start.5 = (bf16[512,1024]{1,0:T(8,128)(2,1)}, bf16[512,1024]{1,0:T(8,128)(2,1)S(1)}, u32[]{:S(2)}, u32[]{:S(2)}) collective-permute-start(bf16[512,1024]{1,0:T(8,128)(2,1)} %get-tuple-element.83), channel_id=1, source_target_pairs={{1,0},{0,1},{3,2},{2,3},{5,4},{4,5},{7,6},{6,7},{9,8},{8,9},{11,10... | collective-permute-start | bytes 3145736 | tf_op jit(solution)/shard_map/ppermute | solution.py:1000
  123.5 12.9 %copy-start.3 = (bf16[512,1024]{1,0:T(8,128)(2,1)}, bf16[512,1024]{1,0:T(8,128)(2,1)S(1)}, u32[]{:S(2)}) copy-start(bf16[512,1024]{1,0:T(8,128)(2,1)S(1)} %collective-permute-done.4.refs_2_) | copy-start | bytes 3145732
  142.4 1.0 copy-start.4
  154.6 82.6 %collective-permute-start.6 = (bf16[1024,1024]{1,0:T(8,128)(2,1)}, bf16[1024,1024]{1,0:T(8,128)(2,1)S(1)}, u32[]{:S(2)}, u32[]{:S(2)}) collective-permute-start(bf16[1024,1024]{1,0:T(8,128)(2,1)} %get-tuple-element.84.refs_0_.refs_5_), channel_id=1, source_target_pairs={{1,0},{0,1},{3,2},{2,3},{5,4},{4,5},{7,6},{6,7},{9,8},{8,9},{11,10... | collective-permute-start | bytes 6291464 | tf_op jit(solution)/shard_map/ppermute | solution.py:1000
  203.1 48.9 %collective-permute-start.8 = (bf16[1024,1024]{1,0:T(8,128)(2,1)}, bf16[1024,1024]{1,0:T(8,128)(2,1)}, u32[]{:S(2)}, u32[]{:S(2)}) collective-permute-start(bf16[1024,1024]{1,0:T(8,128)(2,1)} %get-tuple-element.92.refs_0_.refs_7_), channel_id=1, source_target_pairs={{1,0},{0,1},{3,2},{2,3},{5,4},{4,5},{7,6},{6,7},{9,8},{8,9},{11,10... | collective-permute-start | bytes 6291464 | tf_op jit(solution)/shard_map/ppermute | solution.py:1000
  237.2 1.4 copy-start.13
  238.5 54.8 %collective-permute-start.7 = (bf16[1024,1024]{1,0:T(8,128)(2,1)}, bf16[1024,1024]{1,0:T(8,128)(2,1)S(1)}, u32[]{:S(2)}, u32[]{:S(2)}) collective-permute-start(bf16[1024,1024]{1,0:T(8,128)(2,1)} %get-tuple-element.98.x_ref.refs_2_), channel_id=1, source_target_pairs={{1,0},{0,1},{3,2},{2,3},{5,4},{4,5},{7,6},{6,7},{9,8},{8,9},{11,10... | collective-permute-start | bytes 6291464 | tf_op jit(solution)/shard_map/ppermute | solution.py:1000
  293.4 1.3 copy-start
  293.4 1.3 copy-start.9
  293.4 1.3 copy-start.8
  293.4 1.4 copy-start.10
  498.4 1.8 copy-start.7
  502.7 10.6 %copy-start.2 = (bf16[1024,1024]{1,0:T(8,128)(2,1)S(1)}, bf16[1024,1024]{1,0:T(8,128)(2,1)}, u32[]{:S(2)}) copy-start(bf16[1024,1024]{1,0:T(8,128)(2,1)} %get-tuple-element.114) | copy-start | bytes 6291460
  (2 other events, 1.5 us)
Sparse Core Ops, SparseCore 0:
  71.9 51.0 all-gather.2
  125.2 49.2 all-gather.4
  293.5 202.0 all-reduce.2

commit v3 on v2

--- a/solution.py
+++ b/solution.py
@@ -38,13 +38,14 @@
     o_ref[:, 2 * width :] = dotg(x, wv_ref[...]).astype(BF)
 
 
-def project(where, x, w_query, w_key, w_value, cos, sin, joint=None, blk=256):
+def project(where, x, w_query, w_key, w_value, cos, sin, joint=None, part=0, parts=1, blk=256):
     rows, depth = x.shape
     width, slots = w_query.shape[1], cos.shape[0]
-    blk = min(blk, rows)
-    count = rows // blk
+    blk = min(blk, rows // parts)
+    whole = rows // blk
+    count = whole // parts
     weight = pl.BlockSpec((depth, width), lambda i, at: (0, 0))
-    angle = pl.BlockSpec((blk, 128), lambda i, at: (at[0] * count + i, 0))
+    angle = pl.BlockSpec((blk, 128), lambda i, at: (at[0] * whole + part * count + i, 0))
     kernel = lambda at, *refs: qkv_kernel(*refs[:6], refs[-1])
     held = [] if joint is None else [joint]
     return pl.pallas_call(
@@ -52,9 +53,9 @@
         grid_spec=pltpu.PrefetchScalarGridSpec(
             num_scalar_prefetch=1,
             grid=(count,),
-            in_specs=[pl.BlockSpec((blk, depth), lambda i, at: (i, 0)), weight, weight, weight, angle, angle]
+            in_specs=[pl.BlockSpec((blk, depth), lambda i, at: (part * count + i, 0)), weight, weight, weight, angle, angle]
             + [pl.BlockSpec(memory_space=pl.ANY)] * len(held),
-            out_specs=pl.BlockSpec((blk, 3 * width), lambda i, at: (at[0] * count + i, 0)),
+            out_specs=pl.BlockSpec((blk, 3 * width), lambda i, at: (at[0] * whole + part * count + i, 0)),
         ),
         out_shape=jax.ShapeDtypeStruct((slots, 3 * width), BF),
         input_output_aliases={7: 0} if held else {},
@@ -179,23 +180,39 @@
     len_ref, q_ref, k_ref, v_ref, o_ref, do_ref, lse_ref, cos_ref, sin_ref,
     dq_ref, dk_ref, dv_ref, kt, dlt, dqt, *, blk, blocks,
 ):
-    j = pl.program_id(1)
     length = len_ref[0]
-
-    @pl.when(j == 0)
-    def _():
-        kt[...] = jnp.transpose(k_ref[...])
-        dqt[...] = jnp.zeros_like(dqt)
-
-        def body(i, _):
-            at = pl.ds(pl.multiple_of(i * blk, blk), blk)
-            both = jnp.transpose(do_ref[at, :].astype(F32) * o_ref[at, :].astype(F32))
-            for h in range(2):
-                dlt[h : h + 1, at] = jnp.sum(both[HD * h : HD * h + HD], axis=0, keepdims=True)
-            return 0
-
-        lax.fori_loop(0, blocks, body, 0)
-
+    kt[...] = jnp.transpose(k_ref[...])
+    dqt[...] = jnp.zeros_like(dqt)
+
+    def products(i, _):
+        at = pl.ds(pl.multiple_of(i * blk, blk), blk)
+        both = jnp.transpose(do_ref[at, :].astype(F32) * o_ref[at, :].astype(F32))
+        for h in range(2):
+            dlt[h : h + 1, at] = jnp.sum(both[HD * h : HD * h + HD], axis=0, keepdims=True)
+        return 0
+
+    lax.fori_loop(0, blocks, products, 0)
+
+    def keys(j, _):
+        attend_back_keys(
+            j, length, q_ref, k_ref, v_ref, do_ref, lse_ref, cos_ref, sin_ref, dk_ref, dv_ref, kt, dlt, dqt, blk, blocks
+        )
+        return 0
+
+    lax.fori_loop(0, blocks, keys, 0)
+
+    def turn(i, _):
+        at = pl.ds(pl.multiple_of(i * blk, blk), blk)
+        grad = jnp.transpose(dqt[:, at]) * 0.125
+        dq_ref[at, :] = rotate(grad, cos_ref[at, :], -sin_ref[at, :]).astype(BF)
+        return 0
+
+    lax.fori_loop(0, blocks, turn, 0)
+
+
+def attend_back_keys(
+    j, length, q_ref, k_ref, v_ref, do_ref, lse_ref, cos_ref, sin_ref, dk_ref, dv_ref, kt, dlt, dqt, blk, blocks
+):
     js = pl.multiple_of(j * blk, blk)
     lane = lax.broadcasted_iota(jnp.int32, (blk, 128), 1)
     kb = k_ref[pl.ds(js, blk), :] * jnp.asarray(0.125, BF)
@@ -228,34 +245,23 @@
     c = step(j, ((z, z), (z, z)), True)
     c = lax.fori_loop(j + 1, blocks, lambda i, c: step(i, c, False), c)
     grad = jnp.where(lane < HD, c[0][0], c[1][0]) * 0.125
-    dk_ref[...] = rotate(grad, cos_ref[pl.ds(js, blk), :], -sin_ref[pl.ds(js, blk), :]).astype(BF)
-    dv_ref[...] = jnp.where(lane < HD, c[0][1], c[1][1]).astype(BF)
-
-    @pl.when(j == blocks - 1)
-    def _():
-        def body(i, _):
-            at = pl.ds(pl.multiple_of(i * blk, blk), blk)
-            grad = jnp.transpose(dqt[:, at]) * 0.125
-            dq_ref[at, :] = rotate(grad, cos_ref[at, :], -sin_ref[at, :]).astype(BF)
-            return 0
-
-        lax.fori_loop(0, blocks, body, 0)
+    dk_ref[pl.ds(js, blk), :] = rotate(grad, cos_ref[pl.ds(js, blk), :], -sin_ref[pl.ds(js, blk), :]).astype(BF)
+    dv_ref[pl.ds(js, blk), :] = jnp.where(lane < HD, c[0][1], c[1][1]).astype(BF)
 
 
 def attend_back(length, joint, mixed, dmixed, lse, cos, sin, width, blk=512):
     rows = joint.shape[0]
     pairs, blocks = width // 128, rows // blk
-    full = lambda off: pl.BlockSpec((rows, 128), lambda p, j, *_: (0, off * pairs + p))
-    angle = pl.BlockSpec((rows, 128), lambda p, j, *_: (0, 0))
-    block = pl.BlockSpec((blk, 128), lambda p, j, *_: (j, p))
+    full = lambda off: pl.BlockSpec((rows, 128), lambda p, *_: (0, off * pairs + p))
+    angle = pl.BlockSpec((rows, 128), lambda p, *_: (0, 0))
     return pl.pallas_call(
         functools.partial(attend_back_kernel, blk=blk, blocks=blocks),
         grid_spec=pltpu.PrefetchScalarGridSpec(
             num_scalar_prefetch=1,
-            grid=(pairs, blocks),
+            grid=(pairs,),
             in_specs=[full(0), full(1), full(2), full(0), full(0)]
-            + [pl.BlockSpec((1, 2, rows), lambda p, j, *_: (p, 0, 0)), angle, angle],
-            out_specs=[full(0), block, block],
+            + [pl.BlockSpec((1, 2, rows), lambda p, *_: (p, 0, 0)), angle, angle],
+            out_specs=[full(0)] * 3,
             scratch_shapes=[
                 pltpu.VMEM((128, rows), BF),
                 pltpu.VMEM((2, rows), F32),
@@ -323,20 +329,16 @@
         late = []
     else:
         resid_hbm, cot_hbm, before_hbm, gain_ref, shift_ref = refs[:5]
-        slope_ref, out_ref, gb_ref, sums_ref, acc, resid_ref, cot_ref, sems = refs[5:]
+        slope_ref, out_ref, gb_ref, sums_ref, acc, resid_ref, before_ref, cot_ref, sems = refs[5:]
         late = [
             pltpu.make_async_copy(resid_hbm, resid_ref, sems.at[0]),
             pltpu.make_async_copy(cot_hbm, cot_ref, sems.at[1]),
+            pltpu.make_async_copy(before_hbm, before_ref, sems.at[2]),
         ]
 
     @pl.when(step == 0)
     def _():
-        if own:
-            acc[...] = jnp.zeros_like(acc) + bd_ref[...].astype(F32)
-        else:
-            before = pltpu.make_async_copy(before_hbm, acc, sems.at[2])
-            before.start()
-            before.wait()
+        acc[...] = jnp.zeros_like(acc) + bd_ref[...].astype(F32) if own else jnp.zeros_like(acc)
         for c in late:
             c.start()
 
@@ -366,7 +368,7 @@
         def body(r):
             at = pl.ds(r, blk)
             valid = valid_rows(info_ref, r, blk)
-            hat, scale = norm_parts(acc[at])
+            hat, scale = norm_parts(acc[at] + before_ref[at])
             out_ref[at] = (valid * (resid_ref[at] + hat * gain + shift)).astype(BF)
             g_out = valid * cot_ref[at].astype(F32)
             low = norm_back(g_out, hat, scale, gain).astype(BF)
@@ -400,6 +402,7 @@
         out_specs = [wide, once((rows, depth)), once((rows, depth)), once((8, depth))]
         out_shape = [slope, low, low, jax.ShapeDtypeStruct((8, depth), F32)]
         scratch = [
+            pltpu.VMEM((rows, depth), F32),
             pltpu.VMEM((rows, depth), F32),
             pltpu.VMEM((rows, depth), F32),
             pltpu.VMEM((rows, depth), BF),
@@ -572,25 +575,30 @@
     )(up, down, bias.reshape(-1, 1, cols), act, gp, *n2s, *gbs)
 
 
-def norm_kernel(x_ref, gain_ref, shift_ref, o_ref):
+def norm_kernel(at_ref, x_ref, gain_ref, shift_ref, *refs):
     hat, _ = norm_parts(x_ref[...].astype(F32))
-    o_ref[...] = (hat * gain_ref[0:1] + shift_ref[0:1]).astype(BF)
-
-
-def first_norm(x, gains, shifts, blk=512):
-    rows, depth = x.shape
-    blk = min(blk, rows)
-    whole = pl.BlockSpec(gains.shape, lambda i: (0, 0))
-    block = pl.BlockSpec((blk, depth), lambda i: (i, 0))
+    refs[-1][...] = (hat * gain_ref[0:1] + shift_ref[0:1]).astype(BF)
+
+
+def first_norm(where, x, gains, shifts, rows, held, blk=512):
+    part, depth = x.shape
+    blk = min(blk, part)
+    count = part // blk
+    whole = pl.BlockSpec(gains.shape, lambda i, at: (0, 0))
     return pl.pallas_call(
         norm_kernel,
-        grid=(rows // blk,),
-        in_specs=[block, whole, whole],
-        out_specs=block,
+        grid_spec=pltpu.PrefetchScalarGridSpec(
+            num_scalar_prefetch=1,
+            grid=(count,),
+            in_specs=[pl.BlockSpec((blk, depth), lambda i, at: (i, 0)), whole, whole]
+            + [pl.BlockSpec(memory_space=pl.ANY)] * len(held),
+            out_specs=pl.BlockSpec((blk, depth), lambda i, at: (at[0] * count + i, 0)),
+        ),
         out_shape=jax.ShapeDtypeStruct((rows, depth), BF),
+        input_output_aliases={4: 0} if held else {},
         compiler_params=pltpu.CompilerParams(vmem_limit_bytes=60 * MIB),
         name="first_norm",
-    )(x, gains, shifts)
+    )(where, x, gains, shifts, *held)
 
 
 def join_kernel(pick_ref, x_ref, gain_ref, shift_ref, *refs, blocks, each):
@@ -1042,16 +1050,26 @@
     cosine, sine = jnp.cos(angles), jnp.sin(angles)
     cosine = jnp.concatenate([cosine] * 4, axis=1)
     sine = jnp.concatenate([-sine, sine] * 2, axis=1)
-    x_rest = others(x)
-    normed_one = first_norm(x, norm_gains, norm_shifts)
+    halves = 2
+    index = lambda k: jnp.full((1,), k, jnp.int32)
+    x_rest = [others(v) for v in jnp.split(x, halves)]
+    normed_one = first_norm(index(0), x, norm_gains, norm_shifts, rows, [])
+    up_pieces = others(up_piece)
     weights = (w_query, w_key, w_value)
     joint = project(here, normed_one, *weights, cosine, sine)
-    joint, x_rest, up_piece, down_piece, bias = lax.optimization_barrier((joint, x_rest, up_piece, down_piece, bias_up))
-    up_pieces, down_pieces, bias_rest = others(up_piece), others(down_piece), others(bias)
-    normed_one_rest = [first_norm(v, norm_gains, norm_shifts) for v in x_rest]
-    for r, n in enumerate(normed_one_rest):
-        joint = project(place(r + 1), n, *weights, cosine, sine, joint)
-    joint, up_pieces, down_pieces, bias_rest = lax.optimization_barrier((joint, up_pieces, down_pieces, bias_rest))
+    normed_one_rest = [[] for _ in range(1, groups)]
+    for k in range(halves):
+        pieces = (down_piece, bias_up) if k == halves - 1 else up_pieces
+        joint, x_rest[k], pieces = lax.optimization_barrier((joint, x_rest[k], pieces))
+        if k < halves - 1:
+            up_pieces = pieces
+        else:
+            down_pieces, bias_rest = (others(v) for v in pieces)
+        for r in range(1, groups):
+            n = first_norm(index(k), x_rest[k][r - 1], norm_gains, norm_shifts, rows, normed_one_rest[r - 1])
+            normed_one_rest[r - 1] = [n]
+            joint = project(place(r), n, *weights, cosine, sine, joint, k, halves)
+    normed_one_rest = [v[0] for v in normed_one_rest]
     blk = min(512, rows)
     each = rows // blk
     odd = lambda r: lax.rem(place(r), 2)
@@ -1061,6 +1079,8 @@
         for r in range(1, groups):
             *held, share = attend(place(r) * each + ranks(0, k), lengths, joint, w_out, held, BF, blk)
             arrived[r - 1].append(to_owner(share, r))
+        if k == 0:
+            joint, down_pieces, bias_rest = lax.optimization_barrier((joint, down_pieces, bias_rest))
         if k == each - 1 and k > 0:
             joint, arrived = lax.optimization_barrier((joint, [v[:k] for v in arrived])), arrived
             joint, early = joint

time: 529 us -> 535 us (1.011)
  Pallas kernels: 418 us -> 424 us
    ppermute x9 -> x10, waiting for transfers between devices: 46.3 us -> 43.6 us  [shift(): lax.ppermute(x, axis, [((i + step) % count, i) for i in range(count)])]
    pallas_call x2 -> x3, Pallas kernels: 15 us -> 17.7 us  [project(): pl.pallas_call(kernel, grid_spec=pltpu.PrefetchScalarGridSpec(num_scalar_...]
    ppermute x9 -> x10, starting transfers between devices: 12.8 us -> 12.7 us  [shift(): lax.ppermute(x, axis, [((i + step) % count, i) for i in range(count)])]
  transfers between devices with their start and end apart: 12 -> 13, of which waited for: 4 -> 5; matrix products, arithmetic and copies ran while one was open for 4% -> 4% of each run, Pallas kernels for 78% -> 79%
where the time goes in v3:
time: 535 us; the launch traced here: 526 us
  Pallas kernels  424 us (79%)
  waiting for transfers between devices  43.7 us (8%)
  between operations  15.1 us (3%)
  other arithmetic  14.7 us (3%)
  local copies, waits for them, and re-layouts  14.6 us (3%)
  starting transfers between devices  13.3 us (2%)
    pallas_call x1, Pallas kernels, tail(): pl.pallas_call(functools.partial(tail_kernel, bits=bits, groups=groups, s...  116 us
    pallas_call x1, Pallas kernels, attend_back(): pl.pallas_call(functools.partial(attend_back_kernel, blk=blk, blocks=bloc...  79.6 us
    pallas_call x4, Pallas kernels, attend(): pl.pallas_call(functools.partial(attend_kernel, blk=blk), grid_spec=pltpu...  58 us
    pallas_call x2, Pallas kernels, feed(): pl.pallas_call(functools.partial(feed_kernel, groups=groups, chunks=chunk...  44.7 us
    ppermute x10, waiting for transfers between devices, shift(): lax.ppermute(x, axis, [((i + step) % count, i) for i in range(count)])  43.6 us
    pallas_call x1, Pallas kernels, feed_back(): pl.pallas_call(functools.partial(feed_back_kernel, groups=groups, chunks=...  34 us
    pallas_call x1, Pallas kernels, feed_grad(): pl.pallas_call(functools.partial(feed_grad_kernel, groups=groups), grid=(...  33.6 us
    pallas_call x3, Pallas kernels, project(): pl.pallas_call(kernel, grid_spec=pltpu.PrefetchScalarGridSpec(num_scalar_...  17.7 us
  transfers between devices with their start and end apart: 13, of which 5 were waited for; matrix products, arithmetic and copies ran while one was open for 4% of the time, Pallas kernels for 79%

profile of v3, /device:TPU:0, one launch (start us, length us, event | category | flops | bytes accessed | tf_op | source)
XLA Modules:
  0.0 525.8 jit_solution(3315800129632414565)
XLA Ops:
  13.0 3.7 first_norm.3.refs_0_
  23.5 7.5 %project.3.refs_6_ = bf16[2048,1536]{1,0:T(8,128)(2,1)} custom-call(s32[1]{0:T(128)} %bitcast.1.at.at_ref, bf16[1024,1024]{1,0:T(8,128)(2,1)} %first_norm.3.refs_0_, bf16[1024,512]{1,0:T(8,128)(2,1)} %wq_ref.1, bf16[1024,512]{1,0:T(8,128)(2,1)} %wk_ref.1, bf16[1024,512]{1,0:T(8,128)(2,1)} %wv_ref.1, f32[2048,128]{1,0:T(8,128)} %get-tuple-element.178.refs_4_.cos_ref, ...), custom_call_target="tpu_custom_call" | custom-call | flops 1048576 | bytes 1048576 | tf_op jit(solution)/shard_map/project/pallas_call | solution.py:51
  31.0 9.8 %collective-permute-done.1 = bf16[64,2048]{1,0:T(8,128)(2,1)} collective-permute-done((bf16[64,2048]{1,0:T(8,128)(2,1)S(1)}, bf16[64,2048]{1,0:T(8,128)(2,1)}, u32[]{:S(2)}, u32[]{:S(2)}) %collective-permute-start.1) | collective-permute-done | bytes 262176 | tf_op jit(solution)/shard_map/ppermute | solution.py:1008
  46.7 5.1 project.4.refs_6_
  51.7 13.6 %collective-permute-done.2.x_ref = bf16[512,1024]{1,0:T(8,128)(2,1)S(1)} collective-permute-done((bf16[512,1024]{1,0:T(8,128)(2,1)S(1)}, bf16[512,1024]{1,0:T(8,128)(2,1)S(1)}, u32[]{:S(2)}, u32[]{:S(2)}) %collective-permute-start.2) | collective-permute-done | bytes 1048608 | tf_op jit(solution)/shard_map/ppermute | solution.py:1008
  70.3 5.1 project.5.q_ref.k_ref.v_ref
  77.3 16.3 %attend.4 = (bf16[2048,512]{1,0:T(8,128)(2,1)}, f32[4,2,2048]{2,1,0:T(2,128)}, bf16[512,1024]{1,0:T(8,128)(2,1)}) custom-call(s32[1]{0:T(128)S(6)} %add.81.at_ref, s32[1]{0:T(128)S(6)} %copy.59.len_ref, bf16[2048,1536]{1,0:T(8,128)(2,1)} %project.5.q_ref.k_ref.v_ref, bf16[2048,1536]{1,0:T(8,128)(2,1)} %project.5.q_ref.k_ref.v_ref, ...), custom_call_target="tpu_custom_call" | custom-call | flops 1048576 | bytes 1048576 | tf_op jit(solution)/shard_map/attend/pallas_call | solution.py:148
  93.7 8.5 %attend.5 = (bf16[2048,512]{1,0:T(8,128)(2,1)}, f32[4,2,2048]{2,1,0:T(2,128)}, f32[512,1024]{1,0:T(8,128)}) custom-call(s32[1]{0:T(128)S(6)} %add.78.at_ref, s32[1]{0:T(128)S(6)} %copy.59.len_ref, bf16[2048,1536]{1,0:T(8,128)(2,1)} %project.5.q_ref.k_ref.v_ref, ...), custom_call_target="tpu_custom_call", output_to_operand_aliasing={{0}: (6, {}), {1}: (7, {})} | custom-call | flops 1048576 | bytes 1048576 | tf_op jit(solution)/shard_map/attend/pallas_call | solution.py:148
  102.2 20.3 %attend.6 = (bf16[2048,512]{1,0:T(8,128)(2,1)}, f32[4,2,2048]{2,1,0:T(2,128)}, bf16[512,1024]{1,0:T(8,128)(2,1)}) custom-call(s32[1]{0:T(128)S(6)} %add.83.at_ref, s32[1]{0:T(128)S(6)} %copy.59.len_ref, bf16[2048,1536]{1,0:T(8,128)(2,1)} %project.5.q_ref.k_ref.v_ref, ...), custom_call_target="tpu_custom_call", output_to_operand_aliasing={{0}: (6, {}), {1}: (7, {})} | custom-call | flops 1048576 | bytes 1048576 | tf_op jit(solution)/shard_map/attend/pallas_call | solution.py:148
  127.1 12.9 %attend.7 = (bf16[2048,512]{1,0:T(8,128)(2,1)}, f32[4,2,2048]{2,1,0:T(2,128)}, f32[512,1024]{1,0:T(8,128)}) custom-call(s32[1]{0:T(128)S(6)} %add.82.at_ref, s32[1]{0:T(128)S(6)} %copy.59.len_ref, bf16[2048,1536]{1,0:T(8,128)(2,1)} %project.5.q_ref.k_ref.v_ref, ...), custom_call_target="tpu_custom_call", output_to_operand_aliasing={{0}: (6, {}), {1}: (7, {})} | custom-call | flops 1048576 | bytes 1048576 | tf_op jit(solution)/shard_map/attend/pallas_call | solution.py:148
  140.0 6.4 %collective-permute-done.6.refs_3_ = bf16[512,1024]{1,0:T(8,128)(2,1)S(1)} collective-permute-done((bf16[512,1024]{1,0:T(8,128)(2,1)}, bf16[512,1024]{1,0:T(8,128)(2,1)S(1)}, u32[]{:S(2)}, u32[]{:S(2)}) %collective-permute-start.6) | collective-permute-done | bytes 1048608 | tf_op jit(solution)/shard_map/ppermute | solution.py:1008
  147.4 10.6 %join.1 = (f32[1024,1024]{1,0:T(8,128)}, f32[1024,1024]{1,0:T(8,128)}, bf16[1024,1024]{1,0:T(8,128)(2,1)}) custom-call(s32[4]{0:T(128)} %pad_add_fusion.1.pick_ref, bf16[1024,1024]{1,0:T(8,128)(2,1)} %bitcast.21, f32[4,1024]{1,0:T(4,128)} %gain_ref.9, f32[4,1024]{1,0:T(4,128)} %refs_8_.1, f32[512,1024]{1,0:T(8,128)} %get-tuple-element.76.refs_0_, ...), custom_call_target="tpu_custom_call" | custom-call | tf_op jit(solution)/shard_map/join/pallas_call | solution.py:630
  159.5 20.5 %feed.2 = (bf16[1024,2048]{1,0:T(8,128)(2,1)}, bf16[1024,2048]{1,0:T(8,128)(2,1)}, f32[1024,1024]{1,0:T(8,128)}) custom-call(s32[2]{0:T(128)} %pad_add_fusion.info_ref, bf16[1024,1024]{1,0:T(8,128)(2,1)} %get-tuple-element.86.refs_0_.refs_5_, f32[4,1,512]{2,1,0:T(1,128)} %get-tuple-element.173.refs_1_.refs_2_, bf16[1024,2048]{1,0:T(8,128)(2,1)} %refs_0_.1, ...), custom_call_target="tpu_custom_call" | custom-call | flops 1048576 | bytes 1048576 | tf_op jit(solution)/shard_map/feed/pallas_call | solution.py:411
  180.1 24.2 %feed.3 = (bf16[1024,2048]{1,0:T(8,128)(2,1)}, bf16[1024,1024]{1,0:T(8,128)(2,1)}, bf16[1024,1024]{1,0:T(8,128)(2,1)}, f32[8,1024]{1,0:T(8,128)}) custom-call(s32[2]{0:T(128)} %pad_add_fusion.info_ref, bf16[1024,1024]{1,0:T(8,128)(2,1)} %get-tuple-element.86.refs_0_.refs_5_, f32[4,1,512]{2,1,0:T(1,128)} %get-tuple-element.174.refs_1_, ...), custom_call_target="tpu_custom_call" | custom-call | flops 1048576 | bytes 1048576 | tf_op jit(solution)/shard_map/feed/pallas_call | solution.py:411
  204.8 34.0 %feed_back.1 = (bf16[1024,2048]{1,0:T(8,128)(2,1)}, f32[1024,1024]{1,0:T(8,128)}, bf16[1024,1024]{1,0:T(8,128)(2,1)}, f32[8,1024]{1,0:T(8,128)}) custom-call(s32[2]{0:T(128)} %pad_add_fusion.info_ref, bf16[1024,1024]{1,0:T(8,128)(2,1)} %get-tuple-element.94.refs_0_.refs_7_, bf16[1024,2048]{1,0:T(8,128)(2,1)} %get-tuple-element.95.refs_1_, ...), custom_call_target="tpu_custom_call" | custom-call | flops 1048576 | bytes 1048576 | tf_op jit(solution)/shard_map/feed_back/pallas_call | solution.py:491
  241.7 4.8 mixed_back.2.refs_0_
  246.5 6.7 %collective-permute-done.9.refs_8_ = bf16[1024,1024]{1,0:T(8,128)(2,1)} collective-permute-done((bf16[1024,1024]{1,0:T(8,128)(2,1)}, bf16[1024,1024]{1,0:T(8,128)(2,1)}, u32[]{:S(2)}, u32[]{:S(2)}) %collective-permute-start.9) | collective-permute-done | bytes 2097184 | tf_op jit(solution)/shard_map/ppermute | solution.py:1008
  253.2 33.6 %feed_grad.1 = (bf16[2,2048,1024]{2,1,0:T(8,128)(2,1)}, f32[4,1,512]{2,1,0:T(1,128)}) custom-call(bf16[1024,2048]{1,0:T(8,128)(2,1)} %refs_0_.1, bf16[2048,1024]{1,0:T(8,128)(2,1)} %refs_1_.7, f32[4,1,512]{2,1,0:T(1,128)} %get-tuple-element.173.refs_1_.refs_2_, bf16[1024,2048]{1,0:T(8,128)(2,1)} %get-tuple-element.102.refs_3_, ...), custom_call_target="tpu_custom_call" | custom-call | flops 25769803776 | bytes 20971520 | tf_op jit(solution)/shard_map/feed_grad/pallas_call | solution.py:561
  286.8 7.1 %collective-permute-done.8.x_ref.refs_3_ = bf16[1024,1024]{1,0:T(8,128)(2,1)S(1)} collective-permute-done((bf16[1024,1024]{1,0:T(8,128)(2,1)}, bf16[1024,1024]{1,0:T(8,128)(2,1)S(1)}, u32[]{:S(2)}, u32[]{:S(2)}) %collective-permute-start.8) | collective-permute-done | bytes 2097184 | tf_op jit(solution)/shard_map/ppermute | solution.py:1008
  296.4 5.1 mixed_back.3.do_ref
  301.5 79.6 %attend_back.1 = (bf16[2048,512]{1,0:T(8,128)(2,1)}, bf16[2048,512]{1,0:T(8,128)(2,1)}, bf16[2048,512]{1,0:T(8,128)(2,1)}) custom-call(s32[1]{0:T(128)S(6)} %copy.59.len_ref, bf16[2048,1536]{1,0:T(8,128)(2,1)} %project.5.q_ref.k_ref.v_ref, bf16[2048,1536]{1,0:T(8,128)(2,1)} %project.5.q_ref.k_ref.v_ref, bf16[2048,1536]{1,0:T(8,128)(2,1)} %project.5.q_ref.k_ref.v_ref, ...), custom_call_target="tpu_custom_call" | custom-call | flops 1048576 | bytes 1048576 | tf_op jit(solution)/shard_map/attend_back/pallas_call | solution.py:257
  381.1 116.1 %tail.1 = (bf16[4096,512]{1,0:T(8,128)(2,1)}, bf16[1024,1024]{1,0:T(8,128)(2,1)}, f32[16,1024]{1,0:T(8,128)}) custom-call(bf16[2048,512]{1,0:T(8,128)(2,1)} %get-tuple-element.109.gq_ref, bf16[2048,512]{1,0:T(8,128)(2,1)} %get-tuple-element.110.gk_ref, bf16[2048,512]{1,0:T(8,128)(2,1)} %get-tuple-element.111.gv_ref, ...), custom_call_target="tpu_custom_call" | custom-call | flops 524288 | bytes 524288 | tf_op jit(solution)/shard_map/tail/pallas_call | solution.py:939
  497.2 5.4 %convert_bitcast_fusion = (f32[512,1024]{0,1:T(8,128)S(1)}, f32[1024,512]{1,0:T(8,128)}, f32[1024,512]{1,0:T(8,128)}, f32[1024,512]{1,0:T(8,128)}) fusion(bf16[4096,512]{1,0:T(8,128)(2,1)} %get-tuple-element.117), kind=kLoop, calls=%fused_computation | loop fusion | flops 2097152 | bytes 12582912 | tf_op jit(solution)/shard_map/convert_element_type | solution.py:1140
  506.9 10.6 %widen.1 = (f32[1024,2048]{1,0:T(8,128)}, f32[2048,1024]{1,0:T(8,128)}) custom-call(bf16[4096,1024]{1,0:T(8,128)(2,1)} %all-reduce.3.cloned.1.call-done.up_ref.down_ref, bf16[4096,1024]{1,0:T(8,128)(2,1)} %all-reduce.3.cloned.1.call-done.up_ref.down_ref), custom_call_target="tpu_custom_call" | custom-call | tf_op jit(solution)/shard_map/widen/pallas_call | solution.py:657
  (85 shorter events, 43.3 us)
Async XLA Ops:
  7.2 172.9 %all-gather.3.cloned.1.call-start = ((), (), s32[]{:S(2)}) async-start(), calls=%async_computation | async-start | bytes 4456448 | tf_op jit(solution)/shard_map/all_gather | solution.py:1046
  8.9 31.9 %collective-permute-start = (bf16[512,1024]{1,0:T(8,128)(2,1)S(1)}, bf16[512,1024]{1,0:T(8,128)(2,1)S(1)}, u32[]{:S(2)}, u32[]{:S(2)}) collective-permute-start(bf16[512,1024]{1,0:T(8,128)(2,1)S(1)} %get-tuple-element.163), channel_id=1, source_target_pairs={{1,0},{0,1},{3,2},{2,3},{5,4},{4,5},{7,6},{6,7},{9,8},{8,9},{11,10... | collective-permute-start | bytes 3145736 | tf_op jit(solution)/shard_map/ppermute | solution.py:1008
  12.9 27.9 %collective-permute-start.1 = (bf16[64,2048]{1,0:T(8,128)(2,1)S(1)}, bf16[64,2048]{1,0:T(8,128)(2,1)}, u32[]{:S(2)}, u32[]{:S(2)}) collective-permute-start(bf16[64,2048]{1,0:T(8,128)(2,1)S(1)} %constant_dynamic-slice_fusion.1), channel_id=1, source_target_pairs={{1,0},{0,1},{3,2},{2,3},{5,4},{4,5},{7,6},{6,7},{9,8},{8,9},{11,10... | collective-permute-start | bytes 786440 | tf_op jit(solution)/shard_map/ppermute | solution.py:1008
  40.8 2.9 copy-start.4
  40.9 139.2 %all-gather.5.cloned.1.call-start = ((), (), s32[]{:S(2)}) async-start(), calls=%async_computation.1 | async-start | bytes 4456448 | tf_op jit(solution)/shard_map/all_gather | solution.py:1046
  40.9 24.4 %collective-permute-start.2 = (bf16[512,1024]{1,0:T(8,128)(2,1)S(1)}, bf16[512,1024]{1,0:T(8,128)(2,1)S(1)}, u32[]{:S(2)}, u32[]{:S(2)}) collective-permute-start(bf16[512,1024]{1,0:T(8,128)(2,1)S(1)} %get-tuple-element.162), channel_id=1, source_target_pairs={{1,0},{0,1},{3,2},{2,3},{5,4},{4,5},{7,6},{6,7},{9,8},{8,9},{11,10... | collective-permute-start | bytes 3145736 | tf_op jit(solution)/shard_map/ppermute | solution.py:1008
  46.7 20.1 %copy-start.11 = (bf16[2048]{0:T(1024)(128)(2,1)S(1)}, bf16[2048]{0:T(1024)(128)(2,1)}, u32[]{:S(2)}) copy-start(bf16[2048]{0:T(1024)(128)(2,1)} %param.21) | copy-start | bytes 12292
  65.3 2.0 copy-start.5
  65.3 10.1 %collective-permute-start.3 = (bf16[128,1024]{1,0:T(8,128)(2,1)S(1)}, bf16[128,1024]{1,0:T(8,128)(2,1)S(1)}, u32[]{:S(2)}, u32[]{:S(2)}) collective-permute-start(bf16[128,1024]{1,0:T(8,128)(2,1)S(1)} %constant_dynamic-slice_fusion), channel_id=1, source_target_pairs={{1,0},{0,1},{3,2},{2,3},{5,4},{4,5},{7,6},{6,7},{9,8},{8,9},{11,10... | collective-permute-start | bytes 786440 | tf_op jit(solution)/shard_map/ppermute | solution.py:1008
  66.7 8.7 %collective-permute-start.4 = (bf16[2048]{0:T(1024)(128)(2,1)S(1)}, bf16[2048]{0:T(1024)(128)(2,1)S(1)}, u32[]{:S(2)}, u32[]{:S(2)}) collective-permute-start(bf16[2048]{0:T(1024)(128)(2,1)S(1)} %copy-done.11), channel_id=1, source_target_pairs={{1,0},{0,1},{3,2},{2,3},{5,4},{4,5},{7,6},{6,7},{9,8},{8,9},{11,10... | collective-permute-start | bytes 12296 | tf_op jit(solution)/shard_map/ppermute | solution.py:1008
  76.2 430.7 %all-reduce.3.cloned.1.call-start = ((), (), s32[]{:S(2)}) async-start(), calls=%async_computation.2 | async-start | bytes 16777216 | tf_op jit(solution)/shard_map/psum | solution.py:1121
  93.6 33.5 %collective-permute-start.5 = (bf16[512,1024]{1,0:T(8,128)(2,1)}, bf16[512,1024]{1,0:T(8,128)(2,1)S(1)}, u32[]{:S(2)}, u32[]{:S(2)}) collective-permute-start(bf16[512,1024]{1,0:T(8,128)(2,1)} %get-tuple-element.77), channel_id=1, source_target_pairs={{1,0},{0,1},{3,2},{2,3},{5,4},{4,5},{7,6},{6,7},{9,8},{8,9},{11,10... | collective-permute-start | bytes 3145736 | tf_op jit(solution)/shard_map/ppermute | solution.py:1008
  102.2 22.4 %copy-start.12 = (bf16[1024]{0:T(1024)(128)(2,1)S(1)}, bf16[1024]{0:T(1024)(128)(2,1)}, u32[]{:S(2)}) copy-start(bf16[1024]{0:T(1024)(128)(2,1)} %param.23) | copy-start | bytes 6148
  122.5 23.9 %collective-permute-start.6 = (bf16[512,1024]{1,0:T(8,128)(2,1)}, bf16[512,1024]{1,0:T(8,128)(2,1)S(1)}, u32[]{:S(2)}, u32[]{:S(2)}) collective-permute-start(bf16[512,1024]{1,0:T(8,128)(2,1)} %get-tuple-element.85), channel_id=1, source_target_pairs={{1,0},{0,1},{3,2},{2,3},{5,4},{4,5},{7,6},{6,7},{9,8},{8,9},{11,10... | collective-permute-start | bytes 3145736 | tf_op jit(solution)/shard_map/ppermute | solution.py:1008
  127.1 12.9 %copy-start.2 = (bf16[512,1024]{1,0:T(8,128)(2,1)}, bf16[512,1024]{1,0:T(8,128)(2,1)S(1)}, u32[]{:S(2)}) copy-start(bf16[512,1024]{1,0:T(8,128)(2,1)S(1)} %collective-permute-done.5.refs_2_) | copy-start | bytes 3145732
  157.9 80.8 %collective-permute-start.7 = (bf16[1024,1024]{1,0:T(8,128)(2,1)}, bf16[1024,1024]{1,0:T(8,128)(2,1)S(1)}, u32[]{:S(2)}, u32[]{:S(2)}) collective-permute-start(bf16[1024,1024]{1,0:T(8,128)(2,1)} %get-tuple-element.86.refs_0_.refs_5_), channel_id=1, source_target_pairs={{1,0},{0,1},{3,2},{2,3},{5,4},{4,5},{7,6},{6,7},{9,8},{8,9},{11,10... | collective-permute-start | bytes 6291464 | tf_op jit(solution)/shard_map/ppermute | solution.py:1008
  204.3 48.9 %collective-permute-start.9 = (bf16[1024,1024]{1,0:T(8,128)(2,1)}, bf16[1024,1024]{1,0:T(8,128)(2,1)}, u32[]{:S(2)}, u32[]{:S(2)}) collective-permute-start(bf16[1024,1024]{1,0:T(8,128)(2,1)} %get-tuple-element.94.refs_0_.refs_7_), channel_id=1, source_target_pairs={{1,0},{0,1},{3,2},{2,3},{5,4},{4,5},{7,6},{6,7},{9,8},{8,9},{11,10... | collective-permute-start | bytes 6291464 | tf_op jit(solution)/shard_map/ppermute | solution.py:1008
  238.8 1.4 copy-start.13
  240.1 53.8 %collective-permute-start.8 = (bf16[1024,1024]{1,0:T(8,128)(2,1)}, bf16[1024,1024]{1,0:T(8,128)(2,1)S(1)}, u32[]{:S(2)}, u32[]{:S(2)}) collective-permute-start(bf16[1024,1024]{1,0:T(8,128)(2,1)} %get-tuple-element.100.x_ref.refs_2_), channel_id=1, source_target_pairs={{1,0},{0,1},{3,2},{2,3},{5,4},{4,5},{7,6},{6,7},{9,8},{8,9},{11,10... | collective-permute-start | bytes 6291464 | tf_op jit(solution)/shard_map/ppermute | solution.py:1008
  293.9 1.3 copy-start.9
  293.9 1.3 copy-start.8
  293.9 1.4 copy-start.10
  502.6 1.8 copy-start.7
  506.9 10.6 %copy-start.1 = (bf16[1024,1024]{1,0:T(8,128)(2,1)S(1)}, bf16[1024,1024]{1,0:T(8,128)(2,1)}, u32[]{:S(2)}) copy-start(bf16[1024,1024]{1,0:T(8,128)(2,1)} %get-tuple-element.116) | copy-start | bytes 6291460
  (3 other events, 3.0 us)
Sparse Core Ops, SparseCore 0:
  41.0 52.0 all-gather.2
  95.2 49.2 all-gather.4
  294.1 202.5 all-reduce.2

commit v4 on v3

--- a/solution.py
+++ b/solution.py
@@ -38,14 +38,13 @@
     o_ref[:, 2 * width :] = dotg(x, wv_ref[...]).astype(BF)
 
 
-def project(where, x, w_query, w_key, w_value, cos, sin, joint=None, part=0, parts=1, blk=256):
+def project(where, x, w_query, w_key, w_value, cos, sin, joint=None, blk=256):
     rows, depth = x.shape
     width, slots = w_query.shape[1], cos.shape[0]
-    blk = min(blk, rows // parts)
-    whole = rows // blk
-    count = whole // parts
+    blk = min(blk, rows)
+    count = rows // blk
     weight = pl.BlockSpec((depth, width), lambda i, at: (0, 0))
-    angle = pl.BlockSpec((blk, 128), lambda i, at: (at[0] * whole + part * count + i, 0))
+    angle = pl.BlockSpec((blk, 128), lambda i, at: (at[0] * count + i, 0))
     kernel = lambda at, *refs: qkv_kernel(*refs[:6], refs[-1])
     held = [] if joint is None else [joint]
     return pl.pallas_call(
@@ -53,9 +52,9 @@
         grid_spec=pltpu.PrefetchScalarGridSpec(
             num_scalar_prefetch=1,
             grid=(count,),
-            in_specs=[pl.BlockSpec((blk, depth), lambda i, at: (part * count + i, 0)), weight, weight, weight, angle, angle]
+            in_specs=[pl.BlockSpec((blk, depth), lambda i, at: (i, 0)), weight, weight, weight, angle, angle]
             + [pl.BlockSpec(memory_space=pl.ANY)] * len(held),
-            out_specs=pl.BlockSpec((blk, 3 * width), lambda i, at: (at[0] * whole + part * count + i, 0)),
+            out_specs=pl.BlockSpec((blk, 3 * width), lambda i, at: (at[0] * count + i, 0)),
         ),
         out_shape=jax.ShapeDtypeStruct((slots, 3 * width), BF),
         input_output_aliases={7: 0} if held else {},
@@ -575,30 +574,25 @@
     )(up, down, bias.reshape(-1, 1, cols), act, gp, *n2s, *gbs)
 
 
-def norm_kernel(at_ref, x_ref, gain_ref, shift_ref, *refs):
+def norm_kernel(x_ref, gain_ref, shift_ref, o_ref):
     hat, _ = norm_parts(x_ref[...].astype(F32))
-    refs[-1][...] = (hat * gain_ref[0:1] + shift_ref[0:1]).astype(BF)
-
-
-def first_norm(where, x, gains, shifts, rows, held, blk=512):
-    part, depth = x.shape
-    blk = min(blk, part)
-    count = part // blk
-    whole = pl.BlockSpec(gains.shape, lambda i, at: (0, 0))
+    o_ref[...] = (hat * gain_ref[0:1] + shift_ref[0:1]).astype(BF)
+
+
+def first_norm(x, gains, shifts, blk=512):
+    rows, depth = x.shape
+    blk = min(blk, rows)
+    whole = pl.BlockSpec(gains.shape, lambda i: (0, 0))
+    block = pl.BlockSpec((blk, depth), lambda i: (i, 0))
     return pl.pallas_call(
         norm_kernel,
-        grid_spec=pltpu.PrefetchScalarGridSpec(
-            num_scalar_prefetch=1,
-            grid=(count,),
-            in_specs=[pl.BlockSpec((blk, depth), lambda i, at: (i, 0)), whole, whole]
-            + [pl.BlockSpec(memory_space=pl.ANY)] * len(held),
-            out_specs=pl.BlockSpec((blk, depth), lambda i, at: (at[0] * count + i, 0)),
-        ),
+        grid=(rows // blk,),
+        in_specs=[block, whole, whole],
+        out_specs=block,
         out_shape=jax.ShapeDtypeStruct((rows, depth), BF),
-        input_output_aliases={4: 0} if held else {},
         compiler_params=pltpu.CompilerParams(vmem_limit_bytes=60 * MIB),
         name="first_norm",
-    )(where, x, gains, shifts, *held)
+    )(x, gains, shifts)
 
 
 def join_kernel(pick_ref, x_ref, gain_ref, shift_ref, *refs, blocks, each):
@@ -676,14 +670,13 @@
 MESH = pl.DeviceIdType.MESH
 
 
-def exchange(src, dst, sems, slot, bit):
-    peer = lax.axis_index("dp") ^ (1 << bit)
+def exchange(src, dst, sems, slot, flipped):
     return pltpu.make_async_remote_copy(
         src_ref=src,
         dst_ref=dst,
         send_sem=sems[0].at[slot],
         recv_sem=sems[1].at[slot],
-        device_id={"dp": peer},
+        device_id={"dp": lax.axis_index("dp") ^ flipped},
         device_id_type=MESH,
     )
 
@@ -700,7 +693,8 @@
     place, me = lax.axis_index("tensor"), lax.axis_index("dp")
     bit = lambda b: lax.rem(lax.div(me, 1 << b), 2)
     core = bit(0)
-    order = list(range(1, bits))
+    outer = list(range(1, bits))
+    order = [[b] for b in outer]
     rows, depth = x.shape
     width = weight.shape[2]
     half = 2 * depth
@@ -723,29 +717,41 @@
     third = [fetch(r, left.at[i]) for i, r in enumerate(lefts)] + [fetch(mixed_ref, right.at[3])]
     fourth = [fetch(x_ref, x), fetch(gr_ref, g_resid)]
 
-    greeted = [{"dp": me ^ (1 << b)} for b in range(bits)]
+    flips = {1 << b for b in range(bits)}
+    flips |= {sum(1 << b for b in some) for some in order}
+    greeted = [{"dp": me ^ f} for f in sorted(flips)]
     greeted += [{"tensor": lax.rem(place + r, groups)} for r in range(1, groups)]
-    known = {frozenset([("dp", b)]) for b in range(bits)} | {
-        frozenset([("tensor", b)]) for b in range((groups - 1).bit_length())
-    }
     for bits_of in steps:
         for mask in range(1, 1 << len(bits_of)):
             chosen = [bits_of[i] for i in range(len(bits_of)) if mask >> i & 1]
-            if frozenset(chosen) not in known and any(axis == "dp" for axis, _ in chosen):
-                known.add(frozenset(chosen))
-                peer = {}
-                for axis, b in chosen:
-                    peer[axis] = peer.get(axis, lax.axis_index(axis)) ^ (1 << b)
-                greeted.append(peer)
+            flip = sum(1 << b for axis, b in chosen if axis == "dp")
+            turn_by = sum(1 << b for axis, b in chosen if axis == "tensor")
+            if flip and turn_by:
+                greeted.append({"dp": me ^ flip, "tensor": place ^ turn_by})
+            elif flip and flip not in flips:
+                flips.add(flip)
+                greeted.append({"dp": me ^ flip})
     barrier = pltpu.get_barrier_semaphore()
     for peer in greeted:
         pl.semaphore_signal(barrier, inc=1, device_id=peer, device_id_type=MESH)
     pl.semaphore_wait(barrier, len(greeted))
 
-    def copy(src, dst, b):
-        c = exchange(src, dst, sems, next(slots), b)
+    def copy(src, dst, flipped):
+        c = exchange(src, dst, sems, next(slots), flipped)
         c.start()
         return c
+
+    def rank(some):
+        return sum(bit(b) << i for i, b in enumerate(some))
+
+    def other(mine, mask):
+        for i in range(mask.bit_length()):
+            if mask >> i & 1:
+                mine = mine + (1 << i) * (1 - 2 * lax.rem(lax.div(mine, 1 << i), 2))
+        return mine
+
+    def peer(some, mask):
+        return sum(1 << b for i, b in enumerate(some) if mask >> i & 1)
 
     forwards = []
     cores = {}
@@ -762,69 +768,77 @@
         lax.fori_loop(0, part // 64, join, 0)
         start, size = chunk * part, part
         landing = chunk * (part - part // (1 << (bits - 1)))
-        for b in order:
-            size //= 2
-            away = pl.multiple_of(start + (1 - bit(b)) * size, size)
-            c = copy(acc.at[pl.ds(away, size)], buf.at[pl.ds(landing, size)], b)
-            start = start + bit(b) * size
+        for some in order:
+            size //= 1 << len(some)
+            mine = rank(some)
+            copies = []
+            for mask in range(1, 1 << len(some)):
+                away = pl.multiple_of(start + other(mine, mask) * size, size)
+                at = pl.ds(landing + (mask - 1) * size, size)
+                copies.append(copy(acc.at[pl.ds(away, size)], buf.at[at], peer(some, mask)))
+            start = start + mine * size
             yield
-            c.wait()
+            wait_all(copies)
             step = min(size, 64)
 
-            def body(i, _, start=start, landing=landing, step=step):
+            def body(i, _, start=start, landing=landing, step=step, size=size, count=len(copies)):
                 at = pl.ds(pl.multiple_of(start + i * step, step), step)
-                got = buf[pl.ds(pl.multiple_of(landing + i * step, step), step)].astype(F32)
-                acc[at] = (acc[at].astype(F32) + got).astype(BF)
+                value = acc[at].astype(F32)
+                for n in range(count):
+                    value += buf[pl.ds(pl.multiple_of(landing + n * size + i * step, step), step)].astype(F32)
+                acc[at] = value.astype(BF)
                 return 0
 
             lax.fori_loop(0, size // step, body, 0)
-            landing += size
+            landing += len(copies) * size
         start = base + start
         sum_ref[pl.ds(pl.multiple_of(start, size), size)] = acc[pl.ds(pl.multiple_of(start - base, size), size)]
-        for b in reversed(order):
+        for some in reversed(order):
             have = sum_ref.at[pl.ds(pl.multiple_of(start, size), size)]
-            c = copy(have, have, b)
+            copies = [copy(have, have, peer(some, mask)) for mask in range(1, 1 << len(some))]
             yield
-            c.wait()
-            start = start - bit(b) * size
-            size *= 2
+            wait_all(copies)
+            start = start - rank(some) * size
+            size *= 1 << len(some)
         have = sum_ref.at[pl.ds(pl.multiple_of(start, size), size)]
-        forwards.append(copy(have, have, 0))
-
-    def share(r, store):
-        at = lax.rem(place + r, groups) * rows
-        blk = min(256, rows)
-
+        forwards.append(copy(have, have, 1))
+
+    quarter = rows // 4
+
+    def share(r, piece):
+        g = pl.ds(pl.multiple_of(lax.rem(place + r, groups) * rows + piece * quarter, quarter), quarter)
+        value = dotg(right[0, g, :], weight[0], NT)
+        value += dotg(right[1, g, :], weight[1], NT)
+        value += dotg(right[2, g, :], weight[2], NT)
+        return value
+
+    shares = {}
+
+    def share_away(r):
         def body(i, _):
-            g = pl.ds(pl.multiple_of(at + i * blk, blk), blk)
-            value = dotg(right[0, g, :], weight[0], NT)
-            value += dotg(right[1, g, :], weight[1], NT)
-            value += dotg(right[2, g, :], weight[2], NT)
-            store(pl.ds(pl.multiple_of(i * blk, blk), blk), value)
+            sent[r - 1, pl.ds(pl.multiple_of(i * quarter, quarter), quarter), :] = share(r, i).astype(BF)
             return 0
 
-        lax.fori_loop(0, rows // blk, body, 0)
-
-    shares = []
-
-    def share_away(r):
-        def store(at, value):
-            sent[r - 1, at, :] = value.astype(BF)
-
-        share(r, store)
-        c = pltpu.make_async_remote_copy(
-            src_ref=sent.at[r - 1],
-            dst_ref=came.at[r - 1],
-            send_sem=x_send.at[r - 1],
-            recv_sem=x_recv.at[r - 1],
-            device_id={"tensor": lax.rem(place + r, groups)},
-            device_id_type=MESH,
-        )
-        c.start()
-        shares.append(c)
-
-    def store_own(at, value):
-        own_share[at, :] = value
+        for piece in range(4):
+            lax.fori_loop(piece, piece + 1, body, 0)
+            at, slot = pl.ds(piece * quarter, quarter), (r - 1) * 4 + piece
+            c = pltpu.make_async_remote_copy(
+                src_ref=sent.at[r - 1, at],
+                dst_ref=came.at[r - 1, at],
+                send_sem=x_send.at[slot],
+                recv_sem=x_recv.at[slot],
+                device_id={"tensor": lax.rem(place + r, groups)},
+                device_id_type=MESH,
+            )
+            c.start()
+            shares[r, piece] = c
+
+    def share_own():
+        def body(i, _):
+            own_share[pl.ds(pl.multiple_of(i * quarter, quarter), quarter), :] = share(0, i)
+            return 0
+
+        lax.fori_loop(0, 4, body, 0)
 
     def weight_grad(side, some):
         cols = min(256, part)
@@ -847,13 +861,14 @@
         if side:
             for c in some:
                 at = pl.ds(pl.multiple_of((1 - core) * half + c * part, part), part)
-                cores[c] = copy(packed.at[at], core_buf.at[pl.ds(c * part, part)], 0)
-
-    def last_norm():
-        blk = min(64, rows)
+                cores[c] = copy(packed.at[at], core_buf.at[pl.ds(c * part, part)], 1)
+
+    def last_norm(piece):
+        wait_all([shares[r, piece] for r in range(1, groups)])
+        blk = min(64, quarter)
 
         def body(i, _):
-            at = pl.ds(pl.multiple_of(i * blk, blk), blk)
+            at = pl.ds(pl.multiple_of(piece * quarter + i * blk, blk), blk)
             value = own_share[at, :]
             for r in range(groups - 1):
                 value += came[r, at, :].astype(F32)
@@ -863,7 +878,7 @@
             total_ref[1:2] += column_sum(value)
             return 0
 
-        lax.fori_loop(0, rows // blk, body, 0)
+        lax.fori_loop(0, quarter // blk, body, 0)
 
     def vectors():
         slot = 0
@@ -910,16 +925,20 @@
     all_chunks = list(range(chunks))
     for some in (all_chunks[: chunks // 2], all_chunks[chunks // 2 :]):
         weight_grad(1, some)
+    wait_all(fourth)
+    total_ref[...] = vec_ref[...]
     reduces = []
-    for chunk in all_chunks:
+    for i, chunk in enumerate(all_chunks):
         weight_grad(0, [chunk])
         reduces = turn(reduces + [reduce(chunk)])
-    share(0, store_own)
+    share_own()
     reduces = turn(reduces)
-    wait_all(fourth)
-    wait_all(shares)
-    total_ref[...] = vec_ref[...]
-    last_norm()
+    last_norm(0)
+    last_norm(1)
+    reduces = turn(reduces)
+    last_norm(2)
+    reduces = turn(reduces)
+    last_norm(3)
     chain = turn([vectors()])
     while reduces or chain:
         reduces, chain = turn(reduces), turn(chain)
@@ -930,7 +949,7 @@
     (slots, width), (rows, depth), groups = mixed.shape, x.shape, len(n1s)
     half = 2 * depth
     landing = half - half // (1 << (bits - 1))
-    count = half // min(512, depth) * (2 * bits + 1)
+    count = half // min(512, depth) * (3 * bits + 2)
     vecs = sum((1 << len(b)) - 1 for b in steps)
     vmem = pl.BlockSpec(memory_space=pltpu.VMEM)
     anyspace = pl.BlockSpec(memory_space=pl.ANY)
@@ -963,8 +982,8 @@
             dma((count,)),
             dma((vecs,)),
             dma((vecs,)),
-            dma((peers,)),
-            dma((peers,)),
+            dma((4 * peers,)),
+            dma((4 * peers,)),
             dma((9 + 2 * groups,)),
         ],
         compiler_params=pltpu.CompilerParams(
@@ -1050,26 +1069,16 @@
     cosine, sine = jnp.cos(angles), jnp.sin(angles)
     cosine = jnp.concatenate([cosine] * 4, axis=1)
     sine = jnp.concatenate([-sine, sine] * 2, axis=1)
-    halves = 2
-    index = lambda k: jnp.full((1,), k, jnp.int32)
-    x_rest = [others(v) for v in jnp.split(x, halves)]
-    normed_one = first_norm(index(0), x, norm_gains, norm_shifts, rows, [])
-    up_pieces = others(up_piece)
+    x_rest = others(x)
+    normed_one = first_norm(x, norm_gains, norm_shifts)
     weights = (w_query, w_key, w_value)
     joint = project(here, normed_one, *weights, cosine, sine)
-    normed_one_rest = [[] for _ in range(1, groups)]
-    for k in range(halves):
-        pieces = (down_piece, bias_up) if k == halves - 1 else up_pieces
-        joint, x_rest[k], pieces = lax.optimization_barrier((joint, x_rest[k], pieces))
-        if k < halves - 1:
-            up_pieces = pieces
-        else:
-            down_pieces, bias_rest = (others(v) for v in pieces)
-        for r in range(1, groups):
-            n = first_norm(index(k), x_rest[k][r - 1], norm_gains, norm_shifts, rows, normed_one_rest[r - 1])
-            normed_one_rest[r - 1] = [n]
-            joint = project(place(r), n, *weights, cosine, sine, joint, k, halves)
-    normed_one_rest = [v[0] for v in normed_one_rest]
+    joint, x_rest, up_piece, down_piece, bias = lax.optimization_barrier((joint, x_rest, up_piece, down_piece, bias_up))
+    up_pieces, down_pieces, bias_rest = others(up_piece), others(down_piece), others(bias)
+    normed_one_rest = [first_norm(v, norm_gains, norm_shifts) for v in x_rest]
+    for r, n in enumerate(normed_one_rest):
+        joint = project(place(r + 1), n, *weights, cosine, sine, joint)
+    joint, up_pieces, down_pieces, bias_rest = lax.optimization_barrier((joint, up_pieces, down_pieces, bias_rest))
     blk = min(512, rows)
     each = rows // blk
     odd = lambda r: lax.rem(place(r), 2)
@@ -1079,8 +1088,6 @@
         for r in range(1, groups):
             *held, share = attend(place(r) * each + ranks(0, k), lengths, joint, w_out, held, BF, blk)
             arrived[r - 1].append(to_owner(share, r))
-        if k == 0:
-            joint, down_pieces, bias_rest = lax.optimization_barrier((joint, down_pieces, bias_rest))
         if k == each - 1 and k > 0:
             joint, arrived = lax.optimization_barrier((joint, [v[:k] for v in arrived])), arrived
             joint, early = joint

time: 535 us -> 525 us (0.981)
  Pallas kernels: 424 us -> 414 us
    pallas_call x1, Pallas kernels: 116 us -> 110 us  [tail(): pl.pallas_call(functools.partial(tail_kernel, bits=bits, groups=groups, s...]
    ppermute x10 -> x9, waiting for transfers between devices: 43.6 us -> 46.3 us  [shift(): lax.ppermute(x, axis, [((i + step) % count, i) for i in range(count)])]
    pallas_call x3 -> x2, Pallas kernels: 17.7 us -> 15 us  [project(): pl.pallas_call(kernel, grid_spec=pltpu.PrefetchScalarGridSpec(num_scalar_...]
    ppermute x10 -> x9, starting transfers between devices: 12.7 us -> 12.8 us  [shift(): lax.ppermute(x, axis, [((i + step) % count, i) for i in range(count)])]
  transfers between devices with their start and end apart: 13 -> 12, of which waited for: 5 -> 4; matrix products, arithmetic and copies ran while one was open for 4% -> 4% of each run, Pallas kernels for 79% -> 78%
where the time goes in v4:
time: 525 us; the launch traced here: 517 us
  Pallas kernels  414 us (79%)
  waiting for transfers between devices  47.1 us (9%)
  between operations  15.1 us (3%)
  other arithmetic  14.7 us (3%)
  starting transfers between devices  13.4 us (3%)
  local copies, waits for them, and re-layouts  12.9 us (2%)
    pallas_call x1, Pallas kernels, tail(): pl.pallas_call(functools.partial(tail_kernel, bits=bits, groups=groups, s...  110 us
    pallas_call x1, Pallas kernels, attend_back(): pl.pallas_call(functools.partial(attend_back_kernel, blk=blk, blocks=bloc...  79.6 us
    pallas_call x4, Pallas kernels, attend(): pl.pallas_call(functools.partial(attend_kernel, blk=blk), grid_spec=pltpu...  58.1 us
    ppermute x9, waiting for transfers between devices, shift(): lax.ppermute(x, axis, [((i + step) % count, i) for i in range(count)])  46.3 us
    pallas_call x2, Pallas kernels, feed(): pl.pallas_call(functools.partial(feed_kernel, groups=groups, chunks=chunk...  44.7 us
    pallas_call x1, Pallas kernels, feed_back(): pl.pallas_call(functools.partial(feed_back_kernel, groups=groups, chunks=...  33.9 us
    pallas_call x1, Pallas kernels, feed_grad(): pl.pallas_call(functools.partial(feed_grad_kernel, groups=groups), grid=(...  33.6 us
    pallas_call x2, Pallas kernels, project(): pl.pallas_call(kernel, grid_spec=pltpu.PrefetchScalarGridSpec(num_scalar_...  15 us
  transfers between devices with their start and end apart: 12, of which 4 were waited for; matrix products, arithmetic and copies ran while one was open for 4% of the time, Pallas kernels for 78%

profile of v4, /device:TPU:0, one launch (start us, length us, event | category | flops | bytes accessed | tf_op | source)
XLA Modules:
  0.0 517.1 jit_solution(14663492892201991003)
XLA Ops:
  10.2 3.7 first_norm.2.refs_0_
  14.0 3.7 fusion
  20.7 7.5 %project.2.refs_6_ = bf16[2048,1536]{1,0:T(8,128)(2,1)} custom-call(s32[1]{0:T(128)} %bitcast.1.at.at_ref, bf16[1024,1024]{1,0:T(8,128)(2,1)} %first_norm.2.refs_0_, bf16[1024,512]{1,0:T(8,128)(2,1)} %wq_ref.1, bf16[1024,512]{1,0:T(8,128)(2,1)} %wk_ref.1, bf16[1024,512]{1,0:T(8,128)(2,1)} %wv_ref.1, f32[2048,128]{1,0:T(8,128)} %get-tuple-element.174.refs_4_.cos_ref, ...), custom_call_target="tpu_custom_call" | custom-call | flops 1048576 | bytes 1048576 | tf_op jit(solution)/shard_map/project/pallas_call | solution.py:50
  30.2 25.9 %collective-permute-done.x_ref = bf16[1024,1024]{1,0:T(8,128)(2,1)S(1)} collective-permute-done((bf16[1024,1024]{1,0:T(8,128)(2,1)}, bf16[1024,1024]{1,0:T(8,128)(2,1)S(1)}, u32[]{:S(2)}, u32[]{:S(2)}) %collective-permute-start) | collective-permute-done | bytes 2097184 | tf_op jit(solution)/shard_map/ppermute | solution.py:1027
  59.8 3.7 first_norm.3.refs_0_.refs_1_
  63.6 7.5 %project.3.q_ref.k_ref.v_ref = bf16[2048,1536]{1,0:T(8,128)(2,1)} custom-call(s32[1]{0:T(128)S(6)} %select_n.67.at.at_ref, bf16[1024,1024]{1,0:T(8,128)(2,1)} %first_norm.3.refs_0_.refs_1_, bf16[1024,512]{1,0:T(8,128)(2,1)} %wq_ref.1, bf16[1024,512]{1,0:T(8,128)(2,1)} %wk_ref.1, bf16[1024,512]{1,0:T(8,128)(2,1)} %wv_ref.1, ...), custom_call_target="tpu_custom_call", output_to_operand_aliasing={{}: (7, {})} | custom-call | flops 1048576 | bytes 1048576 | tf_op jit(solution)/shard_map/project/pallas_call | solution.py:50
  73.8 16.2 %attend.4 = (bf16[2048,512]{1,0:T(8,128)(2,1)}, f32[4,2,2048]{2,1,0:T(2,128)}, bf16[512,1024]{1,0:T(8,128)(2,1)}) custom-call(s32[1]{0:T(128)S(6)} %add.78.at_ref, s32[1]{0:T(128)S(6)} %copy.55.len_ref, bf16[2048,1536]{1,0:T(8,128)(2,1)} %project.3.q_ref.k_ref.v_ref, bf16[2048,1536]{1,0:T(8,128)(2,1)} %project.3.q_ref.k_ref.v_ref, ...), custom_call_target="tpu_custom_call" | custom-call | flops 1048576 | bytes 1048576 | tf_op jit(solution)/shard_map/attend/pallas_call | solution.py:147
  90.1 8.5 %attend.5 = (bf16[2048,512]{1,0:T(8,128)(2,1)}, f32[4,2,2048]{2,1,0:T(2,128)}, f32[512,1024]{1,0:T(8,128)}) custom-call(s32[1]{0:T(128)S(6)} %add.75.at_ref, s32[1]{0:T(128)S(6)} %copy.55.len_ref, bf16[2048,1536]{1,0:T(8,128)(2,1)} %project.3.q_ref.k_ref.v_ref, ...), custom_call_target="tpu_custom_call", output_to_operand_aliasing={{0}: (6, {}), {1}: (7, {})} | custom-call | flops 1048576 | bytes 1048576 | tf_op jit(solution)/shard_map/attend/pallas_call | solution.py:147
  98.6 20.5 %attend.6 = (bf16[2048,512]{1,0:T(8,128)(2,1)}, f32[4,2,2048]{2,1,0:T(2,128)}, bf16[512,1024]{1,0:T(8,128)(2,1)}) custom-call(s32[1]{0:T(128)S(6)} %add.80.at_ref, s32[1]{0:T(128)S(6)} %copy.55.len_ref, bf16[2048,1536]{1,0:T(8,128)(2,1)} %project.3.q_ref.k_ref.v_ref, ...), custom_call_target="tpu_custom_call", output_to_operand_aliasing={{0}: (6, {}), {1}: (7, {})} | custom-call | flops 1048576 | bytes 1048576 | tf_op jit(solution)/shard_map/attend/pallas_call | solution.py:147
  123.5 12.9 %attend.7 = (bf16[2048,512]{1,0:T(8,128)(2,1)}, f32[4,2,2048]{2,1,0:T(2,128)}, f32[512,1024]{1,0:T(8,128)}) custom-call(s32[1]{0:T(128)S(6)} %add.79.at_ref, s32[1]{0:T(128)S(6)} %copy.55.len_ref, bf16[2048,1536]{1,0:T(8,128)(2,1)} %project.3.q_ref.k_ref.v_ref, ...), custom_call_target="tpu_custom_call", output_to_operand_aliasing={{0}: (6, {}), {1}: (7, {})} | custom-call | flops 1048576 | bytes 1048576 | tf_op jit(solution)/shard_map/attend/pallas_call | solution.py:147
  136.4 6.0 %collective-permute-done.5.refs_3_ = bf16[512,1024]{1,0:T(8,128)(2,1)S(1)} collective-permute-done((bf16[512,1024]{1,0:T(8,128)(2,1)}, bf16[512,1024]{1,0:T(8,128)(2,1)S(1)}, u32[]{:S(2)}, u32[]{:S(2)}) %collective-permute-start.5) | collective-permute-done | bytes 1048608 | tf_op jit(solution)/shard_map/ppermute | solution.py:1027
  143.4 11.2 %join.1 = (f32[1024,1024]{1,0:T(8,128)}, f32[1024,1024]{1,0:T(8,128)}, bf16[1024,1024]{1,0:T(8,128)(2,1)}) custom-call(s32[4]{0:T(128)} %pad_add_fusion.1.pick_ref, bf16[1024,1024]{1,0:T(8,128)(2,1)} %bitcast.18, f32[4,1024]{1,0:T(4,128)} %gain_ref.7, f32[4,1024]{1,0:T(4,128)} %refs_8_.1, f32[512,1024]{1,0:T(8,128)} %get-tuple-element.74.refs_0_, ...), custom_call_target="tpu_custom_call" | custom-call | tf_op jit(solution)/shard_map/join/pallas_call | solution.py:624
  156.6 20.5 %feed.2 = (bf16[1024,2048]{1,0:T(8,128)(2,1)}, bf16[1024,2048]{1,0:T(8,128)(2,1)}, f32[1024,1024]{1,0:T(8,128)}) custom-call(s32[2]{0:T(128)} %pad_add_fusion.info_ref, bf16[1024,1024]{1,0:T(8,128)(2,1)} %get-tuple-element.84.refs_0_.refs_5_, f32[4,1,512]{2,1,0:T(1,128)} %get-tuple-element.169.refs_1_.refs_2_, bf16[1024,2048]{1,0:T(8,128)(2,1)} %refs_0_.1, ...), custom_call_target="tpu_custom_call" | custom-call | flops 1048576 | bytes 1048576 | tf_op jit(solution)/shard_map/feed/pallas_call | solution.py:410
  177.2 24.2 %feed.3 = (bf16[1024,2048]{1,0:T(8,128)(2,1)}, bf16[1024,1024]{1,0:T(8,128)(2,1)}, bf16[1024,1024]{1,0:T(8,128)(2,1)}, f32[8,1024]{1,0:T(8,128)}) custom-call(s32[2]{0:T(128)} %pad_add_fusion.info_ref, bf16[1024,1024]{1,0:T(8,128)(2,1)} %get-tuple-element.84.refs_0_.refs_5_, f32[4,1,512]{2,1,0:T(1,128)} %get-tuple-element.170.refs_1_, ...), custom_call_target="tpu_custom_call" | custom-call | flops 1048576 | bytes 1048576 | tf_op jit(solution)/shard_map/feed/pallas_call | solution.py:410
  201.5 33.9 %feed_back.1 = (bf16[1024,2048]{1,0:T(8,128)(2,1)}, f32[1024,1024]{1,0:T(8,128)}, bf16[1024,1024]{1,0:T(8,128)(2,1)}, f32[8,1024]{1,0:T(8,128)}) custom-call(s32[2]{0:T(128)} %pad_add_fusion.info_ref, bf16[1024,1024]{1,0:T(8,128)(2,1)} %get-tuple-element.92.refs_0_.refs_7_, bf16[1024,2048]{1,0:T(8,128)(2,1)} %get-tuple-element.93.refs_1_, ...), custom_call_target="tpu_custom_call" | custom-call | flops 1048576 | bytes 1048576 | tf_op jit(solution)/shard_map/feed_back/pallas_call | solution.py:490
  238.8 4.8 mixed_back.2.refs_0_
  243.6 6.7 %collective-permute-done.8.refs_8_ = bf16[1024,1024]{1,0:T(8,128)(2,1)} collective-permute-done((bf16[1024,1024]{1,0:T(8,128)(2,1)}, bf16[1024,1024]{1,0:T(8,128)(2,1)}, u32[]{:S(2)}, u32[]{:S(2)}) %collective-permute-start.8) | collective-permute-done | bytes 2097184 | tf_op jit(solution)/shard_map/ppermute | solution.py:1027
  250.3 33.6 %feed_grad.1 = (bf16[2,2048,1024]{2,1,0:T(8,128)(2,1)}, f32[4,1,512]{2,1,0:T(1,128)}) custom-call(bf16[1024,2048]{1,0:T(8,128)(2,1)} %refs_0_.1, bf16[2048,1024]{1,0:T(8,128)(2,1)} %refs_1_.5, f32[4,1,512]{2,1,0:T(1,128)} %get-tuple-element.169.refs_1_.refs_2_, bf16[1024,2048]{1,0:T(8,128)(2,1)} %get-tuple-element.100.refs_3_, ...), custom_call_target="tpu_custom_call" | custom-call | flops 25769803776 | bytes 20971520 | tf_op jit(solution)/shard_map/feed_grad/pallas_call | solution.py:560
  283.9 7.7 %collective-permute-done.7.x_ref.refs_3_ = bf16[1024,1024]{1,0:T(8,128)(2,1)S(1)} collective-permute-done((bf16[1024,1024]{1,0:T(8,128)(2,1)}, bf16[1024,1024]{1,0:T(8,128)(2,1)S(1)}, u32[]{:S(2)}, u32[]{:S(2)}) %collective-permute-start.7) | collective-permute-done | bytes 2097184 | tf_op jit(solution)/shard_map/ppermute | solution.py:1027
  294.1 5.2 %mixed_back.3.do_ref = bf16[2048,512]{1,0:T(8,128)(2,1)} custom-call(s32[1]{0:T(128)S(6)} %select_n.67.at.at_ref, bf16[1024,1024]{1,0:T(8,128)(2,1)} %copy-done, bf16[512,1024]{1,0:T(8,128)(2,1)} %w_ref.11, bf16[2048,512]{1,0:T(8,128)(2,1)} %mixed_back.2.refs_0_), custom_call_target="tpu_custom_call", output_to_operand_aliasing={{}: (3, {})} | custom-call | flops 1048576 | bytes 1048576 | tf_op jit(solution)/shard_map/mixed_back/pallas_call | solution.py:1006
  299.2 79.6 %attend_back.1 = (bf16[2048,512]{1,0:T(8,128)(2,1)}, bf16[2048,512]{1,0:T(8,128)(2,1)}, bf16[2048,512]{1,0:T(8,128)(2,1)}) custom-call(s32[1]{0:T(128)S(6)} %copy.55.len_ref, bf16[2048,1536]{1,0:T(8,128)(2,1)} %project.3.q_ref.k_ref.v_ref, bf16[2048,1536]{1,0:T(8,128)(2,1)} %project.3.q_ref.k_ref.v_ref, bf16[2048,1536]{1,0:T(8,128)(2,1)} %project.3.q_ref.k_ref.v_ref, ...), custom_call_target="tpu_custom_call" | custom-call | flops 1048576 | bytes 1048576 | tf_op jit(solution)/shard_map/attend_back/pallas_call | solution.py:256
  378.9 109.6 %tail.1 = (bf16[4096,512]{1,0:T(8,128)(2,1)}, bf16[1024,1024]{1,0:T(8,128)(2,1)}, f32[16,1024]{1,0:T(8,128)}) custom-call(bf16[2048,512]{1,0:T(8,128)(2,1)} %get-tuple-element.107.gq_ref, bf16[2048,512]{1,0:T(8,128)(2,1)} %get-tuple-element.108.gk_ref, bf16[2048,512]{1,0:T(8,128)(2,1)} %get-tuple-element.109.gv_ref, ...), custom_call_target="tpu_custom_call" | custom-call | flops 524288 | bytes 524288 | tf_op jit(solution)/shard_map/tail/pallas_call | solution.py:958
  488.5 5.4 %convert_bitcast_fusion = (f32[512,1024]{0,1:T(8,128)S(1)}, f32[1024,512]{1,0:T(8,128)}, f32[1024,512]{1,0:T(8,128)}, f32[1024,512]{1,0:T(8,128)}) fusion(bf16[4096,512]{1,0:T(8,128)(2,1)} %get-tuple-element.115), kind=kLoop, calls=%fused_computation | loop fusion | flops 2097152 | bytes 12582912 | tf_op jit(solution)/shard_map/convert_element_type | solution.py:1147
  498.2 10.6 %widen.1 = (f32[1024,2048]{1,0:T(8,128)}, f32[2048,1024]{1,0:T(8,128)}) custom-call(bf16[4096,1024]{1,0:T(8,128)(2,1)} %all-reduce.3.cloned.1.call-done.up_ref.down_ref, bf16[4096,1024]{1,0:T(8,128)(2,1)} %all-reduce.3.cloned.1.call-done.up_ref.down_ref), custom_call_target="tpu_custom_call" | custom-call | tf_op jit(solution)/shard_map/widen/pallas_call | solution.py:651
  (80 shorter events, 32.6 us)
Async XLA Ops:
  7.2 169.9 %all-gather.3.cloned.1.call-start = ((), (), s32[]{:S(2)}) async-start(), calls=%async_computation | async-start | bytes 4456448 | tf_op jit(solution)/shard_map/all_gather | solution.py:1065
  7.2 48.8 %collective-permute-start = (bf16[1024,1024]{1,0:T(8,128)(2,1)}, bf16[1024,1024]{1,0:T(8,128)(2,1)S(1)}, u32[]{:S(2)}, u32[]{:S(2)}) collective-permute-start(bf16[1024,1024]{1,0:T(8,128)(2,1)} %bitcast.16), channel_id=1, source_target_pairs={{1,0},{0,1},{3,2},{2,3},{5,4},{4,5},{7,6},{6,7},{9,8},{8,9},{11,10... | collective-permute-start | bytes 6291464 | tf_op jit(solution)/shard_map/ppermute | solution.py:1027
  20.7 37.4 %copy-start.11 = (bf16[2048]{0:T(1024)(128)(2,1)S(1)}, bf16[2048]{0:T(1024)(128)(2,1)}, u32[]{:S(2)}) copy-start(bf16[2048]{0:T(1024)(128)(2,1)} %param.21) | copy-start | bytes 12292
  56.1 3.8 copy-start.1
  56.1 15.0 %collective-permute-start.1 = (bf16[64,2048]{1,0:T(8,128)(2,1)S(1)}, bf16[64,2048]{1,0:T(8,128)(2,1)S(1)}, u32[]{:S(2)}, u32[]{:S(2)}) collective-permute-start(bf16[64,2048]{1,0:T(8,128)(2,1)S(1)} %constant_dynamic-slice_fusion.1), channel_id=1, source_target_pairs={{1,0},{0,1},{3,2},{2,3},{5,4},{4,5},{7,6},{6,7},{9,8},{8,9},{11,10... | collective-permute-start | bytes 786440 | tf_op jit(solution)/shard_map/ppermute | solution.py:1027
  57.8 13.3 %collective-permute-start.2 = (bf16[128,1024]{1,0:T(8,128)(2,1)S(1)}, bf16[128,1024]{1,0:T(8,128)(2,1)S(1)}, u32[]{:S(2)}, u32[]{:S(2)}) collective-permute-start(bf16[128,1024]{1,0:T(8,128)(2,1)S(1)} %constant_dynamic-slice_fusion), channel_id=1, source_target_pairs={{1,0},{0,1},{3,2},{2,3},{5,4},{4,5},{7,6},{6,7},{9,8},{8,9},{11,10... | collective-permute-start | bytes 786440 | tf_op jit(solution)/shard_map/ppermute | solution.py:1027
  58.1 13.0 %collective-permute-start.3 = (bf16[2048]{0:T(1024)(128)(2,1)S(1)}, bf16[2048]{0:T(1024)(128)(2,1)S(1)}, u32[]{:S(2)}, u32[]{:S(2)}) collective-permute-start(bf16[2048]{0:T(1024)(128)(2,1)S(1)} %copy-done.11), channel_id=1, source_target_pairs={{1,0},{0,1},{3,2},{2,3},{5,4},{4,5},{7,6},{6,7},{9,8},{8,9},{11,10... | collective-permute-start | bytes 12296 | tf_op jit(solution)/shard_map/ppermute | solution.py:1027
  71.8 105.3 %all-gather.5.cloned.1.call-start = ((), (), s32[]{:S(2)}) async-start(), calls=%async_computation.1 | async-start | bytes 4456448 | tf_op jit(solution)/shard_map/all_gather | solution.py:1065
  72.6 425.6 %all-reduce.3.cloned.1.call-start = ((), (), s32[]{:S(2)}) async-start(), calls=%async_computation.2 | async-start | bytes 16777216 | tf_op jit(solution)/shard_map/psum | solution.py:1128
  90.0 33.5 %collective-permute-start.4 = (bf16[512,1024]{1,0:T(8,128)(2,1)}, bf16[512,1024]{1,0:T(8,128)(2,1)S(1)}, u32[]{:S(2)}, u32[]{:S(2)}) collective-permute-start(bf16[512,1024]{1,0:T(8,128)(2,1)} %get-tuple-element.75), channel_id=1, source_target_pairs={{1,0},{0,1},{3,2},{2,3},{5,4},{4,5},{7,6},{6,7},{9,8},{8,9},{11,10... | collective-permute-start | bytes 3145736 | tf_op jit(solution)/shard_map/ppermute | solution.py:1027
  98.6 22.4 %copy-start.12 = (bf16[1024]{0:T(1024)(128)(2,1)S(1)}, bf16[1024]{0:T(1024)(128)(2,1)}, u32[]{:S(2)}) copy-start(bf16[1024]{0:T(1024)(128)(2,1)} %param.23) | copy-start | bytes 6148
  119.1 23.3 %collective-permute-start.5 = (bf16[512,1024]{1,0:T(8,128)(2,1)}, bf16[512,1024]{1,0:T(8,128)(2,1)S(1)}, u32[]{:S(2)}, u32[]{:S(2)}) collective-permute-start(bf16[512,1024]{1,0:T(8,128)(2,1)} %get-tuple-element.83), channel_id=1, source_target_pairs={{1,0},{0,1},{3,2},{2,3},{5,4},{4,5},{7,6},{6,7},{9,8},{8,9},{11,10... | collective-permute-start | bytes 3145736 | tf_op jit(solution)/shard_map/ppermute | solution.py:1027
  123.5 12.9 %copy-start.3 = (bf16[512,1024]{1,0:T(8,128)(2,1)}, bf16[512,1024]{1,0:T(8,128)(2,1)S(1)}, u32[]{:S(2)}) copy-start(bf16[512,1024]{1,0:T(8,128)(2,1)S(1)} %collective-permute-done.4.refs_2_) | copy-start | bytes 3145732
  142.4 1.0 copy-start.4
  154.6 80.9 %collective-permute-start.6 = (bf16[1024,1024]{1,0:T(8,128)(2,1)}, bf16[1024,1024]{1,0:T(8,128)(2,1)S(1)}, u32[]{:S(2)}, u32[]{:S(2)}) collective-permute-start(bf16[1024,1024]{1,0:T(8,128)(2,1)} %get-tuple-element.84.refs_0_.refs_5_), channel_id=1, source_target_pairs={{1,0},{0,1},{3,2},{2,3},{5,4},{4,5},{7,6},{6,7},{9,8},{8,9},{11,10... | collective-permute-start | bytes 6291464 | tf_op jit(solution)/shard_map/ppermute | solution.py:1027
  201.3 48.9 %collective-permute-start.8 = (bf16[1024,1024]{1,0:T(8,128)(2,1)}, bf16[1024,1024]{1,0:T(8,128)(2,1)}, u32[]{:S(2)}, u32[]{:S(2)}) collective-permute-start(bf16[1024,1024]{1,0:T(8,128)(2,1)} %get-tuple-element.92.refs_0_.refs_7_), channel_id=1, source_target_pairs={{1,0},{0,1},{3,2},{2,3},{5,4},{4,5},{7,6},{6,7},{9,8},{8,9},{11,10... | collective-permute-start | bytes 6291464 | tf_op jit(solution)/shard_map/ppermute | solution.py:1027
  235.4 1.4 copy-start.13
  236.8 54.8 %collective-permute-start.7 = (bf16[1024,1024]{1,0:T(8,128)(2,1)}, bf16[1024,1024]{1,0:T(8,128)(2,1)S(1)}, u32[]{:S(2)}, u32[]{:S(2)}) collective-permute-start(bf16[1024,1024]{1,0:T(8,128)(2,1)} %get-tuple-element.98.x_ref.refs_2_), channel_id=1, source_target_pairs={{1,0},{0,1},{3,2},{2,3},{5,4},{4,5},{7,6},{6,7},{9,8},{8,9},{11,10... | collective-permute-start | bytes 6291464 | tf_op jit(solution)/shard_map/ppermute | solution.py:1027
  291.6 1.3 copy-start
  291.6 1.3 copy-start.9
  291.6 1.3 copy-start.8
  291.6 1.4 copy-start.10
  493.9 1.8 copy-start.7
  498.2 10.6 %copy-start.2 = (bf16[1024,1024]{1,0:T(8,128)(2,1)S(1)}, bf16[1024,1024]{1,0:T(8,128)(2,1)}, u32[]{:S(2)}) copy-start(bf16[1024,1024]{1,0:T(8,128)(2,1)} %get-tuple-element.114) | copy-start | bytes 6291460
  (2 other events, 1.5 us)
Sparse Core Ops, SparseCore 0:
  71.9 51.0 all-gather.2
  125.2 49.2 all-gather.4
  291.8 201.8 all-reduce.2

commit v5 on v4

--- a/solution.py
+++ b/solution.py
@@ -318,43 +318,34 @@
     lax.fori_loop(0, rows // blk, step, 0)
 
 
-def feed_kernel(info_ref, *refs, groups, chunks, sub, own):
-    x_ref, bias_ref = refs[:2]
-    ups, downs, refs = refs[2 : 2 + groups], refs[2 + groups : 2 + 2 * groups], refs[2 + 2 * groups :]
+def feed_kernel(info_ref, *refs, groups, chunks, sub):
+    x_ref, bias_ref, resid_hbm, cot_hbm, bd_ref, gain_ref, shift_ref = refs[:7]
+    ups, downs = refs[7 : 7 + groups], refs[7 + groups : 7 + 2 * groups]
+    slope_ref, act_ref, out_ref, gb_ref, sums_ref, acc, resid_ref, cot_ref, sems = refs[7 + 2 * groups :]
     step = pl.program_id(0)
     rows = x_ref.shape[0]
-    if own:
-        bd_ref, slope_ref, act_ref, acc = refs
-        late = []
-    else:
-        resid_hbm, cot_hbm, before_hbm, gain_ref, shift_ref = refs[:5]
-        slope_ref, out_ref, gb_ref, sums_ref, acc, resid_ref, before_ref, cot_ref, sems = refs[5:]
-        late = [
-            pltpu.make_async_copy(resid_hbm, resid_ref, sems.at[0]),
-            pltpu.make_async_copy(cot_hbm, cot_ref, sems.at[1]),
-            pltpu.make_async_copy(before_hbm, before_ref, sems.at[2]),
-        ]
+    late = [
+        pltpu.make_async_copy(resid_hbm, resid_ref, sems.at[0]),
+        pltpu.make_async_copy(cot_hbm, cot_ref, sems.at[1]),
+    ]
 
     @pl.when(step == 0)
     def _():
-        acc[...] = jnp.zeros_like(acc) + bd_ref[...].astype(F32) if own else jnp.zeros_like(acc)
         for c in late:
             c.start()
+        acc[...] = jnp.zeros_like(acc) + bd_ref[...].astype(F32)
 
     for g in range(groups):
 
         @pl.when(step // chunks == g)
         def _():
             for r in range(0, rows, sub):
-                act, slope = gelu_both(dotg(x_ref[r : r + sub], ups[g][...]) + bias_ref[0])
+                act, slope = gelu_both(dotg(x_ref[r : r + sub], ups[g][...], NT if g else NN) + bias_ref[0])
                 slope_ref[r : r + sub] = slope.astype(BF)
                 act = act.astype(BF)
-                if own:
+                if g == 0:
                     act_ref[r : r + sub] = act
                 acc[r : r + sub] += dotg(act, downs[g][...])
-
-    if own:
-        return
 
     @pl.when(step == groups * chunks - 1)
     def _():
@@ -367,7 +358,7 @@
         def body(r):
             at = pl.ds(r, blk)
             valid = valid_rows(info_ref, r, blk)
-            hat, scale = norm_parts(acc[at] + before_ref[at])
+            hat, scale = norm_parts(acc[at])
             out_ref[at] = (valid * (resid_ref[at] + hat * gain + shift)).astype(BF)
             g_out = valid * cot_ref[at].astype(F32)
             low = norm_back(g_out, hat, scale, gain).astype(BF)
@@ -379,57 +370,72 @@
         loop_rows(rows, blk, body)
 
 
-def feed(info, x, biases, ups, downs, own=None, rest=None, cols=512):
+def feed_specs(depth, cols, chunks, rest):
+    own = [
+        pl.BlockSpec((depth, cols), lambda s, *_: (0, jnp.minimum(s, chunks - 1))),
+        pl.BlockSpec((cols, depth), lambda s, *_: (jnp.minimum(s, chunks - 1), 0)),
+    ]
+    part = lambda g, i: pl.BlockSpec(
+        (None, cols, depth), lambda s, *_: (i, jnp.clip(s - g * chunks, 0, chunks - 1), 0)
+    )
+    return [
+        spec for i in range(2) for spec in [own[i]] + [part(g + 1, i) for g in range(len(rest))]
+    ]
+
+
+def feed(info, x, biases, up, down, rest, resid, cot, bias_down, gains, shifts, cols=512):
     rows, depth = x.shape
-    groups, hidden = len(ups), ups[0].shape[1]
+    groups, hidden = 1 + len(rest), up.shape[1]
     chunks = hidden // cols
     once = lambda shape: pl.BlockSpec(shape, lambda s, *_: (0, 0), pipeline_mode=pl.Buffered(1))
     anyspace = pl.BlockSpec(memory_space=pl.ANY)
-    part = lambda g: (lambda s, *_: (0, jnp.clip(s - g * chunks, 0, chunks - 1)))
-    part_t = lambda g: (lambda s, *_: (jnp.clip(s - g * chunks, 0, chunks - 1), 0))
-    wide = pl.BlockSpec((rows, cols), lambda s, *_: (0, s))
-    low = jax.ShapeDtypeStruct((rows, depth), BF)
-    slope = jax.ShapeDtypeStruct((rows, groups * hidden), BF)
-    if rest is None:
-        more, args = [once((1, depth))], [own]
-        out_specs = [wide, wide, once((rows, depth))]
-        out_shape = [slope, slope, jax.ShapeDtypeStruct((rows, depth), F32)]
-        scratch = []
-    else:
-        before, resid, cot, gains, shifts = rest
-        more, args = [anyspace] * 3 + [once(gains.shape)] * 2, [resid, cot, before, gains, shifts]
-        out_specs = [wide, once((rows, depth)), once((rows, depth)), once((8, depth))]
-        out_shape = [slope, low, low, jax.ShapeDtypeStruct((8, depth), F32)]
-        scratch = [
-            pltpu.VMEM((rows, depth), F32),
-            pltpu.VMEM((rows, depth), F32),
-            pltpu.VMEM((rows, depth), F32),
-            pltpu.VMEM((rows, depth), BF),
-            pltpu.SemaphoreType.DMA((3,)),
-        ]
+    own = lambda g: (lambda s, *_: (0, jnp.clip(s - g * chunks, 0, chunks - 1)))
     return pl.pallas_call(
-        functools.partial(feed_kernel, groups=groups, chunks=chunks, sub=min(512, rows), own=rest is None),
+        functools.partial(feed_kernel, groups=groups, chunks=chunks, sub=min(512, rows)),
         grid_spec=pltpu.PrefetchScalarGridSpec(
             num_scalar_prefetch=1,
             grid=(groups * chunks,),
-            in_specs=[once((rows, depth)), pl.BlockSpec((1, 1, cols), lambda s, *_: (s, 0, 0))]
-            + [pl.BlockSpec((depth, cols), part(g)) for g in range(groups)]
-            + [pl.BlockSpec((cols, depth), part_t(g)) for g in range(groups)]
-            + more,
-            out_specs=out_specs,
-            scratch_shapes=scratch,
+            in_specs=[
+                once((rows, depth)),
+                pl.BlockSpec((1, 1, cols), lambda s, *_: (s, 0, 0)),
+                anyspace,
+                anyspace,
+                once((1, depth)),
+                once(gains.shape),
+                once(gains.shape),
+            ]
+            + feed_specs(depth, cols, chunks, rest),
+            out_specs=[
+                pl.BlockSpec((rows, cols), lambda s, *_: (0, s)),
+                pl.BlockSpec((rows, cols), own(0)),
+                once((rows, depth)),
+                once((rows, depth)),
+                once((8, depth)),
+            ],
+            scratch_shapes=[
+                pltpu.VMEM((rows, depth), F32),
+                pltpu.VMEM((rows, depth), F32),
+                pltpu.VMEM((rows, depth), BF),
+                pltpu.SemaphoreType.DMA((2,)),
+            ],
         ),
-        out_shape=out_shape,
+        out_shape=[
+            jax.ShapeDtypeStruct((rows, groups * hidden), BF),
+            jax.ShapeDtypeStruct((rows, hidden), BF),
+            jax.ShapeDtypeStruct((rows, depth), BF),
+            jax.ShapeDtypeStruct((rows, depth), BF),
+            jax.ShapeDtypeStruct((8, depth), F32),
+        ],
         compiler_params=pltpu.CompilerParams(vmem_limit_bytes=60 * MIB),
         cost_estimate=pl.CostEstimate(flops=rows * depth, bytes_accessed=rows * depth, transcendentals=0),
         name="feed",
-    )(info, x, biases.reshape(-1, 1, cols), *ups, *downs, *args)
+    )(info, x, biases.reshape(-1, 1, cols), resid, cot, bias_down, gains, shifts, up, *rest, down, *rest)
 
 
 def feed_back_kernel(info_ref, *refs, groups, chunks, sub):
-    gb_ref, own_slope, rest_slope, resid_hbm, attn_hbm, cot_hbm, gain_ref = refs[:7]
-    ups, downs = refs[7 : 7 + groups], refs[7 + groups : 7 + 2 * groups]
-    gp_ref, gr_ref, ga_ref, sums_ref, acc, resid_ref, attn_ref, cot_ref, sems = refs[7 + 2 * groups :]
+    gb_ref, slope_ref, resid_hbm, attn_hbm, cot_hbm, gain_ref = refs[:6]
+    ups, downs = refs[6 : 6 + groups], refs[6 + groups : 6 + 2 * groups]
+    gp_ref, gr_ref, ga_ref, sums_ref, acc, resid_ref, attn_ref, cot_ref, sems = refs[6 + 2 * groups :]
     step = pl.program_id(0)
     rows = gb_ref.shape[0]
     late = [
@@ -449,11 +455,10 @@
         def _():
             for r in range(0, rows, sub):
                 grad = dotg(gb_ref[r : r + sub], downs[g][...], NT)
-                slope_ref = rest_slope if g else own_slope
                 low = (grad * slope_ref[r : r + sub].astype(F32)).astype(BF)
                 if g == 0:
                     gp_ref[r : r + sub] = low
-                acc[r : r + sub] += dotg(low, ups[g][...], NT)
+                acc[r : r + sub] += dotg(low, ups[g][...], NN if g else NT)
 
     @pl.when(step == groups * chunks - 1)
     def _():
@@ -479,14 +484,13 @@
         loop_rows(rows, blk, body)
 
 
-def feed_back(info, gb, own_slope, rest_slope, ups, downs, resid, attn_sum, cot, gains, cols=512):
+def feed_back(info, gb, slope, up, down, rest, resid, attn_sum, cot, gains, cols=512):
     rows, depth = gb.shape
-    groups, hidden = len(ups), ups[0].shape[1]
+    groups, hidden = 1 + len(rest), up.shape[1]
     chunks = hidden // cols
     once = lambda shape: pl.BlockSpec(shape, lambda s, *_: (0, 0), pipeline_mode=pl.Buffered(1))
     anyspace = pl.BlockSpec(memory_space=pl.ANY)
     own = lambda g: (lambda s, *_: (0, jnp.clip(s - g * chunks, 0, chunks - 1)))
-    own_t = lambda g: (lambda s, *_: (jnp.clip(s - g * chunks, 0, chunks - 1), 0))
     return pl.pallas_call(
         functools.partial(feed_back_kernel, groups=groups, chunks=chunks, sub=min(512, rows)),
         grid_spec=pltpu.PrefetchScalarGridSpec(
@@ -494,15 +498,13 @@
             grid=(groups * chunks,),
             in_specs=[
                 once((rows, depth)),
-                pl.BlockSpec((rows, cols), own(0)),
-                pl.BlockSpec((rows, cols), lambda s, *_: (0, jnp.maximum(s - chunks, 0))),
+                pl.BlockSpec((rows, cols), lambda s, *_: (0, s)),
                 anyspace,
                 anyspace,
                 anyspace,
                 once(gains.shape),
             ]
-            + [pl.BlockSpec((depth, cols), own(g)) for g in range(groups)]
-            + [pl.BlockSpec((cols, depth), own_t(g)) for g in range(groups)],
+            + feed_specs(depth, cols, chunks, rest),
             out_specs=[
                 pl.BlockSpec((rows, cols), own(0)),
                 once((rows, depth)),
@@ -526,7 +528,7 @@
         compiler_params=pltpu.CompilerParams(vmem_limit_bytes=60 * MIB),
         cost_estimate=pl.CostEstimate(flops=rows * depth, bytes_accessed=rows * depth, transcendentals=0),
         name="feed_back",
-    )(info, gb, own_slope, rest_slope, resid, attn_sum, cot, gains, *ups, *downs)
+    )(info, gb, slope, resid, attn_sum, cot, gains, up, *rest, down, *rest)
 
 
 def feed_grad_kernel(*refs, groups):
@@ -598,13 +600,13 @@
 def join_kernel(pick_ref, x_ref, gain_ref, shift_ref, *refs, blocks, each):
     parts, (attn_ref, resid_ref, low_ref) = refs[:-3], refs[-3:]
     block = pl.program_id(0) // each
-    total = None
+    total = 0.0
     for g in range(len(parts) // blocks):
         wanted = pick_ref[g * blocks + block]
         part = parts[g * blocks][...]
         for b in range(1, blocks):
             part = jnp.where(wanted == b, parts[g * blocks + b][...], part)
-        total = part if total is None else total + part.astype(F32)
+        total = total + part.astype(F32)
     attn_ref[...] = total
     hat, _ = norm_parts(total)
     resid = x_ref[...].astype(F32) + hat * gain_ref[1:2] + shift_ref[1:2]
@@ -620,13 +622,15 @@
     each = rows // blocks // blk
     whole = pl.BlockSpec(gains.shape, lambda i, *_: (0, 0))
     block = pl.BlockSpec((blk, depth), lambda i, *_: (i, 0))
-    part = pl.BlockSpec((blk, depth), lambda i, *_: (lax.rem(i, each), 0))
+    part = lambda g, b: pl.BlockSpec(
+        (blk, depth), lambda i, pick: (jnp.clip(i - pick[g * blocks + b] * each, 0, each - 1), 0)
+    )
     return pl.pallas_call(
         functools.partial(join_kernel, blocks=blocks, each=each),
         grid_spec=pltpu.PrefetchScalarGridSpec(
             num_scalar_prefetch=1,
             grid=(rows // blk,),
-            in_specs=[block, whole, whole] + [part] * (len(shares) * blocks),
+            in_specs=[block, whole, whole] + [part(g, b) for g in range(len(shares)) for b in range(blocks)],
             out_specs=[block, block, block],
         ),
         out_shape=[
@@ -644,7 +648,7 @@
     ddown_ref[...] = down_ref[...].astype(F32)
 
 
-def widen(grads, blk=256):
+def widen(grads, blk=512):
     hidden, depth = grads.shape[0] // 2, grads.shape[1]
     blk = min(blk, hidden)
     count = hidden // blk
@@ -1058,11 +1062,10 @@
     def to_owner(v, r):
         return shift(v, "tensor", groups, groups - r)
 
-    up_piece = lax.dynamic_slice_in_dim(up_weight, replica * (depth // replicas), depth // replicas, 0)
-    down_piece = lax.dynamic_slice_in_dim(
-        down_weight, replica * (hidden // replicas), hidden // replicas, 0
-    )
-    gather = lambda v: lax.all_gather(v, "dp", axis=0, tiled=True)
+    count = hidden // replicas
+    up_piece = lax.dynamic_slice_in_dim(up_weight, replica * count, count, 1)
+    down_piece = lax.dynamic_slice_in_dim(down_weight, replica * count, count, 0)
+    piece = jnp.stack([jnp.transpose(up_piece), down_piece])
 
     freqs = 10000.0 ** (-jnp.arange(HD // 2).astype(F32) * 2.0 / HD)
     angles = jnp.arange(slots).astype(F32)[:, None] * freqs[None, :]
@@ -1073,12 +1076,12 @@
     normed_one = first_norm(x, norm_gains, norm_shifts)
     weights = (w_query, w_key, w_value)
     joint = project(here, normed_one, *weights, cosine, sine)
-    joint, x_rest, up_piece, down_piece, bias = lax.optimization_barrier((joint, x_rest, up_piece, down_piece, bias_up))
-    up_pieces, down_pieces, bias_rest = others(up_piece), others(down_piece), others(bias)
+    joint, x_rest, piece, bias = lax.optimization_barrier((joint, x_rest, piece, bias_up))
+    pieces, bias_rest = others(piece), others(bias)
     normed_one_rest = [first_norm(v, norm_gains, norm_shifts) for v in x_rest]
     for r, n in enumerate(normed_one_rest):
         joint = project(place(r + 1), n, *weights, cosine, sine, joint)
-    joint, up_pieces, down_pieces, bias_rest = lax.optimization_barrier((joint, up_pieces, down_pieces, bias_rest))
+    joint, pieces, bias_rest = lax.optimization_barrier((joint, pieces, bias_rest))
     blk = min(512, rows)
     each = rows // blk
     odd = lambda r: lax.rem(place(r), 2)
@@ -1092,28 +1095,25 @@
             joint, arrived = lax.optimization_barrier((joint, [v[:k] for v in arrived])), arrived
             joint, early = joint
             arrived = [list(e) + v[k:] for e, v in zip(early, arrived)]
-        *held, share = attend(here * each + ranks(0, k), lengths, joint, w_out, held, F32, blk)
+        *held, share = attend(here * each + ranks(0, k), lengths, joint, w_out, held, BF, blk)
         shares.append(share)
     mixed, lse = held
     shares = [shares] + arrived
     picks = jnp.concatenate([ranks(groups - r, k) for r in range(groups) for k in range(each)])
-    up_rest, down_rest = [gather(p) for p in up_pieces], [gather(p) for p in down_pieces]
+    rest = [lax.all_gather(p, "dp", axis=1, tiled=True) for p in pieces]
     biases = jnp.concatenate([bias_up] + bias_rest).astype(F32)
 
     info = jnp.stack([lengths[0], me * rows]).astype(jnp.int32)
     cot = cotangent.reshape(rows, depth)
     attn_sum, resid, normed_two = join(x, norm_gains, norm_shifts, shares, picks)
     normed_two_rest = others(normed_two)
-    slope, act, branch = feed(
-        info, normed_two, biases[:hidden], [up_weight], [down_weight], own=bias_down.reshape(1, depth)
+    slope, act, layer_out, g_branch, sums3 = feed(
+        info, normed_two, biases, up_weight, down_weight, rest, resid, cot,
+        bias_down.reshape(1, depth), norm_gains, norm_shifts,
     )
-    slope_rest, layer_out, g_branch, sums3 = feed(
-        info, normed_two, biases[hidden:], up_rest, down_rest, rest=(branch, resid, cot, norm_gains, norm_shifts)
-    )
-    ups, downs = [up_weight] + up_rest, [down_weight] + down_rest
     g_branch_rest = others(g_branch)
     g_pre, g_resid, g_attn, sums21 = feed_back(
-        info, g_branch, slope, slope_rest, ups, downs, resid, attn_sum, cot, norm_gains
+        info, g_branch, slope, up_weight, down_weight, rest, resid, attn_sum, cot, norm_gains
     )
     g_attn_rest = others(g_attn)
     g_pre, normed_two_rest = lax.optimization_barrier((g_pre, normed_two_rest))

time: 525 us -> 519 us (0.989)
  Pallas kernels: 414 us -> 405 us
    pallas_call x2 -> x1, Pallas kernels: 44.7 us -> 40.1 us  [feed(): pl.pallas_call(functools.partial(feed_kernel, groups=groups, chunks=chunk...]
    ppermute x9 -> x8, waiting for transfers between devices: 46.3 us -> 49.7 us  [shift(): lax.ppermute(x, axis, [((i + step) % count, i) for i in range(count)])]
    ppermute x9 -> x8, starting transfers between devices: 12.8 us -> 10.9 us  [shift(): lax.ppermute(x, axis, [((i + step) % count, i) for i in range(count)])]
  transfers between devices with their start and end apart: 12 -> 10, of which waited for: 4 -> 4; matrix products, arithmetic and copies ran while one was open for 4% -> 4% of each run, Pallas kernels for 78% -> 77%
where the time goes in v5:
time: 519 us; the launch traced here: 510 us
  Pallas kernels  405 us (78%)
  waiting for transfers between devices  49.8 us (10%)
  between operations  15.4 us (3%)
  other arithmetic  15.3 us (3%)
  local copies, waits for them, and re-layouts  13 us (3%)
  starting transfers between devices  11.5 us (2%)
    pallas_call x1, Pallas kernels, tail(): pl.pallas_call(functools.partial(tail_kernel, bits=bits, groups=groups, s...  109 us
    pallas_call x1, Pallas kernels, attend_back(): pl.pallas_call(functools.partial(attend_back_kernel, blk=blk, blocks=bloc...  79.6 us
    pallas_call x4, Pallas kernels, attend(): pl.pallas_call(functools.partial(attend_kernel, blk=blk), grid_spec=pltpu...  57.2 us
    ppermute x8, waiting for transfers between devices, shift(): lax.ppermute(x, axis, [((i + step) % count, i) for i in range(count)])  49.7 us
    pallas_call x1, Pallas kernels, feed(): pl.pallas_call(functools.partial(feed_kernel, groups=groups, chunks=chunk...  40.1 us
    pallas_call x1, Pallas kernels, feed_back(): pl.pallas_call(functools.partial(feed_back_kernel, groups=groups, chunks=...  34.1 us
    pallas_call x1, Pallas kernels, feed_grad(): pl.pallas_call(functools.partial(feed_grad_kernel, groups=groups), grid=(...  33.6 us
    pallas_call x2, Pallas kernels, project(): pl.pallas_call(kernel, grid_spec=pltpu.PrefetchScalarGridSpec(num_scalar_...  15 us
  transfers between devices with their start and end apart: 10, of which 4 were waited for; matrix products, arithmetic and copies ran while one was open for 4% of the time, Pallas kernels for 77%

profile of v5, /device:TPU:0, one launch (start us, length us, event | category | flops | bytes accessed | tf_op | source)
XLA Modules:
  0.0 509.5 jit_solution(9050575487639800998)
XLA Ops:
  11.4 3.7 first_norm.2.refs_0_
  15.1 3.7 fusion
  18.8 3.0 pad_maximum_fusion
  21.8 7.5 %project.2.refs_6_ = bf16[2048,1536]{1,0:T(8,128)(2,1)} custom-call(s32[1]{0:T(128)} %bitcast.1.at.at_ref, bf16[1024,1024]{1,0:T(8,128)(2,1)} %first_norm.2.refs_0_, bf16[1024,512]{1,0:T(8,128)(2,1)} %wq_ref.1, bf16[1024,512]{1,0:T(8,128)(2,1)} %wk_ref.1, bf16[1024,512]{1,0:T(8,128)(2,1)} %wv_ref.1, f32[2048,128]{1,0:T(8,128)} %get-tuple-element.164.refs_4_.cos_ref, ...), custom_call_target="tpu_custom_call" | custom-call | flops 1048576 | bytes 1048576 | tf_op jit(solution)/shard_map/project/pallas_call | solution.py:50
  30.4 25.7 %collective-permute-done.x_ref = bf16[1024,1024]{1,0:T(8,128)(2,1)S(1)} collective-permute-done((bf16[1024,1024]{1,0:T(8,128)(2,1)}, bf16[1024,1024]{1,0:T(8,128)(2,1)S(1)}, u32[]{:S(2)}, u32[]{:S(2)}) %collective-permute-start) | collective-permute-done | bytes 2097184 | tf_op jit(solution)/shard_map/ppermute | solution.py:1031
  58.1 3.7 first_norm.3.refs_0_.refs_1_
  61.8 7.5 %project.3.q_ref.k_ref.v_ref = bf16[2048,1536]{1,0:T(8,128)(2,1)} custom-call(s32[1]{0:T(128)S(6)} %select_n.65.at.at_ref, bf16[1024,1024]{1,0:T(8,128)(2,1)} %first_norm.3.refs_0_.refs_1_, bf16[1024,512]{1,0:T(8,128)(2,1)} %wq_ref.1, bf16[1024,512]{1,0:T(8,128)(2,1)} %wk_ref.1, bf16[1024,512]{1,0:T(8,128)(2,1)} %wv_ref.1, ...), custom_call_target="tpu_custom_call", output_to_operand_aliasing={{}: (7, {})} | custom-call | flops 1048576 | bytes 1048576 | tf_op jit(solution)/shard_map/project/pallas_call | solution.py:50
  71.4 16.2 %attend.4 = (bf16[2048,512]{1,0:T(8,128)(2,1)}, f32[4,2,2048]{2,1,0:T(2,128)}, bf16[512,1024]{1,0:T(8,128)(2,1)}) custom-call(s32[1]{0:T(128)S(6)} %add.75.at_ref, s32[1]{0:T(128)S(6)} %copy.59.len_ref, bf16[2048,1536]{1,0:T(8,128)(2,1)} %project.3.q_ref.k_ref.v_ref, bf16[2048,1536]{1,0:T(8,128)(2,1)} %project.3.q_ref.k_ref.v_ref, ...), custom_call_target="tpu_custom_call" | custom-call | flops 1048576 | bytes 1048576 | tf_op jit(solution)/shard_map/attend/pallas_call | solution.py:147
  87.7 8.2 %attend.5 = (bf16[2048,512]{1,0:T(8,128)(2,1)}, f32[4,2,2048]{2,1,0:T(2,128)}, bf16[512,1024]{1,0:T(8,128)(2,1)}) custom-call(s32[1]{0:T(128)S(6)} %add.73.at_ref, s32[1]{0:T(128)S(6)} %copy.59.len_ref, bf16[2048,1536]{1,0:T(8,128)(2,1)} %project.3.q_ref.k_ref.v_ref, ...), custom_call_target="tpu_custom_call", output_to_operand_aliasing={{0}: (6, {}), {1}: (7, {})} | custom-call | flops 1048576 | bytes 1048576 | tf_op jit(solution)/shard_map/attend/pallas_call | solution.py:147
  95.9 20.3 %attend.6 = (bf16[2048,512]{1,0:T(8,128)(2,1)}, f32[4,2,2048]{2,1,0:T(2,128)}, bf16[512,1024]{1,0:T(8,128)(2,1)}) custom-call(s32[1]{0:T(128)S(6)} %add.77.at_ref, s32[1]{0:T(128)S(6)} %copy.59.len_ref, bf16[2048,1536]{1,0:T(8,128)(2,1)} %project.3.q_ref.k_ref.v_ref, ...), custom_call_target="tpu_custom_call", output_to_operand_aliasing={{0}: (6, {}), {1}: (7, {})} | custom-call | flops 1048576 | bytes 1048576 | tf_op jit(solution)/shard_map/attend/pallas_call | solution.py:147
  120.0 12.5 %attend.7 = (bf16[2048,512]{1,0:T(8,128)(2,1)}, f32[4,2,2048]{2,1,0:T(2,128)}, bf16[512,1024]{1,0:T(8,128)(2,1)}) custom-call(s32[1]{0:T(128)S(6)} %add.76.at_ref, s32[1]{0:T(128)S(6)} %copy.59.len_ref, bf16[2048,1536]{1,0:T(8,128)(2,1)} %project.3.q_ref.k_ref.v_ref, ...), custom_call_target="tpu_custom_call", output_to_operand_aliasing={{0}: (6, {}), {1}: (7, {})} | custom-call | flops 1048576 | bytes 1048576 | tf_op jit(solution)/shard_map/attend/pallas_call | solution.py:147
  132.6 7.7 %collective-permute-done.4.refs_3_ = bf16[512,1024]{1,0:T(8,128)(2,1)S(1)} collective-permute-done((bf16[512,1024]{1,0:T(8,128)(2,1)}, bf16[512,1024]{1,0:T(8,128)(2,1)S(1)}, u32[]{:S(2)}, u32[]{:S(2)}) %collective-permute-start.4) | collective-permute-done | bytes 1048608 | tf_op jit(solution)/shard_map/ppermute | solution.py:1031
  141.2 8.9 %join.1 = (f32[1024,1024]{1,0:T(8,128)}, f32[1024,1024]{1,0:T(8,128)}, bf16[1024,1024]{1,0:T(8,128)(2,1)}) custom-call(s32[4]{0:T(128)} %pad_add_fusion.1.pick_ref, bf16[1024,1024]{1,0:T(8,128)(2,1)} %bitcast.23, f32[4,1024]{1,0:T(4,128)} %gain_ref.7, f32[4,1024]{1,0:T(4,128)} %refs_6_.2, bf16[512,1024]{1,0:T(8,128)(2,1)} %get-tuple-element.69.refs_0_, ...), custom_call_target="tpu_custom_call" | custom-call | tf_op jit(solution)/shard_map/join/pallas_call | solution.py:628
  152.5 40.1 %feed.1 = (bf16[1024,4096]{1,0:T(8,128)(2,1)}, bf16[1024,2048]{1,0:T(8,128)(2,1)}, bf16[1024,1024]{1,0:T(8,128)(2,1)}, bf16[1024,1024]{1,0:T(8,128)(2,1)}, f32[8,1024]{1,0:T(8,128)}) custom-call(s32[2]{0:T(128)} %pad_add_fusion.info_ref, bf16[1024,1024]{1,0:T(8,128)(2,1)} %get-tuple-element.79.refs_0_.refs_5_, f32[8,1,512]{2,1,0:T(1,128)} %maximum_convert_fusion.refs_1_, ...), custom_call_target="tpu_custom_call" | custom-call | flops 1048576 | bytes 1048576 | tf_op jit(solution)/shard_map/feed/pallas_call | solution.py:393
  193.6 34.1 %feed_back.1 = (bf16[1024,2048]{1,0:T(8,128)(2,1)}, f32[1024,1024]{1,0:T(8,128)}, bf16[1024,1024]{1,0:T(8,128)(2,1)}, f32[8,1024]{1,0:T(8,128)}) custom-call(s32[2]{0:T(128)} %pad_add_fusion.info_ref, bf16[1024,1024]{1,0:T(8,128)(2,1)} %get-tuple-element.85.refs_0_.refs_7_, bf16[1024,4096]{1,0:T(8,128)(2,1)} %get-tuple-element.86.refs_1_, ...), custom_call_target="tpu_custom_call" | custom-call | flops 1048576 | bytes 1048576 | tf_op jit(solution)/shard_map/feed_back/pallas_call | solution.py:494
  230.8 4.8 mixed_back.2.refs_0_
  235.6 8.1 %collective-permute-done.7.refs_8_ = bf16[1024,1024]{1,0:T(8,128)(2,1)} collective-permute-done((bf16[1024,1024]{1,0:T(8,128)(2,1)}, bf16[1024,1024]{1,0:T(8,128)(2,1)}, u32[]{:S(2)}, u32[]{:S(2)}) %collective-permute-start.7) | collective-permute-done | bytes 2097184 | tf_op jit(solution)/shard_map/ppermute | solution.py:1031
  243.7 33.6 %feed_grad.1 = (bf16[2,2048,1024]{2,1,0:T(8,128)(2,1)}, f32[4,1,512]{2,1,0:T(1,128)}) custom-call(bf16[1024,2048]{1,0:T(8,128)(2,1)} %refs_0_.1, bf16[2048,1024]{1,0:T(8,128)(2,1)} %refs_1_.5, f32[4,1,512]{2,1,0:T(1,128)} %slice.69.refs_2_, bf16[1024,2048]{1,0:T(8,128)(2,1)} %get-tuple-element.92.refs_3_, bf16[1024,2048]{1,0:T(8,128)(2,1)} %get-tuple-element.93.refs_4_, ...), custom_call_target="tpu_custom_call" | custom-call | flops 25769803776 | bytes 20971520 | tf_op jit(solution)/shard_map/feed_grad/pallas_call | solution.py:562
  277.3 8.3 %collective-permute-done.6.x_ref.refs_3_ = bf16[1024,1024]{1,0:T(8,128)(2,1)S(1)} collective-permute-done((bf16[1024,1024]{1,0:T(8,128)(2,1)}, bf16[1024,1024]{1,0:T(8,128)(2,1)S(1)}, u32[]{:S(2)}, u32[]{:S(2)}) %collective-permute-start.6) | collective-permute-done | bytes 2097184 | tf_op jit(solution)/shard_map/ppermute | solution.py:1031
  288.0 5.1 %mixed_back.3.do_ref = bf16[2048,512]{1,0:T(8,128)(2,1)} custom-call(s32[1]{0:T(128)S(6)} %select_n.65.at.at_ref, bf16[1024,1024]{1,0:T(8,128)(2,1)} %copy-done, bf16[512,1024]{1,0:T(8,128)(2,1)} %w_ref.11, bf16[2048,512]{1,0:T(8,128)(2,1)} %mixed_back.2.refs_0_), custom_call_target="tpu_custom_call", output_to_operand_aliasing={{}: (3, {})} | custom-call | flops 1048576 | bytes 1048576 | tf_op jit(solution)/shard_map/mixed_back/pallas_call | solution.py:1010
  293.1 79.6 %attend_back.1 = (bf16[2048,512]{1,0:T(8,128)(2,1)}, bf16[2048,512]{1,0:T(8,128)(2,1)}, bf16[2048,512]{1,0:T(8,128)(2,1)}) custom-call(s32[1]{0:T(128)S(6)} %copy.59.len_ref, bf16[2048,1536]{1,0:T(8,128)(2,1)} %project.3.q_ref.k_ref.v_ref, bf16[2048,1536]{1,0:T(8,128)(2,1)} %project.3.q_ref.k_ref.v_ref, bf16[2048,1536]{1,0:T(8,128)(2,1)} %project.3.q_ref.k_ref.v_ref, ...), custom_call_target="tpu_custom_call" | custom-call | flops 1048576 | bytes 1048576 | tf_op jit(solution)/shard_map/attend_back/pallas_call | solution.py:256
  372.7 108.6 %tail.1 = (bf16[4096,512]{1,0:T(8,128)(2,1)}, bf16[1024,1024]{1,0:T(8,128)(2,1)}, f32[16,1024]{1,0:T(8,128)}) custom-call(bf16[2048,512]{1,0:T(8,128)(2,1)} %get-tuple-element.99.gq_ref, bf16[2048,512]{1,0:T(8,128)(2,1)} %get-tuple-element.100.gk_ref, bf16[2048,512]{1,0:T(8,128)(2,1)} %get-tuple-element.101.gv_ref, ...), custom_call_target="tpu_custom_call" | custom-call | flops 524288 | bytes 524288 | tf_op jit(solution)/shard_map/tail/pallas_call | solution.py:962
  481.3 5.4 %convert_bitcast_fusion = (f32[512,1024]{0,1:T(8,128)S(1)}, f32[1024,512]{1,0:T(8,128)}, f32[1024,512]{1,0:T(8,128)}, f32[1024,512]{1,0:T(8,128)}) fusion(bf16[4096,512]{1,0:T(8,128)(2,1)} %get-tuple-element.107), kind=kLoop, calls=%fused_computation | loop fusion | flops 2097152 | bytes 12582912 | tf_op jit(solution)/shard_map/convert_element_type | solution.py:1147
  491.0 9.9 %widen.1 = (f32[1024,2048]{1,0:T(8,128)}, f32[2048,1024]{1,0:T(8,128)}) custom-call(bf16[4096,1024]{1,0:T(8,128)(2,1)} %all-reduce.3.cloned.1.call-done.up_ref.down_ref, bf16[4096,1024]{1,0:T(8,128)(2,1)} %all-reduce.3.cloned.1.call-done.up_ref.down_ref), custom_call_target="tpu_custom_call" | custom-call | tf_op jit(solution)/shard_map/widen/pallas_call | solution.py:655
  (76 shorter events, 27.7 us)
Async XLA Ops:
  7.2 145.3 %all-gather.2.cloned.1.call-start = ((), (), s32[]{:S(2)}) async-start(), calls=%async_computation | async-start | bytes 8912896 | tf_op jit(solution)/shard_map/all_gather | solution.py:1103
  7.2 48.8 %collective-permute-start = (bf16[1024,1024]{1,0:T(8,128)(2,1)}, bf16[1024,1024]{1,0:T(8,128)(2,1)S(1)}, u32[]{:S(2)}, u32[]{:S(2)}) collective-permute-start(bf16[1024,1024]{1,0:T(8,128)(2,1)} %bitcast.21), channel_id=1, source_target_pairs={{1,0},{0,1},{3,2},{2,3},{5,4},{4,5},{7,6},{6,7},{9,8},{8,9},{11,10... | collective-permute-start | bytes 6291464 | tf_op jit(solution)/shard_map/ppermute | solution.py:1031
  21.8 36.0 %copy-start.11 = (bf16[2048]{0:T(1024)(128)(2,1)S(1)}, bf16[2048]{0:T(1024)(128)(2,1)}, u32[]{:S(2)}) copy-start(bf16[2048]{0:T(1024)(128)(2,1)} %param.21) | copy-start | bytes 12292
  56.1 2.0 copy-start.1
  56.1 13.3 %collective-permute-start.1 = (bf16[2,128,1024]{2,1,0:T(8,128)(2,1)S(1)}, bf16[2,128,1024]{2,1,0:T(8,128)(2,1)S(1)}, u32[]{:S(2)}, u32[]{:S(2)}) collective-permute-start(bf16[2,128,1024]{2,1,0:T(8,128)(2,1)S(1)} %pad_maximum_fusion.2), channel_id=1, source_target_pairs={{1,0},{0,1},{3,2},{2,3},{5,4},{4,5},{7,6},{6,7},{9,8},{8,9},{11,10... | collective-permute-start | bytes 1572872 | tf_op jit(solution)/shard_map/ppermute | solution.py:1031
  57.8 11.5 %collective-permute-start.2 = (bf16[2048]{0:T(1024)(128)(2,1)S(1)}, bf16[2048]{0:T(1024)(128)(2,1)S(1)}, u32[]{:S(2)}, u32[]{:S(2)}) collective-permute-start(bf16[2048]{0:T(1024)(128)(2,1)S(1)} %copy-done.11), channel_id=1, source_target_pairs={{1,0},{0,1},{3,2},{2,3},{5,4},{4,5},{7,6},{6,7},{9,8},{8,9},{11,10... | collective-permute-start | bytes 12296 | tf_op jit(solution)/shard_map/ppermute | solution.py:1031
  69.3 0.8 copy-start.5
  70.2 420.9 %all-reduce.3.cloned.1.call-start = ((), (), s32[]{:S(2)}) async-start(), calls=%async_computation.1 | async-start | bytes 16777216 | tf_op jit(solution)/shard_map/psum | solution.py:1128
  87.6 32.4 %collective-permute-start.3 = (bf16[512,1024]{1,0:T(8,128)(2,1)}, bf16[512,1024]{1,0:T(8,128)(2,1)S(1)}, u32[]{:S(2)}, u32[]{:S(2)}) collective-permute-start(bf16[512,1024]{1,0:T(8,128)(2,1)} %get-tuple-element.70), channel_id=1, source_target_pairs={{1,0},{0,1},{3,2},{2,3},{5,4},{4,5},{7,6},{6,7},{9,8},{8,9},{11,10... | collective-permute-start | bytes 3145736 | tf_op jit(solution)/shard_map/ppermute | solution.py:1031
  95.9 22.4 %copy-start.12 = (bf16[1024]{0:T(1024)(128)(2,1)S(1)}, bf16[1024]{0:T(1024)(128)(2,1)}, u32[]{:S(2)}) copy-start(bf16[1024]{0:T(1024)(128)(2,1)} %param.23) | copy-start | bytes 6148
  116.2 24.1 %collective-permute-start.4 = (bf16[512,1024]{1,0:T(8,128)(2,1)}, bf16[512,1024]{1,0:T(8,128)(2,1)S(1)}, u32[]{:S(2)}, u32[]{:S(2)}) collective-permute-start(bf16[512,1024]{1,0:T(8,128)(2,1)} %get-tuple-element.78), channel_id=1, source_target_pairs={{1,0},{0,1},{3,2},{2,3},{5,4},{4,5},{7,6},{6,7},{9,8},{8,9},{11,10... | collective-permute-start | bytes 3145736 | tf_op jit(solution)/shard_map/ppermute | solution.py:1031
  120.0 12.5 %copy-start.3 = (bf16[512,1024]{1,0:T(8,128)(2,1)}, bf16[512,1024]{1,0:T(8,128)(2,1)S(1)}, u32[]{:S(2)}) copy-start(bf16[512,1024]{1,0:T(8,128)(2,1)S(1)} %collective-permute-done.3.refs_2_) | copy-start | bytes 3145732
  140.3 1.0 copy-start.4
  150.2 77.6 %collective-permute-start.5 = (bf16[1024,1024]{1,0:T(8,128)(2,1)}, bf16[1024,1024]{1,0:T(8,128)(2,1)S(1)}, u32[]{:S(2)}, u32[]{:S(2)}) collective-permute-start(bf16[1024,1024]{1,0:T(8,128)(2,1)} %get-tuple-element.79.refs_0_.refs_5_), channel_id=1, source_target_pairs={{1,0},{0,1},{3,2},{2,3},{5,4},{4,5},{7,6},{6,7},{9,8},{8,9},{11,10... | collective-permute-start | bytes 6291464 | tf_op jit(solution)/shard_map/ppermute | solution.py:1031
  152.5 40.5 %copy-start.6 = (f32[8,1,512]{2,1,0:T(1,128)S(1)}, f32[8,1,512]{2,1,0:T(1,128)}, u32[]{:S(2)}) copy-start(f32[8,1,512]{2,1,0:T(1,128)} %maximum_convert_fusion.refs_1_) | copy-start | bytes 49156
  192.6 51.1 %collective-permute-start.7 = (bf16[1024,1024]{1,0:T(8,128)(2,1)}, bf16[1024,1024]{1,0:T(8,128)(2,1)}, u32[]{:S(2)}, u32[]{:S(2)}) collective-permute-start(bf16[1024,1024]{1,0:T(8,128)(2,1)} %get-tuple-element.85.refs_0_.refs_7_), channel_id=1, source_target_pairs={{1,0},{0,1},{3,2},{2,3},{5,4},{4,5},{7,6},{6,7},{9,8},{8,9},{11,10... | collective-permute-start | bytes 6291464 | tf_op jit(solution)/shard_map/ppermute | solution.py:1031
  227.7 1.3 copy-start.13
  229.1 56.5 %collective-permute-start.6 = (bf16[1024,1024]{1,0:T(8,128)(2,1)}, bf16[1024,1024]{1,0:T(8,128)(2,1)S(1)}, u32[]{:S(2)}, u32[]{:S(2)}) collective-permute-start(bf16[1024,1024]{1,0:T(8,128)(2,1)} %get-tuple-element.90.x_ref.refs_2_), channel_id=1, source_target_pairs={{1,0},{0,1},{3,2},{2,3},{5,4},{4,5},{7,6},{6,7},{9,8},{8,9},{11,10... | collective-permute-start | bytes 6291464 | tf_op jit(solution)/shard_map/ppermute | solution.py:1031
  285.6 1.3 copy-start
  285.6 1.3 copy-start.9
  285.6 1.3 copy-start.8
  285.6 1.4 copy-start.10
  486.7 1.8 copy-start.7
  491.0 9.9 %copy-start.2 = (bf16[1024,1024]{1,0:T(8,128)(2,1)S(1)}, bf16[1024,1024]{1,0:T(8,128)(2,1)}, u32[]{:S(2)}) copy-start(bf16[1024,1024]{1,0:T(8,128)(2,1)} %get-tuple-element.106) | copy-start | bytes 6291460
Sparse Core Ops, SparseCore 0:
  70.3 76.4 all-gather.1
  285.7 203.7 all-reduce.2

commit v6 on v5

--- a/solution.py
+++ b/solution.py
@@ -30,38 +30,44 @@
     return jnp.concatenate(parts, axis=1) if len(parts) > 1 else parts[0]
 
 
-def qkv_kernel(x_ref, wq_ref, wk_ref, wv_ref, cos_ref, sin_ref, o_ref):
+def qkv_kernel(at_ref, x_ref, wq_ref, wk_ref, wv_ref, cos_ref, sin_ref, gain_ref, shift_ref, *refs):
+    o_ref, normed_ref = refs[-2:]
     width = wq_ref.shape[1]
-    x, cos, sin = x_ref[...], cos_ref[...], sin_ref[...]
+    hat, _ = norm_parts(x_ref[...].astype(F32))
+    x = (hat * gain_ref[0:1] + shift_ref[0:1]).astype(BF)
+    normed_ref[...] = x
+    cos, sin = cos_ref[...], sin_ref[...]
     o_ref[:, :width] = rotate(dotg(x, wq_ref[...]), cos, sin).astype(BF)
     o_ref[:, width : 2 * width] = rotate(dotg(x, wk_ref[...]), cos, sin).astype(BF)
     o_ref[:, 2 * width :] = dotg(x, wv_ref[...]).astype(BF)
 
 
-def project(where, x, w_query, w_key, w_value, cos, sin, joint=None, blk=256):
+def project(where, x, gains, shifts, w_query, w_key, w_value, cos, sin, held, blk=512):
     rows, depth = x.shape
     width, slots = w_query.shape[1], cos.shape[0]
     blk = min(blk, rows)
     count = rows // blk
-    weight = pl.BlockSpec((depth, width), lambda i, at: (0, 0))
+    once = lambda shape: pl.BlockSpec(shape, lambda i, at: (0, 0), pipeline_mode=pl.Buffered(1))
     angle = pl.BlockSpec((blk, 128), lambda i, at: (at[0] * count + i, 0))
-    kernel = lambda at, *refs: qkv_kernel(*refs[:6], refs[-1])
-    held = [] if joint is None else [joint]
+    block = pl.BlockSpec((blk, depth), lambda i, at: (i, 0))
     return pl.pallas_call(
-        kernel,
+        qkv_kernel,
         grid_spec=pltpu.PrefetchScalarGridSpec(
             num_scalar_prefetch=1,
             grid=(count,),
-            in_specs=[pl.BlockSpec((blk, depth), lambda i, at: (i, 0)), weight, weight, weight, angle, angle]
+            in_specs=[block] + [once((depth, width))] * 3 + [angle, angle, once(gains.shape), once(gains.shape)]
             + [pl.BlockSpec(memory_space=pl.ANY)] * len(held),
-            out_specs=pl.BlockSpec((blk, 3 * width), lambda i, at: (at[0] * count + i, 0)),
+            out_specs=[pl.BlockSpec((blk, 3 * width), lambda i, at: (at[0] * count + i, 0)), block],
         ),
-        out_shape=jax.ShapeDtypeStruct((slots, 3 * width), BF),
-        input_output_aliases={7: 0} if held else {},
+        out_shape=[
+            jax.ShapeDtypeStruct((slots, 3 * width), BF),
+            jax.ShapeDtypeStruct((rows, depth), BF),
+        ],
+        input_output_aliases={9: 0} if held else {},
         compiler_params=pltpu.CompilerParams(vmem_limit_bytes=60 * MIB),
         cost_estimate=pl.CostEstimate(flops=rows * depth, bytes_accessed=rows * depth, transcendentals=0),
         name="project",
-    )(where, x, w_query, w_key, w_value, cos, sin, *held)
+    )(where, x, w_query, w_key, w_value, cos, sin, gains, shifts, *held)
 
 
 def attend_kernel(at_ref, len_ref, q_ref, k_ref, v_ref, w_ref, *refs, blk):
@@ -383,15 +389,16 @@
     ]
 
 
-def feed(info, x, biases, up, down, rest, resid, cot, bias_down, gains, shifts, cols=512):
+def feed(info, x, biases, up, down, rest, resid, cot, bias_down, gains, shifts, cols=1024):
     rows, depth = x.shape
     groups, hidden = 1 + len(rest), up.shape[1]
+    cols = min(cols, hidden)
     chunks = hidden // cols
     once = lambda shape: pl.BlockSpec(shape, lambda s, *_: (0, 0), pipeline_mode=pl.Buffered(1))
     anyspace = pl.BlockSpec(memory_space=pl.ANY)
     own = lambda g: (lambda s, *_: (0, jnp.clip(s - g * chunks, 0, chunks - 1)))
     return pl.pallas_call(
-        functools.partial(feed_kernel, groups=groups, chunks=chunks, sub=min(512, rows)),
+        functools.partial(feed_kernel, groups=groups, chunks=chunks, sub=min(1024, rows)),
         grid_spec=pltpu.PrefetchScalarGridSpec(
             num_scalar_prefetch=1,
             grid=(groups * chunks,),
@@ -492,7 +499,7 @@
     anyspace = pl.BlockSpec(memory_space=pl.ANY)
     own = lambda g: (lambda s, *_: (0, jnp.clip(s - g * chunks, 0, chunks - 1)))
     return pl.pallas_call(
-        functools.partial(feed_back_kernel, groups=groups, chunks=chunks, sub=min(512, rows)),
+        functools.partial(feed_back_kernel, groups=groups, chunks=chunks, sub=min(1024, rows)),
         grid_spec=pltpu.PrefetchScalarGridSpec(
             num_scalar_prefetch=1,
             grid=(groups * chunks,),
@@ -574,27 +581,6 @@
         ),
         name="feed_grad",
     )(up, down, bias.reshape(-1, 1, cols), act, gp, *n2s, *gbs)
-
-
-def norm_kernel(x_ref, gain_ref, shift_ref, o_ref):
-    hat, _ = norm_parts(x_ref[...].astype(F32))
-    o_ref[...] = (hat * gain_ref[0:1] + shift_ref[0:1]).astype(BF)
-
-
-def first_norm(x, gains, shifts, blk=512):
-    rows, depth = x.shape
-    blk = min(blk, rows)
-    whole = pl.BlockSpec(gains.shape, lambda i: (0, 0))
-    block = pl.BlockSpec((blk, depth), lambda i: (i, 0))
-    return pl.pallas_call(
-        norm_kernel,
-        grid=(rows // blk,),
-        in_specs=[block, whole, whole],
-        out_specs=block,
-        out_shape=jax.ShapeDtypeStruct((rows, depth), BF),
-        compiler_params=pltpu.CompilerParams(vmem_limit_bytes=60 * MIB),
-        name="first_norm",
-    )(x, gains, shifts)
 
 
 def join_kernel(pick_ref, x_ref, gain_ref, shift_ref, *refs, blocks, each):
@@ -1002,7 +988,7 @@
     refs[-1][...] = dotg(x_ref[...], w_ref[...], NT).astype(BF)
 
 
-def mixed_back(where, x, w_out, slots, held, blk=256):
+def mixed_back(where, x, w_out, slots, held, blk=512):
     rows, depth = x.shape
     width = w_out.shape[0]
     blk = min(blk, rows)
@@ -1073,14 +1059,14 @@
     cosine = jnp.concatenate([cosine] * 4, axis=1)
     sine = jnp.concatenate([-sine, sine] * 2, axis=1)
     x_rest = others(x)
-    normed_one = first_norm(x, norm_gains, norm_shifts)
     weights = (w_query, w_key, w_value)
-    joint = project(here, normed_one, *weights, cosine, sine)
+    joint, normed_one = project(here, x, norm_gains, norm_shifts, *weights, cosine, sine, [])
     joint, x_rest, piece, bias = lax.optimization_barrier((joint, x_rest, piece, bias_up))
     pieces, bias_rest = others(piece), others(bias)
-    normed_one_rest = [first_norm(v, norm_gains, norm_shifts) for v in x_rest]
-    for r, n in enumerate(normed_one_rest):
-        joint = project(place(r + 1), n, *weights, cosine, sine, joint)
+    normed_one_rest = []
+    for r, v in enumerate(x_rest):
+        joint, n = project(place(r + 1), v, norm_gains, norm_shifts, *weights, cosine, sine, [joint])
+        normed_one_rest.append(n)
     joint, pieces, bias_rest = lax.optimization_barrier((joint, pieces, bias_rest))
     blk = min(512, rows)
     each = rows // blk

time: 519 us -> 516 us (level)
  Pallas kernels: 405 us -> 393 us
  waiting for transfers between devices: 49.8 us -> 58.8 us
    ppermute x8, waiting for transfers between devices: 49.7 us -> 58.8 us  [shift(): lax.ppermute(x, axis, [((i + step) % count, i) for i in range(count)])]
    pallas_call x4 -> x2, Pallas kernels: 22.5 us -> 16.4 us  [project(): pl.pallas_call(qkv_kernel, grid_spec=pltpu.PrefetchScalarGridSpec(num_sca...]
  transfers between devices with their start and end apart: 10 -> 10, of which waited for: 4 -> 5; matrix products, arithmetic and copies ran while one was open for 4% -> 5% of each run, Pallas kernels for 77% -> 76%
where the time goes in v6:
time: 516 us; the launch traced here: 507 us
  Pallas kernels  393 us (76%)
  waiting for transfers between devices  58.8 us (11%)
  other arithmetic  16 us (3%)
  between operations  15.4 us (3%)
  local copies, waits for them, and re-layouts  12.6 us (2%)
  starting transfers between devices  11.4 us (2%)
    pallas_call x1, Pallas kernels, tail(): pl.pallas_call(functools.partial(tail_kernel, bits=bits, groups=groups, s...  108 us
    pallas_call x1, Pallas kernels, attend_back(): pl.pallas_call(functools.partial(attend_back_kernel, blk=blk, blocks=bloc...  79.9 us
    ppermute x8, waiting for transfers between devices, shift(): lax.ppermute(x, axis, [((i + step) % count, i) for i in range(count)])  58.8 us
    pallas_call x4, Pallas kernels, attend(): pl.pallas_call(functools.partial(attend_kernel, blk=blk), grid_spec=pltpu...  57.2 us
    pallas_call x1, Pallas kernels, feed(): pl.pallas_call(functools.partial(feed_kernel, groups=groups, chunks=chunk...  37.2 us
    pallas_call x1, Pallas kernels, feed_back(): pl.pallas_call(functools.partial(feed_back_kernel, groups=groups, chunks=...  34.1 us
    pallas_call x1, Pallas kernels, feed_grad(): pl.pallas_call(functools.partial(feed_grad_kernel, groups=groups), grid=(...  33.6 us
    pallas_call x2, Pallas kernels, project(): pl.pallas_call(qkv_kernel, grid_spec=pltpu.PrefetchScalarGridSpec(num_sca...  16.4 us
  transfers between devices with their start and end apart: 10, of which 5 were waited for; matrix products, arithmetic and copies ran while one was open for 5% of the time, Pallas kernels for 76%

profile of v6, /device:TPU:0, one launch (start us, length us, event | category | flops | bytes accessed | tf_op | source)
XLA Modules:
  0.0 507.2 jit_solution(15227014388396508501)
XLA Ops:
  7.2 3.0 collective-permute-start
  11.4 3.7 fusion
  15.1 3.0 pad_maximum_fusion
  18.1 8.2 %project.2 = (bf16[2048,1536]{1,0:T(8,128)(2,1)}, bf16[1024,1024]{1,0:T(8,128)(2,1)}) custom-call(s32[1]{0:T(128)} %bitcast.1.at_ref, bf16[1024,1024]{1,0:T(8,128)(2,1)} %bitcast.23, bf16[1024,512]{1,0:T(8,128)(2,1)} %wq_ref.5, bf16[1024,512]{1,0:T(8,128)(2,1)} %wk_ref.5, bf16[1024,512]{1,0:T(8,128)(2,1)} %wv_ref.5, f32[2048,128]{1,0:T(8,128)} %get-tuple-element.172.cos_ref, ...), custom_call_target="tpu_custom_call" | custom-call | flops 1048576 | bytes 1048576 | tf_op jit(solution)/shard_map/project/pallas_call | solution.py:53
  27.4 28.7 %collective-permute-done.x_ref = bf16[1024,1024]{1,0:T(8,128)(2,1)S(1)} collective-permute-done((bf16[1024,1024]{1,0:T(8,128)(2,1)}, bf16[1024,1024]{1,0:T(8,128)(2,1)S(1)}, u32[]{:S(2)}, u32[]{:S(2)}) %collective-permute-start) | collective-permute-done | bytes 2097184 | tf_op jit(solution)/shard_map/ppermute | solution.py:1017
  58.1 8.2 %project.3 = (bf16[2048,1536]{1,0:T(8,128)(2,1)}, bf16[1024,1024]{1,0:T(8,128)(2,1)}) custom-call(s32[1]{0:T(128)S(6)} %select_n.65.at_ref, bf16[1024,1024]{1,0:T(8,128)(2,1)} %copy-done.2, bf16[1024,512]{1,0:T(8,128)(2,1)} %wq_ref.5, bf16[1024,512]{1,0:T(8,128)(2,1)} %wk_ref.5, bf16[1024,512]{1,0:T(8,128)(2,1)} %wv_ref.5, ...), custom_call_target="tpu_custom_call", output_to_operand_aliasing={{0}: (9, {})} | custom-call | flops 1048576 | bytes 1048576 | tf_op jit(solution)/shard_map/project/pallas_call | solution.py:53
  66.3 3.0 collective-permute-done.2
  71.0 16.2 %attend.4 = (bf16[2048,512]{1,0:T(8,128)(2,1)}, f32[4,2,2048]{2,1,0:T(2,128)}, bf16[512,1024]{1,0:T(8,128)(2,1)}) custom-call(s32[1]{0:T(128)S(6)} %add.75.at_ref, s32[1]{0:T(128)S(6)} %copy.59.len_ref, bf16[2048,1536]{1,0:T(8,128)(2,1)} %get-tuple-element.77.q_ref.k_ref.v_ref, bf16[2048,1536]{1,0:T(8,128)(2,1)} %get-tuple-element.77.q_ref.k_ref.v_ref, ...), custom_call_target="tpu_custom_call" | custom-call | flops 1048576 | bytes 1048576 | tf_op jit(solution)/shard_map/attend/pallas_call | solution.py:153
  87.3 8.2 %attend.5 = (bf16[2048,512]{1,0:T(8,128)(2,1)}, f32[4,2,2048]{2,1,0:T(2,128)}, bf16[512,1024]{1,0:T(8,128)(2,1)}) custom-call(s32[1]{0:T(128)S(6)} %add.73.at_ref, s32[1]{0:T(128)S(6)} %copy.59.len_ref, bf16[2048,1536]{1,0:T(8,128)(2,1)} %get-tuple-element.77.q_ref.k_ref.v_ref, ...), custom_call_target="tpu_custom_call", output_to_operand_aliasing={{0}: (6, {}), {1}: (7, {})} | custom-call | flops 1048576 | bytes 1048576 | tf_op jit(solution)/shard_map/attend/pallas_call | solution.py:153
  95.5 20.3 %attend.6 = (bf16[2048,512]{1,0:T(8,128)(2,1)}, f32[4,2,2048]{2,1,0:T(2,128)}, bf16[512,1024]{1,0:T(8,128)(2,1)}) custom-call(s32[1]{0:T(128)S(6)} %add.77.at_ref, s32[1]{0:T(128)S(6)} %copy.59.len_ref, bf16[2048,1536]{1,0:T(8,128)(2,1)} %get-tuple-element.77.q_ref.k_ref.v_ref, ...), custom_call_target="tpu_custom_call", output_to_operand_aliasing={{0}: (6, {}), {1}: (7, {})} | custom-call | flops 1048576 | bytes 1048576 | tf_op jit(solution)/shard_map/attend/pallas_call | solution.py:153
  119.8 12.5 %attend.7 = (bf16[2048,512]{1,0:T(8,128)(2,1)}, f32[4,2,2048]{2,1,0:T(2,128)}, bf16[512,1024]{1,0:T(8,128)(2,1)}) custom-call(s32[1]{0:T(128)S(6)} %add.76.at_ref, s32[1]{0:T(128)S(6)} %copy.59.len_ref, bf16[2048,1536]{1,0:T(8,128)(2,1)} %get-tuple-element.77.q_ref.k_ref.v_ref, ...), custom_call_target="tpu_custom_call", output_to_operand_aliasing={{0}: (6, {}), {1}: (7, {})} | custom-call | flops 1048576 | bytes 1048576 | tf_op jit(solution)/shard_map/attend/pallas_call | solution.py:153
  132.3 7.3 %collective-permute-done.4.refs_3_ = bf16[512,1024]{1,0:T(8,128)(2,1)S(1)} collective-permute-done((bf16[512,1024]{1,0:T(8,128)(2,1)}, bf16[512,1024]{1,0:T(8,128)(2,1)S(1)}, u32[]{:S(2)}, u32[]{:S(2)}) %collective-permute-start.4) | collective-permute-done | bytes 1048608 | tf_op jit(solution)/shard_map/ppermute | solution.py:1017
  140.6 8.8 %join.1 = (f32[1024,1024]{1,0:T(8,128)}, f32[1024,1024]{1,0:T(8,128)}, bf16[1024,1024]{1,0:T(8,128)(2,1)}) custom-call(s32[4]{0:T(128)} %pad_add_fusion.1.pick_ref, bf16[1024,1024]{1,0:T(8,128)(2,1)} %bitcast.24, f32[4,1024]{1,0:T(4,128)} %gain_ref.7, f32[4,1024]{1,0:T(4,128)} %refs_6_.2, bf16[512,1024]{1,0:T(8,128)(2,1)} %get-tuple-element.75.refs_0_, ...), custom_call_target="tpu_custom_call" | custom-call | tf_op jit(solution)/shard_map/join/pallas_call | solution.py:614
  151.9 37.2 %feed.1 = (bf16[1024,4096]{1,0:T(8,128)(2,1)}, bf16[1024,2048]{1,0:T(8,128)(2,1)}, bf16[1024,1024]{1,0:T(8,128)(2,1)}, bf16[1024,1024]{1,0:T(8,128)(2,1)}, f32[8,1024]{1,0:T(8,128)}) custom-call(s32[2]{0:T(128)} %pad_add_fusion.info_ref, bf16[1024,1024]{1,0:T(8,128)(2,1)} %get-tuple-element.85.refs_0_.refs_5_, f32[4,1,1024]{2,1,0:T(1,128)} %maximum_convert_fusion.refs_1_, ...), custom_call_target="tpu_custom_call" | custom-call | flops 1048576 | bytes 1048576 | tf_op jit(solution)/shard_map/feed/pallas_call | solution.py:400
  190.0 34.1 %feed_back.1 = (bf16[1024,2048]{1,0:T(8,128)(2,1)}, f32[1024,1024]{1,0:T(8,128)}, bf16[1024,1024]{1,0:T(8,128)(2,1)}, f32[8,1024]{1,0:T(8,128)}) custom-call(s32[2]{0:T(128)} %pad_add_fusion.info_ref, bf16[1024,1024]{1,0:T(8,128)(2,1)} %get-tuple-element.91.refs_0_.refs_7_, bf16[1024,4096]{1,0:T(8,128)(2,1)} %get-tuple-element.92.refs_1_, ...), custom_call_target="tpu_custom_call" | custom-call | flops 1048576 | bytes 1048576 | tf_op jit(solution)/shard_map/feed_back/pallas_call | solution.py:501
  227.2 3.9 mixed_back.2.refs_0_
  231.1 12.2 %collective-permute-done.7.refs_8_ = bf16[1024,1024]{1,0:T(8,128)(2,1)} collective-permute-done((bf16[1024,1024]{1,0:T(8,128)(2,1)}, bf16[1024,1024]{1,0:T(8,128)(2,1)}, u32[]{:S(2)}, u32[]{:S(2)}) %collective-permute-start.7) | collective-permute-done | bytes 2097184 | tf_op jit(solution)/shard_map/ppermute | solution.py:1017
  243.3 33.6 %feed_grad.1 = (bf16[2,2048,1024]{2,1,0:T(8,128)(2,1)}, f32[4,1,512]{2,1,0:T(1,128)}) custom-call(bf16[1024,2048]{1,0:T(8,128)(2,1)} %refs_0_.1, bf16[2048,1024]{1,0:T(8,128)(2,1)} %refs_1_.1, f32[4,1,512]{2,1,0:T(1,128)} %bitcast.32, bf16[1024,2048]{1,0:T(8,128)(2,1)} %get-tuple-element.98.refs_3_, bf16[1024,2048]{1,0:T(8,128)(2,1)} %get-tuple-element.99.refs_4_, ...), custom_call_target="tpu_custom_call" | custom-call | flops 25769803776 | bytes 20971520 | tf_op jit(solution)/shard_map/feed_grad/pallas_call | solution.py:569
  276.9 7.6 %collective-permute-done.6.x_ref.refs_3_ = bf16[1024,1024]{1,0:T(8,128)(2,1)S(1)} collective-permute-done((bf16[1024,1024]{1,0:T(8,128)(2,1)}, bf16[1024,1024]{1,0:T(8,128)(2,1)S(1)}, u32[]{:S(2)}, u32[]{:S(2)}) %collective-permute-start.6) | collective-permute-done | bytes 2097184 | tf_op jit(solution)/shard_map/ppermute | solution.py:1017
  287.2 3.9 mixed_back.3.do_ref
  291.0 79.9 %attend_back.1 = (bf16[2048,512]{1,0:T(8,128)(2,1)}, bf16[2048,512]{1,0:T(8,128)(2,1)}, bf16[2048,512]{1,0:T(8,128)(2,1)}) custom-call(s32[1]{0:T(128)S(6)} %copy.59.len_ref, bf16[2048,1536]{1,0:T(8,128)(2,1)} %get-tuple-element.77.q_ref.k_ref.v_ref, bf16[2048,1536]{1,0:T(8,128)(2,1)} %get-tuple-element.77.q_ref.k_ref.v_ref, ...), custom_call_target="tpu_custom_call" | custom-call | flops 1048576 | bytes 1048576 | tf_op jit(solution)/shard_map/attend_back/pallas_call | solution.py:262
  370.9 108.1 %tail.1 = (bf16[4096,512]{1,0:T(8,128)(2,1)}, bf16[1024,1024]{1,0:T(8,128)(2,1)}, f32[16,1024]{1,0:T(8,128)}) custom-call(bf16[2048,512]{1,0:T(8,128)(2,1)} %get-tuple-element.105.gq_ref, bf16[2048,512]{1,0:T(8,128)(2,1)} %get-tuple-element.106.gk_ref, bf16[2048,512]{1,0:T(8,128)(2,1)} %get-tuple-element.107.gv_ref, ...), custom_call_target="tpu_custom_call" | custom-call | flops 524288 | bytes 524288 | tf_op jit(solution)/shard_map/tail/pallas_call | solution.py:948
  479.0 5.4 %convert_bitcast_fusion = (f32[512,1024]{0,1:T(8,128)S(1)}, f32[1024,512]{1,0:T(8,128)}, f32[1024,512]{1,0:T(8,128)}, f32[1024,512]{1,0:T(8,128)}) fusion(bf16[4096,512]{1,0:T(8,128)(2,1)} %get-tuple-element.115), kind=kLoop, calls=%fused_computation | loop fusion | flops 2097152 | bytes 12582912 | tf_op jit(solution)/shard_map/convert_element_type | solution.py:1133
  488.7 9.9 %widen.1 = (f32[1024,2048]{1,0:T(8,128)}, f32[2048,1024]{1,0:T(8,128)}) custom-call(bf16[4096,1024]{1,0:T(8,128)(2,1)} %all-reduce.3.cloned.1.call-done.up_ref.down_ref, bf16[4096,1024]{1,0:T(8,128)(2,1)} %all-reduce.3.cloned.1.call-done.up_ref.down_ref), custom_call_target="tpu_custom_call" | custom-call | tf_op jit(solution)/shard_map/widen/pallas_call | solution.py:641
  (72 shorter events, 24.9 us)
Async XLA Ops:
  7.2 144.7 %all-gather.2.cloned.1.call-start = ((), (), s32[]{:S(2)}) async-start(), calls=%async_computation | async-start | bytes 8912896 | tf_op jit(solution)/shard_map/all_gather | solution.py:1089
  7.2 48.8 %collective-permute-start = (bf16[1024,1024]{1,0:T(8,128)(2,1)}, bf16[1024,1024]{1,0:T(8,128)(2,1)S(1)}, u32[]{:S(2)}, u32[]{:S(2)}) collective-permute-start(bf16[1024,1024]{1,0:T(8,128)(2,1)} %bitcast.22), channel_id=1, source_target_pairs={{1,0},{0,1},{3,2},{2,3},{5,4},{4,5},{7,6},{6,7},{9,8},{8,9},{11,10... | collective-permute-start | bytes 6291464 | tf_op jit(solution)/shard_map/ppermute | solution.py:1017
  18.1 39.7 %copy-start.7 = (bf16[2048]{0:T(1024)(128)(2,1)S(1)}, bf16[2048]{0:T(1024)(128)(2,1)}, u32[]{:S(2)}) copy-start(bf16[2048]{0:T(1024)(128)(2,1)} %param.21) | copy-start | bytes 12292
  56.1 2.0 copy-start.2
  56.1 13.2 %collective-permute-start.1 = (bf16[2,128,1024]{2,1,0:T(8,128)(2,1)S(1)}, bf16[2,128,1024]{2,1,0:T(8,128)(2,1)S(1)}, u32[]{:S(2)}, u32[]{:S(2)}) collective-permute-start(bf16[2,128,1024]{2,1,0:T(8,128)(2,1)S(1)} %pad_maximum_fusion.2), channel_id=1, source_target_pairs={{1,0},{0,1},{3,2},{2,3},{5,4},{4,5},{7,6},{6,7},{9,8},{8,9},{11,10... | collective-permute-start | bytes 1572872 | tf_op jit(solution)/shard_map/ppermute | solution.py:1017
  57.8 11.5 %collective-permute-start.2 = (bf16[2048]{0:T(1024)(128)(2,1)S(1)}, bf16[2048]{0:T(1024)(128)(2,1)S(1)}, u32[]{:S(2)}, u32[]{:S(2)}) collective-permute-start(bf16[2048]{0:T(1024)(128)(2,1)S(1)} %copy-done.7), channel_id=1, source_target_pairs={{1,0},{0,1},{3,2},{2,3},{5,4},{4,5},{7,6},{6,7},{9,8},{8,9},{11,10... | collective-permute-start | bytes 12296 | tf_op jit(solution)/shard_map/ppermute | solution.py:1017
  69.3 0.8 copy-start.5
  70.1 418.6 %all-reduce.3.cloned.1.call-start = ((), (), s32[]{:S(2)}) async-start(), calls=%async_computation.1 | async-start | bytes 16777216 | tf_op jit(solution)/shard_map/psum | solution.py:1114
  87.3 32.5 %collective-permute-start.3 = (bf16[512,1024]{1,0:T(8,128)(2,1)}, bf16[512,1024]{1,0:T(8,128)(2,1)S(1)}, u32[]{:S(2)}, u32[]{:S(2)}) collective-permute-start(bf16[512,1024]{1,0:T(8,128)(2,1)} %get-tuple-element.76), channel_id=1, source_target_pairs={{1,0},{0,1},{3,2},{2,3},{5,4},{4,5},{7,6},{6,7},{9,8},{8,9},{11,10... | collective-permute-start | bytes 3145736 | tf_op jit(solution)/shard_map/ppermute | solution.py:1017
  95.5 22.4 %copy-start.11 = (bf16[1024]{0:T(1024)(128)(2,1)S(1)}, bf16[1024]{0:T(1024)(128)(2,1)}, u32[]{:S(2)}) copy-start(bf16[1024]{0:T(1024)(128)(2,1)} %param.23) | copy-start | bytes 6148
  115.8 23.8 %collective-permute-start.4 = (bf16[512,1024]{1,0:T(8,128)(2,1)}, bf16[512,1024]{1,0:T(8,128)(2,1)S(1)}, u32[]{:S(2)}, u32[]{:S(2)}) collective-permute-start(bf16[512,1024]{1,0:T(8,128)(2,1)} %get-tuple-element.84), channel_id=1, source_target_pairs={{1,0},{0,1},{3,2},{2,3},{5,4},{4,5},{7,6},{6,7},{9,8},{8,9},{11,10... | collective-permute-start | bytes 3145736 | tf_op jit(solution)/shard_map/ppermute | solution.py:1017
  119.8 12.5 %copy-start.3 = (bf16[512,1024]{1,0:T(8,128)(2,1)}, bf16[512,1024]{1,0:T(8,128)(2,1)S(1)}, u32[]{:S(2)}) copy-start(bf16[512,1024]{1,0:T(8,128)(2,1)S(1)} %collective-permute-done.3.refs_2_) | copy-start | bytes 3145732
  139.6 1.0 copy-start.4
  149.4 74.6 %collective-permute-start.5 = (bf16[1024,1024]{1,0:T(8,128)(2,1)}, bf16[1024,1024]{1,0:T(8,128)(2,1)S(1)}, u32[]{:S(2)}, u32[]{:S(2)}) collective-permute-start(bf16[1024,1024]{1,0:T(8,128)(2,1)} %get-tuple-element.85.refs_0_.refs_5_), channel_id=1, source_target_pairs={{1,0},{0,1},{3,2},{2,3},{5,4},{4,5},{7,6},{6,7},{9,8},{8,9},{11,10... | collective-permute-start | bytes 6291464 | tf_op jit(solution)/shard_map/ppermute | solution.py:1017
  189.2 54.1 %collective-permute-start.7 = (bf16[1024,1024]{1,0:T(8,128)(2,1)}, bf16[1024,1024]{1,0:T(8,128)(2,1)}, u32[]{:S(2)}, u32[]{:S(2)}) collective-permute-start(bf16[1024,1024]{1,0:T(8,128)(2,1)} %get-tuple-element.91.refs_0_.refs_7_), channel_id=1, source_target_pairs={{1,0},{0,1},{3,2},{2,3},{5,4},{4,5},{7,6},{6,7},{9,8},{8,9},{11,10... | collective-permute-start | bytes 6291464 | tf_op jit(solution)/shard_map/ppermute | solution.py:1017
  224.1 1.3 copy-start.12
  225.4 59.1 %collective-permute-start.6 = (bf16[1024,1024]{1,0:T(8,128)(2,1)}, bf16[1024,1024]{1,0:T(8,128)(2,1)S(1)}, u32[]{:S(2)}, u32[]{:S(2)}) collective-permute-start(bf16[1024,1024]{1,0:T(8,128)(2,1)} %get-tuple-element.96.x_ref.refs_2_), channel_id=1, source_target_pairs={{1,0},{0,1},{3,2},{2,3},{5,4},{4,5},{7,6},{6,7},{9,8},{8,9},{11,10... | collective-permute-start | bytes 6291464 | tf_op jit(solution)/shard_map/ppermute | solution.py:1017
  284.5 1.3 copy-start
  284.5 1.3 copy-start.9
  284.5 1.3 copy-start.8
  284.5 1.4 copy-start.10
  484.4 1.8 copy-start.6
  488.7 9.9 %copy-start.1 = (bf16[1024,1024]{1,0:T(8,128)(2,1)S(1)}, bf16[1024,1024]{1,0:T(8,128)(2,1)}, u32[]{:S(2)}) copy-start(bf16[1024,1024]{1,0:T(8,128)(2,1)} %get-tuple-element.114) | copy-start | bytes 6291460
Sparse Core Ops, SparseCore 0:
  70.2 76.1 all-gather.1
  284.7 203.8 all-reduce.2

commit v7 on v6

--- a/solution.py
+++ b/solution.py
@@ -988,7 +988,7 @@
     refs[-1][...] = dotg(x_ref[...], w_ref[...], NT).astype(BF)
 
 
-def mixed_back(where, x, w_out, slots, held, blk=512):
+def mixed_back(where, x, w_out, slots, held, flops, blk=512):
     rows, depth = x.shape
     width = w_out.shape[0]
     blk = min(blk, rows)
@@ -1008,7 +1008,7 @@
         out_shape=jax.ShapeDtypeStruct((slots, width), BF),
         input_output_aliases={3: 0} if held else {},
         compiler_params=pltpu.CompilerParams(vmem_limit_bytes=60 * MIB),
-        cost_estimate=pl.CostEstimate(flops=rows * depth, bytes_accessed=rows * depth, transcendentals=0),
+        cost_estimate=pl.CostEstimate(flops=flops, bytes_accessed=rows * depth, transcendentals=0),
         name="mixed_back",
     )(where, x, w_out, *held)
 
@@ -1103,17 +1103,17 @@
     )
     g_attn_rest = others(g_attn)
     g_pre, normed_two_rest = lax.optimization_barrier((g_pre, normed_two_rest))
-    g_mixed = mixed_back(here, g_attn, w_out, slots, [])
+    g_mixed = mixed_back(here, g_attn, w_out, slots, [], rows * depth)
     g_pre, g_mixed = lax.optimization_barrier((g_pre, g_mixed))
     grad_feed, bias_up_sum = feed_grad(
         up_weight, down_weight, biases[:hidden], act, g_pre,
         [normed_two] + normed_two_rest, [g_branch] + g_branch_rest,
     )
     grad_feed = grad_feed.reshape(2 * hidden, depth)
-    g_mixed, g_attn_rest, grad_feed = lax.optimization_barrier((g_mixed, g_attn_rest, grad_feed))
     grad_feed = lax.psum(grad_feed, "dp")
+    g_mixed, g_attn_rest, bias_up_sum = lax.optimization_barrier((g_mixed, g_attn_rest, bias_up_sum))
     for r, g in enumerate(g_attn_rest):
-        g_mixed = mixed_back(place(r + 1), g, w_out, slots, [g_mixed])
+        g_mixed = mixed_back(place(r + 1), g, w_out, slots, [g_mixed], 50 * rows * depth * width)
 
     grads = attend_back(lengths, joint, mixed, g_mixed, lse, cosine, sine, width)
     placed = lax.dynamic_update_slice(

time: 516 us -> 520 us (level)
  Pallas kernels: 393 us -> 399 us
    pallas_call x1, Pallas kernels: 108 us -> 115 us  [tail(): pl.pallas_call(functools.partial(tail_kernel, bits=bits, groups=groups, s...]
  transfers between devices with their start and end apart: 10 -> 10, of which waited for: 5 -> 5; matrix products, arithmetic and copies ran while one was open for 5% -> 4% of each run, Pallas kernels for 76% -> 76%
where the time goes in v7:
time: 520 us; the launch traced here: 512 us
  Pallas kernels  399 us (77%)
  waiting for transfers between devices  58.1 us (11%)
  other arithmetic  16 us (3%)
  between operations  15.4 us (3%)
  local copies, waits for them, and re-layouts  12.1 us (2%)
  starting transfers between devices  11.4 us (2%)
    pallas_call x1, Pallas kernels, tail(): pl.pallas_call(functools.partial(tail_kernel, bits=bits, groups=groups, s...  115 us
    pallas_call x1, Pallas kernels, attend_back(): pl.pallas_call(functools.partial(attend_back_kernel, blk=blk, blocks=bloc...  79.7 us
    ppermute x8, waiting for transfers between devices, shift(): lax.ppermute(x, axis, [((i + step) % count, i) for i in range(count)])  58 us
    pallas_call x4, Pallas kernels, attend(): pl.pallas_call(functools.partial(attend_kernel, blk=blk), grid_spec=pltpu...  57.2 us
    pallas_call x1, Pallas kernels, feed(): pl.pallas_call(functools.partial(feed_kernel, groups=groups, chunks=chunk...  37.2 us
    pallas_call x1, Pallas kernels, feed_back(): pl.pallas_call(functools.partial(feed_back_kernel, groups=groups, chunks=...  34.1 us
    pallas_call x1, Pallas kernels, feed_grad(): pl.pallas_call(functools.partial(feed_grad_kernel, groups=groups), grid=(...  33.6 us
    pallas_call x2, Pallas kernels, project(): pl.pallas_call(qkv_kernel, grid_spec=pltpu.PrefetchScalarGridSpec(num_sca...  16.4 us
  transfers between devices with their start and end apart: 10, of which 5 were waited for; matrix products, arithmetic and copies ran while one was open for 4% of the time, Pallas kernels for 76%

profile of v7, /device:TPU:0, one launch (start us, length us, event | category | flops | bytes accessed | tf_op | source)
XLA Modules:
  0.0 512.3 jit_solution(13134897234707895320)
XLA Ops:
  7.2 3.0 collective-permute-start
  11.4 3.7 fusion
  15.1 3.0 pad_maximum_fusion
  18.1 8.2 %project.2 = (bf16[2048,1536]{1,0:T(8,128)(2,1)}, bf16[1024,1024]{1,0:T(8,128)(2,1)}) custom-call(s32[1]{0:T(128)} %bitcast.1.at_ref, bf16[1024,1024]{1,0:T(8,128)(2,1)} %bitcast.23, bf16[1024,512]{1,0:T(8,128)(2,1)} %wq_ref.5, bf16[1024,512]{1,0:T(8,128)(2,1)} %wk_ref.5, bf16[1024,512]{1,0:T(8,128)(2,1)} %wv_ref.5, f32[2048,128]{1,0:T(8,128)} %get-tuple-element.172.cos_ref, ...), custom_call_target="tpu_custom_call" | custom-call | flops 1048576 | bytes 1048576 | tf_op jit(solution)/shard_map/project/pallas_call | solution.py:53
  27.4 28.7 %collective-permute-done.x_ref = bf16[1024,1024]{1,0:T(8,128)(2,1)S(1)} collective-permute-done((bf16[1024,1024]{1,0:T(8,128)(2,1)}, bf16[1024,1024]{1,0:T(8,128)(2,1)S(1)}, u32[]{:S(2)}, u32[]{:S(2)}) %collective-permute-start) | collective-permute-done | bytes 2097184 | tf_op jit(solution)/shard_map/ppermute | solution.py:1017
  58.1 8.2 %project.3 = (bf16[2048,1536]{1,0:T(8,128)(2,1)}, bf16[1024,1024]{1,0:T(8,128)(2,1)}) custom-call(s32[1]{0:T(128)S(6)} %select_n.65.at_ref, bf16[1024,1024]{1,0:T(8,128)(2,1)} %copy-done.1, bf16[1024,512]{1,0:T(8,128)(2,1)} %wq_ref.5, bf16[1024,512]{1,0:T(8,128)(2,1)} %wk_ref.5, bf16[1024,512]{1,0:T(8,128)(2,1)} %wv_ref.5, ...), custom_call_target="tpu_custom_call", output_to_operand_aliasing={{0}: (9, {})} | custom-call | flops 1048576 | bytes 1048576 | tf_op jit(solution)/shard_map/project/pallas_call | solution.py:53
  66.3 3.0 collective-permute-done.2
  71.0 16.2 %attend.4 = (bf16[2048,512]{1,0:T(8,128)(2,1)}, f32[4,2,2048]{2,1,0:T(2,128)}, bf16[512,1024]{1,0:T(8,128)(2,1)}) custom-call(s32[1]{0:T(128)S(6)} %add.75.at_ref, s32[1]{0:T(128)S(6)} %copy.59.len_ref, bf16[2048,1536]{1,0:T(8,128)(2,1)} %get-tuple-element.77.q_ref.k_ref.v_ref, bf16[2048,1536]{1,0:T(8,128)(2,1)} %get-tuple-element.77.q_ref.k_ref.v_ref, ...), custom_call_target="tpu_custom_call" | custom-call | flops 1048576 | bytes 1048576 | tf_op jit(solution)/shard_map/attend/pallas_call | solution.py:153
  87.3 8.2 %attend.5 = (bf16[2048,512]{1,0:T(8,128)(2,1)}, f32[4,2,2048]{2,1,0:T(2,128)}, bf16[512,1024]{1,0:T(8,128)(2,1)}) custom-call(s32[1]{0:T(128)S(6)} %add.73.at_ref, s32[1]{0:T(128)S(6)} %copy.59.len_ref, bf16[2048,1536]{1,0:T(8,128)(2,1)} %get-tuple-element.77.q_ref.k_ref.v_ref, ...), custom_call_target="tpu_custom_call", output_to_operand_aliasing={{0}: (6, {}), {1}: (7, {})} | custom-call | flops 1048576 | bytes 1048576 | tf_op jit(solution)/shard_map/attend/pallas_call | solution.py:153
  95.5 20.3 %attend.6 = (bf16[2048,512]{1,0:T(8,128)(2,1)}, f32[4,2,2048]{2,1,0:T(2,128)}, bf16[512,1024]{1,0:T(8,128)(2,1)}) custom-call(s32[1]{0:T(128)S(6)} %add.77.at_ref, s32[1]{0:T(128)S(6)} %copy.59.len_ref, bf16[2048,1536]{1,0:T(8,128)(2,1)} %get-tuple-element.77.q_ref.k_ref.v_ref, ...), custom_call_target="tpu_custom_call", output_to_operand_aliasing={{0}: (6, {}), {1}: (7, {})} | custom-call | flops 1048576 | bytes 1048576 | tf_op jit(solution)/shard_map/attend/pallas_call | solution.py:153
  119.8 12.5 %attend.7 = (bf16[2048,512]{1,0:T(8,128)(2,1)}, f32[4,2,2048]{2,1,0:T(2,128)}, bf16[512,1024]{1,0:T(8,128)(2,1)}) custom-call(s32[1]{0:T(128)S(6)} %add.76.at_ref, s32[1]{0:T(128)S(6)} %copy.59.len_ref, bf16[2048,1536]{1,0:T(8,128)(2,1)} %get-tuple-element.77.q_ref.k_ref.v_ref, ...), custom_call_target="tpu_custom_call", output_to_operand_aliasing={{0}: (6, {}), {1}: (7, {})} | custom-call | flops 1048576 | bytes 1048576 | tf_op jit(solution)/shard_map/attend/pallas_call | solution.py:153
  132.3 7.3 %collective-permute-done.4.refs_3_ = bf16[512,1024]{1,0:T(8,128)(2,1)S(1)} collective-permute-done((bf16[512,1024]{1,0:T(8,128)(2,1)}, bf16[512,1024]{1,0:T(8,128)(2,1)S(1)}, u32[]{:S(2)}, u32[]{:S(2)}) %collective-permute-start.4) | collective-permute-done | bytes 1048608 | tf_op jit(solution)/shard_map/ppermute | solution.py:1017
  140.6 8.8 %join.1 = (f32[1024,1024]{1,0:T(8,128)}, f32[1024,1024]{1,0:T(8,128)}, bf16[1024,1024]{1,0:T(8,128)(2,1)}) custom-call(s32[4]{0:T(128)} %pad_add_fusion.1.pick_ref, bf16[1024,1024]{1,0:T(8,128)(2,1)} %bitcast.24, f32[4,1024]{1,0:T(4,128)} %gain_ref.7, f32[4,1024]{1,0:T(4,128)} %refs_6_.2, bf16[512,1024]{1,0:T(8,128)(2,1)} %get-tuple-element.75.refs_0_, ...), custom_call_target="tpu_custom_call" | custom-call | tf_op jit(solution)/shard_map/join/pallas_call | solution.py:614
  151.9 37.2 %feed.1 = (bf16[1024,4096]{1,0:T(8,128)(2,1)}, bf16[1024,2048]{1,0:T(8,128)(2,1)}, bf16[1024,1024]{1,0:T(8,128)(2,1)}, bf16[1024,1024]{1,0:T(8,128)(2,1)}, f32[8,1024]{1,0:T(8,128)}) custom-call(s32[2]{0:T(128)} %pad_add_fusion.info_ref, bf16[1024,1024]{1,0:T(8,128)(2,1)} %get-tuple-element.85.refs_0_.refs_5_, f32[4,1,1024]{2,1,0:T(1,128)} %maximum_convert_fusion.refs_1_, ...), custom_call_target="tpu_custom_call" | custom-call | flops 1048576 | bytes 1048576 | tf_op jit(solution)/shard_map/feed/pallas_call | solution.py:400
  190.0 34.1 %feed_back.1 = (bf16[1024,2048]{1,0:T(8,128)(2,1)}, f32[1024,1024]{1,0:T(8,128)}, bf16[1024,1024]{1,0:T(8,128)(2,1)}, f32[8,1024]{1,0:T(8,128)}) custom-call(s32[2]{0:T(128)} %pad_add_fusion.info_ref, bf16[1024,1024]{1,0:T(8,128)(2,1)} %get-tuple-element.91.refs_0_.refs_7_, bf16[1024,4096]{1,0:T(8,128)(2,1)} %get-tuple-element.92.refs_1_, ...), custom_call_target="tpu_custom_call" | custom-call | flops 1048576 | bytes 1048576 | tf_op jit(solution)/shard_map/feed_back/pallas_call | solution.py:501
  227.2 3.9 mixed_back.2.refs_0_
  231.1 12.2 %collective-permute-done.7.refs_8_ = bf16[1024,1024]{1,0:T(8,128)(2,1)} collective-permute-done((bf16[1024,1024]{1,0:T(8,128)(2,1)}, bf16[1024,1024]{1,0:T(8,128)(2,1)}, u32[]{:S(2)}, u32[]{:S(2)}) %collective-permute-start.7) | collective-permute-done | bytes 2097184 | tf_op jit(solution)/shard_map/ppermute | solution.py:1017
  243.3 33.6 %feed_grad.1 = (bf16[2,2048,1024]{2,1,0:T(8,128)(2,1)}, f32[4,1,512]{2,1,0:T(1,128)}) custom-call(bf16[1024,2048]{1,0:T(8,128)(2,1)} %refs_0_.1, bf16[2048,1024]{1,0:T(8,128)(2,1)} %refs_1_.1, f32[4,1,512]{2,1,0:T(1,128)} %bitcast.32, bf16[1024,2048]{1,0:T(8,128)(2,1)} %get-tuple-element.98.refs_3_, bf16[1024,2048]{1,0:T(8,128)(2,1)} %get-tuple-element.99.refs_4_, ...), custom_call_target="tpu_custom_call" | custom-call | flops 25769803776 | bytes 20971520 | tf_op jit(solution)/shard_map/feed_grad/pallas_call | solution.py:569
  277.6 6.9 %collective-permute-done.6.x_ref.refs_3_ = bf16[1024,1024]{1,0:T(8,128)(2,1)S(1)} collective-permute-done((bf16[1024,1024]{1,0:T(8,128)(2,1)}, bf16[1024,1024]{1,0:T(8,128)(2,1)S(1)}, u32[]{:S(2)}, u32[]{:S(2)}) %collective-permute-start.6) | collective-permute-done | bytes 2097184 | tf_op jit(solution)/shard_map/ppermute | solution.py:1017
  285.8 3.9 mixed_back.3.do_ref
  289.7 79.7 %attend_back.1 = (bf16[2048,512]{1,0:T(8,128)(2,1)}, bf16[2048,512]{1,0:T(8,128)(2,1)}, bf16[2048,512]{1,0:T(8,128)(2,1)}) custom-call(s32[1]{0:T(128)S(6)} %copy.59.len_ref, bf16[2048,1536]{1,0:T(8,128)(2,1)} %get-tuple-element.77.q_ref.k_ref.v_ref, bf16[2048,1536]{1,0:T(8,128)(2,1)} %get-tuple-element.77.q_ref.k_ref.v_ref, ...), custom_call_target="tpu_custom_call" | custom-call | flops 1048576 | bytes 1048576 | tf_op jit(solution)/shard_map/attend_back/pallas_call | solution.py:262
  369.4 114.7 %tail.1 = (bf16[4096,512]{1,0:T(8,128)(2,1)}, bf16[1024,1024]{1,0:T(8,128)(2,1)}, f32[16,1024]{1,0:T(8,128)}) custom-call(bf16[2048,512]{1,0:T(8,128)(2,1)} %get-tuple-element.105.gq_ref, bf16[2048,512]{1,0:T(8,128)(2,1)} %get-tuple-element.106.gk_ref, bf16[2048,512]{1,0:T(8,128)(2,1)} %get-tuple-element.107.gv_ref, ...), custom_call_target="tpu_custom_call" | custom-call | flops 524288 | bytes 524288 | tf_op jit(solution)/shard_map/tail/pallas_call | solution.py:948
  484.1 5.4 %convert_bitcast_fusion = (f32[512,1024]{0,1:T(8,128)S(1)}, f32[1024,512]{1,0:T(8,128)}, f32[1024,512]{1,0:T(8,128)}, f32[1024,512]{1,0:T(8,128)}) fusion(bf16[4096,512]{1,0:T(8,128)(2,1)} %get-tuple-element.115), kind=kLoop, calls=%fused_computation | loop fusion | flops 2097152 | bytes 12582912 | tf_op jit(solution)/shard_map/convert_element_type | solution.py:1133
  493.8 9.9 %widen.1 = (f32[1024,2048]{1,0:T(8,128)}, f32[2048,1024]{1,0:T(8,128)}) custom-call(bf16[4096,1024]{1,0:T(8,128)(2,1)} %all-reduce.3.cloned.1.call-done.up_ref.down_ref, bf16[4096,1024]{1,0:T(8,128)(2,1)} %all-reduce.3.cloned.1.call-done.up_ref.down_ref), custom_call_target="tpu_custom_call" | custom-call | tf_op jit(solution)/shard_map/widen/pallas_call | solution.py:641
  (72 shorter events, 24.4 us)
Async XLA Ops:
  7.2 144.7 %all-gather.2.cloned.1.call-start = ((), (), s32[]{:S(2)}) async-start(), calls=%async_computation | async-start | bytes 8912896 | tf_op jit(solution)/shard_map/all_gather | solution.py:1089
  7.2 48.8 %collective-permute-start = (bf16[1024,1024]{1,0:T(8,128)(2,1)}, bf16[1024,1024]{1,0:T(8,128)(2,1)S(1)}, u32[]{:S(2)}, u32[]{:S(2)}) collective-permute-start(bf16[1024,1024]{1,0:T(8,128)(2,1)} %bitcast.22), channel_id=1, source_target_pairs={{1,0},{0,1},{3,2},{2,3},{5,4},{4,5},{7,6},{6,7},{9,8},{8,9},{11,10... | collective-permute-start | bytes 6291464 | tf_op jit(solution)/shard_map/ppermute | solution.py:1017
  18.1 39.7 %copy-start.7 = (bf16[2048]{0:T(1024)(128)(2,1)S(1)}, bf16[2048]{0:T(1024)(128)(2,1)}, u32[]{:S(2)}) copy-start(bf16[2048]{0:T(1024)(128)(2,1)} %param.21) | copy-start | bytes 12292
  56.1 2.0 copy-start.1
  56.1 13.2 %collective-permute-start.1 = (bf16[2,128,1024]{2,1,0:T(8,128)(2,1)S(1)}, bf16[2,128,1024]{2,1,0:T(8,128)(2,1)S(1)}, u32[]{:S(2)}, u32[]{:S(2)}) collective-permute-start(bf16[2,128,1024]{2,1,0:T(8,128)(2,1)S(1)} %pad_maximum_fusion.2), channel_id=1, source_target_pairs={{1,0},{0,1},{3,2},{2,3},{5,4},{4,5},{7,6},{6,7},{9,8},{8,9},{11,10... | collective-permute-start | bytes 1572872 | tf_op jit(solution)/shard_map/ppermute | solution.py:1017
  57.8 11.5 %collective-permute-start.2 = (bf16[2048]{0:T(1024)(128)(2,1)S(1)}, bf16[2048]{0:T(1024)(128)(2,1)S(1)}, u32[]{:S(2)}, u32[]{:S(2)}) collective-permute-start(bf16[2048]{0:T(1024)(128)(2,1)S(1)} %copy-done.7), channel_id=1, source_target_pairs={{1,0},{0,1},{3,2},{2,3},{5,4},{4,5},{7,6},{6,7},{9,8},{8,9},{11,10... | collective-permute-start | bytes 12296 | tf_op jit(solution)/shard_map/ppermute | solution.py:1017
  69.3 0.8 copy-start.5
  70.1 423.7 %all-reduce.3.cloned.1.call-start = ((), (), s32[]{:S(2)}) async-start(), calls=%async_computation.1 | async-start | bytes 16777216 | tf_op jit(solution)/shard_map/psum | solution.py:1113
  87.3 32.5 %collective-permute-start.3 = (bf16[512,1024]{1,0:T(8,128)(2,1)}, bf16[512,1024]{1,0:T(8,128)(2,1)S(1)}, u32[]{:S(2)}, u32[]{:S(2)}) collective-permute-start(bf16[512,1024]{1,0:T(8,128)(2,1)} %get-tuple-element.76), channel_id=1, source_target_pairs={{1,0},{0,1},{3,2},{2,3},{5,4},{4,5},{7,6},{6,7},{9,8},{8,9},{11,10... | collective-permute-start | bytes 3145736 | tf_op jit(solution)/shard_map/ppermute | solution.py:1017
  95.5 22.4 %copy-start.11 = (bf16[1024]{0:T(1024)(128)(2,1)S(1)}, bf16[1024]{0:T(1024)(128)(2,1)}, u32[]{:S(2)}) copy-start(bf16[1024]{0:T(1024)(128)(2,1)} %param.23) | copy-start | bytes 6148
  115.8 23.8 %collective-permute-start.4 = (bf16[512,1024]{1,0:T(8,128)(2,1)}, bf16[512,1024]{1,0:T(8,128)(2,1)S(1)}, u32[]{:S(2)}, u32[]{:S(2)}) collective-permute-start(bf16[512,1024]{1,0:T(8,128)(2,1)} %get-tuple-element.84), channel_id=1, source_target_pairs={{1,0},{0,1},{3,2},{2,3},{5,4},{4,5},{7,6},{6,7},{9,8},{8,9},{11,10... | collective-permute-start | bytes 3145736 | tf_op jit(solution)/shard_map/ppermute | solution.py:1017
  119.8 12.5 %copy-start.3 = (bf16[512,1024]{1,0:T(8,128)(2,1)}, bf16[512,1024]{1,0:T(8,128)(2,1)S(1)}, u32[]{:S(2)}) copy-start(bf16[512,1024]{1,0:T(8,128)(2,1)S(1)} %collective-permute-done.3.refs_2_) | copy-start | bytes 3145732
  139.6 1.0 copy-start.4
  149.4 74.6 %collective-permute-start.5 = (bf16[1024,1024]{1,0:T(8,128)(2,1)}, bf16[1024,1024]{1,0:T(8,128)(2,1)S(1)}, u32[]{:S(2)}, u32[]{:S(2)}) collective-permute-start(bf16[1024,1024]{1,0:T(8,128)(2,1)} %get-tuple-element.85.refs_0_.refs_5_), channel_id=1, source_target_pairs={{1,0},{0,1},{3,2},{2,3},{5,4},{4,5},{7,6},{6,7},{9,8},{8,9},{11,10... | collective-permute-start | bytes 6291464 | tf_op jit(solution)/shard_map/ppermute | solution.py:1017
  189.2 54.1 %collective-permute-start.7 = (bf16[1024,1024]{1,0:T(8,128)(2,1)}, bf16[1024,1024]{1,0:T(8,128)(2,1)}, u32[]{:S(2)}, u32[]{:S(2)}) collective-permute-start(bf16[1024,1024]{1,0:T(8,128)(2,1)} %get-tuple-element.91.refs_0_.refs_7_), channel_id=1, source_target_pairs={{1,0},{0,1},{3,2},{2,3},{5,4},{4,5},{7,6},{6,7},{9,8},{8,9},{11,10... | collective-permute-start | bytes 6291464 | tf_op jit(solution)/shard_map/ppermute | solution.py:1017
  224.1 1.3 copy-start.12
  225.4 59.1 %collective-permute-start.6 = (bf16[1024,1024]{1,0:T(8,128)(2,1)}, bf16[1024,1024]{1,0:T(8,128)(2,1)S(1)}, u32[]{:S(2)}, u32[]{:S(2)}) collective-permute-start(bf16[1024,1024]{1,0:T(8,128)(2,1)} %get-tuple-element.96.x_ref.refs_2_), channel_id=1, source_target_pairs={{1,0},{0,1},{3,2},{2,3},{5,4},{4,5},{7,6},{6,7},{9,8},{8,9},{11,10... | collective-permute-start | bytes 6291464 | tf_op jit(solution)/shard_map/ppermute | solution.py:1017
  276.9 0.8 copy-start.9
  276.9 0.8 copy-start.8
  276.9 7.6 %copy-start.10 = (f32[4,1,512]{2,1,0:T(1,128)S(1)}, f32[4,1,512]{2,1,0:T(1,128)}, u32[]{:S(2)}) copy-start(f32[4,1,512]{2,1,0:T(1,128)} %get-tuple-element.111) | copy-start | bytes 24580
  284.5 1.3 copy-start.2
  489.4 1.8 copy-start.6
  493.8 9.9 %copy-start = (bf16[1024,1024]{1,0:T(8,128)(2,1)S(1)}, bf16[1024,1024]{1,0:T(8,128)(2,1)}, u32[]{:S(2)}) copy-start(bf16[1024,1024]{1,0:T(8,128)(2,1)} %get-tuple-element.114) | copy-start | bytes 6291460
Sparse Core Ops, SparseCore 0:
  70.2 76.1 all-gather.1
  277.0 207.5 all-reduce.2

commit v8 on v6

--- a/solution.py
+++ b/solution.py
@@ -855,7 +855,7 @@
 
     def last_norm(piece):
         wait_all([shares[r, piece] for r in range(1, groups)])
-        blk = min(64, quarter)
+        blk = min(128, quarter)
 
         def body(i, _):
             at = pl.ds(pl.multiple_of(piece * quarter + i * blk, blk), blk)

time: 516 us -> 516 us (level)
  no operation moved by 1% of the time
where the time goes in v8:
time: 516 us; the launch traced here: 507 us
  Pallas kernels  393 us (76%)
  waiting for transfers between devices  58.8 us (11%)
  other arithmetic  16 us (3%)
  between operations  15.4 us (3%)
  local copies, waits for them, and re-layouts  12.6 us (2%)
  starting transfers between devices  11.4 us (2%)
    pallas_call x1, Pallas kernels, tail(): pl.pallas_call(functools.partial(tail_kernel, bits=bits, groups=groups, s...  108 us
    pallas_call x1, Pallas kernels, attend_back(): pl.pallas_call(functools.partial(attend_back_kernel, blk=blk, blocks=bloc...  79.9 us
    ppermute x8, waiting for transfers between devices, shift(): lax.ppermute(x, axis, [((i + step) % count, i) for i in range(count)])  58.8 us
    pallas_call x4, Pallas kernels, attend(): pl.pallas_call(functools.partial(attend_kernel, blk=blk), grid_spec=pltpu...  57.2 us
    pallas_call x1, Pallas kernels, feed(): pl.pallas_call(functools.partial(feed_kernel, groups=groups, chunks=chunk...  37.2 us
    pallas_call x1, Pallas kernels, feed_back(): pl.pallas_call(functools.partial(feed_back_kernel, groups=groups, chunks=...  34.1 us
    pallas_call x1, Pallas kernels, feed_grad(): pl.pallas_call(functools.partial(feed_grad_kernel, groups=groups), grid=(...  33.6 us
    pallas_call x2, Pallas kernels, project(): pl.pallas_call(qkv_kernel, grid_spec=pltpu.PrefetchScalarGridSpec(num_sca...  16.4 us
  transfers between devices with their start and end apart: 10, of which 5 were waited for; matrix products, arithmetic and copies ran while one was open for 5% of the time, Pallas kernels for 76%

profile of v8, /device:TPU:0, one launch (start us, length us, event | category | flops | bytes accessed | tf_op | source)
XLA Modules:
  0.0 507.1 jit_solution(6147545588901441632)
XLA Ops:
  7.2 3.0 collective-permute-start
  11.4 3.7 fusion
  15.1 3.0 pad_maximum_fusion
  18.1 8.2 %project.2 = (bf16[2048,1536]{1,0:T(8,128)(2,1)}, bf16[1024,1024]{1,0:T(8,128)(2,1)}) custom-call(s32[1]{0:T(128)} %bitcast.1.at_ref, bf16[1024,1024]{1,0:T(8,128)(2,1)} %bitcast.23, bf16[1024,512]{1,0:T(8,128)(2,1)} %wq_ref.5, bf16[1024,512]{1,0:T(8,128)(2,1)} %wk_ref.5, bf16[1024,512]{1,0:T(8,128)(2,1)} %wv_ref.5, f32[2048,128]{1,0:T(8,128)} %get-tuple-element.172.cos_ref, ...), custom_call_target="tpu_custom_call" | custom-call | flops 1048576 | bytes 1048576 | tf_op jit(solution)/shard_map/project/pallas_call | solution.py:53
  27.4 28.7 %collective-permute-done.x_ref = bf16[1024,1024]{1,0:T(8,128)(2,1)S(1)} collective-permute-done((bf16[1024,1024]{1,0:T(8,128)(2,1)}, bf16[1024,1024]{1,0:T(8,128)(2,1)S(1)}, u32[]{:S(2)}, u32[]{:S(2)}) %collective-permute-start) | collective-permute-done | bytes 2097184 | tf_op jit(solution)/shard_map/ppermute | solution.py:1017
  58.1 8.2 %project.3 = (bf16[2048,1536]{1,0:T(8,128)(2,1)}, bf16[1024,1024]{1,0:T(8,128)(2,1)}) custom-call(s32[1]{0:T(128)S(6)} %select_n.65.at_ref, bf16[1024,1024]{1,0:T(8,128)(2,1)} %copy-done.2, bf16[1024,512]{1,0:T(8,128)(2,1)} %wq_ref.5, bf16[1024,512]{1,0:T(8,128)(2,1)} %wk_ref.5, bf16[1024,512]{1,0:T(8,128)(2,1)} %wv_ref.5, ...), custom_call_target="tpu_custom_call", output_to_operand_aliasing={{0}: (9, {})} | custom-call | flops 1048576 | bytes 1048576 | tf_op jit(solution)/shard_map/project/pallas_call | solution.py:53
  66.3 3.0 collective-permute-done.2
  71.0 16.2 %attend.4 = (bf16[2048,512]{1,0:T(8,128)(2,1)}, f32[4,2,2048]{2,1,0:T(2,128)}, bf16[512,1024]{1,0:T(8,128)(2,1)}) custom-call(s32[1]{0:T(128)S(6)} %add.75.at_ref, s32[1]{0:T(128)S(6)} %copy.59.len_ref, bf16[2048,1536]{1,0:T(8,128)(2,1)} %get-tuple-element.77.q_ref.k_ref.v_ref, bf16[2048,1536]{1,0:T(8,128)(2,1)} %get-tuple-element.77.q_ref.k_ref.v_ref, ...), custom_call_target="tpu_custom_call" | custom-call | flops 1048576 | bytes 1048576 | tf_op jit(solution)/shard_map/attend/pallas_call | solution.py:153
  87.3 8.2 %attend.5 = (bf16[2048,512]{1,0:T(8,128)(2,1)}, f32[4,2,2048]{2,1,0:T(2,128)}, bf16[512,1024]{1,0:T(8,128)(2,1)}) custom-call(s32[1]{0:T(128)S(6)} %add.73.at_ref, s32[1]{0:T(128)S(6)} %copy.59.len_ref, bf16[2048,1536]{1,0:T(8,128)(2,1)} %get-tuple-element.77.q_ref.k_ref.v_ref, ...), custom_call_target="tpu_custom_call", output_to_operand_aliasing={{0}: (6, {}), {1}: (7, {})} | custom-call | flops 1048576 | bytes 1048576 | tf_op jit(solution)/shard_map/attend/pallas_call | solution.py:153
  95.5 20.3 %attend.6 = (bf16[2048,512]{1,0:T(8,128)(2,1)}, f32[4,2,2048]{2,1,0:T(2,128)}, bf16[512,1024]{1,0:T(8,128)(2,1)}) custom-call(s32[1]{0:T(128)S(6)} %add.77.at_ref, s32[1]{0:T(128)S(6)} %copy.59.len_ref, bf16[2048,1536]{1,0:T(8,128)(2,1)} %get-tuple-element.77.q_ref.k_ref.v_ref, ...), custom_call_target="tpu_custom_call", output_to_operand_aliasing={{0}: (6, {}), {1}: (7, {})} | custom-call | flops 1048576 | bytes 1048576 | tf_op jit(solution)/shard_map/attend/pallas_call | solution.py:153
  119.8 12.5 %attend.7 = (bf16[2048,512]{1,0:T(8,128)(2,1)}, f32[4,2,2048]{2,1,0:T(2,128)}, bf16[512,1024]{1,0:T(8,128)(2,1)}) custom-call(s32[1]{0:T(128)S(6)} %add.76.at_ref, s32[1]{0:T(128)S(6)} %copy.59.len_ref, bf16[2048,1536]{1,0:T(8,128)(2,1)} %get-tuple-element.77.q_ref.k_ref.v_ref, ...), custom_call_target="tpu_custom_call", output_to_operand_aliasing={{0}: (6, {}), {1}: (7, {})} | custom-call | flops 1048576 | bytes 1048576 | tf_op jit(solution)/shard_map/attend/pallas_call | solution.py:153
  132.3 7.3 %collective-permute-done.4.refs_3_ = bf16[512,1024]{1,0:T(8,128)(2,1)S(1)} collective-permute-done((bf16[512,1024]{1,0:T(8,128)(2,1)}, bf16[512,1024]{1,0:T(8,128)(2,1)S(1)}, u32[]{:S(2)}, u32[]{:S(2)}) %collective-permute-start.4) | collective-permute-done | bytes 1048608 | tf_op jit(solution)/shard_map/ppermute | solution.py:1017
  140.6 8.8 %join.1 = (f32[1024,1024]{1,0:T(8,128)}, f32[1024,1024]{1,0:T(8,128)}, bf16[1024,1024]{1,0:T(8,128)(2,1)}) custom-call(s32[4]{0:T(128)} %pad_add_fusion.1.pick_ref, bf16[1024,1024]{1,0:T(8,128)(2,1)} %bitcast.24, f32[4,1024]{1,0:T(4,128)} %gain_ref.7, f32[4,1024]{1,0:T(4,128)} %refs_6_.2, bf16[512,1024]{1,0:T(8,128)(2,1)} %get-tuple-element.75.refs_0_, ...), custom_call_target="tpu_custom_call" | custom-call | tf_op jit(solution)/shard_map/join/pallas_call | solution.py:614
  151.9 37.2 %feed.1 = (bf16[1024,4096]{1,0:T(8,128)(2,1)}, bf16[1024,2048]{1,0:T(8,128)(2,1)}, bf16[1024,1024]{1,0:T(8,128)(2,1)}, bf16[1024,1024]{1,0:T(8,128)(2,1)}, f32[8,1024]{1,0:T(8,128)}) custom-call(s32[2]{0:T(128)} %pad_add_fusion.info_ref, bf16[1024,1024]{1,0:T(8,128)(2,1)} %get-tuple-element.85.refs_0_.refs_5_, f32[4,1,1024]{2,1,0:T(1,128)} %maximum_convert_fusion.refs_1_, ...), custom_call_target="tpu_custom_call" | custom-call | flops 1048576 | bytes 1048576 | tf_op jit(solution)/shard_map/feed/pallas_call | solution.py:400
  190.0 34.1 %feed_back.1 = (bf16[1024,2048]{1,0:T(8,128)(2,1)}, f32[1024,1024]{1,0:T(8,128)}, bf16[1024,1024]{1,0:T(8,128)(2,1)}, f32[8,1024]{1,0:T(8,128)}) custom-call(s32[2]{0:T(128)} %pad_add_fusion.info_ref, bf16[1024,1024]{1,0:T(8,128)(2,1)} %get-tuple-element.91.refs_0_.refs_7_, bf16[1024,4096]{1,0:T(8,128)(2,1)} %get-tuple-element.92.refs_1_, ...), custom_call_target="tpu_custom_call" | custom-call | flops 1048576 | bytes 1048576 | tf_op jit(solution)/shard_map/feed_back/pallas_call | solution.py:501
  227.2 3.9 mixed_back.2.refs_0_
  231.1 12.2 %collective-permute-done.7.refs_8_ = bf16[1024,1024]{1,0:T(8,128)(2,1)} collective-permute-done((bf16[1024,1024]{1,0:T(8,128)(2,1)}, bf16[1024,1024]{1,0:T(8,128)(2,1)}, u32[]{:S(2)}, u32[]{:S(2)}) %collective-permute-start.7) | collective-permute-done | bytes 2097184 | tf_op jit(solution)/shard_map/ppermute | solution.py:1017
  243.3 33.6 %feed_grad.1 = (bf16[2,2048,1024]{2,1,0:T(8,128)(2,1)}, f32[4,1,512]{2,1,0:T(1,128)}) custom-call(bf16[1024,2048]{1,0:T(8,128)(2,1)} %refs_0_.1, bf16[2048,1024]{1,0:T(8,128)(2,1)} %refs_1_.1, f32[4,1,512]{2,1,0:T(1,128)} %bitcast.32, bf16[1024,2048]{1,0:T(8,128)(2,1)} %get-tuple-element.98.refs_3_, bf16[1024,2048]{1,0:T(8,128)(2,1)} %get-tuple-element.99.refs_4_, ...), custom_call_target="tpu_custom_call" | custom-call | flops 25769803776 | bytes 20971520 | tf_op jit(solution)/shard_map/feed_grad/pallas_call | solution.py:569
  276.9 7.6 %collective-permute-done.6.x_ref.refs_3_ = bf16[1024,1024]{1,0:T(8,128)(2,1)S(1)} collective-permute-done((bf16[1024,1024]{1,0:T(8,128)(2,1)}, bf16[1024,1024]{1,0:T(8,128)(2,1)S(1)}, u32[]{:S(2)}, u32[]{:S(2)}) %collective-permute-start.6) | collective-permute-done | bytes 2097184 | tf_op jit(solution)/shard_map/ppermute | solution.py:1017
  287.2 3.9 mixed_back.3.do_ref
  291.0 79.9 %attend_back.1 = (bf16[2048,512]{1,0:T(8,128)(2,1)}, bf16[2048,512]{1,0:T(8,128)(2,1)}, bf16[2048,512]{1,0:T(8,128)(2,1)}) custom-call(s32[1]{0:T(128)S(6)} %copy.59.len_ref, bf16[2048,1536]{1,0:T(8,128)(2,1)} %get-tuple-element.77.q_ref.k_ref.v_ref, bf16[2048,1536]{1,0:T(8,128)(2,1)} %get-tuple-element.77.q_ref.k_ref.v_ref, ...), custom_call_target="tpu_custom_call" | custom-call | flops 1048576 | bytes 1048576 | tf_op jit(solution)/shard_map/attend_back/pallas_call | solution.py:262
  370.9 108.0 %tail.1 = (bf16[4096,512]{1,0:T(8,128)(2,1)}, bf16[1024,1024]{1,0:T(8,128)(2,1)}, f32[16,1024]{1,0:T(8,128)}) custom-call(bf16[2048,512]{1,0:T(8,128)(2,1)} %get-tuple-element.105.gq_ref, bf16[2048,512]{1,0:T(8,128)(2,1)} %get-tuple-element.106.gk_ref, bf16[2048,512]{1,0:T(8,128)(2,1)} %get-tuple-element.107.gv_ref, ...), custom_call_target="tpu_custom_call" | custom-call | flops 524288 | bytes 524288 | tf_op jit(solution)/shard_map/tail/pallas_call | solution.py:948
  478.9 5.4 %convert_bitcast_fusion = (f32[512,1024]{0,1:T(8,128)S(1)}, f32[1024,512]{1,0:T(8,128)}, f32[1024,512]{1,0:T(8,128)}, f32[1024,512]{1,0:T(8,128)}) fusion(bf16[4096,512]{1,0:T(8,128)(2,1)} %get-tuple-element.115), kind=kLoop, calls=%fused_computation | loop fusion | flops 2097152 | bytes 12582912 | tf_op jit(solution)/shard_map/convert_element_type | solution.py:1133
  488.6 9.9 %widen.1 = (f32[1024,2048]{1,0:T(8,128)}, f32[2048,1024]{1,0:T(8,128)}) custom-call(bf16[4096,1024]{1,0:T(8,128)(2,1)} %all-reduce.3.cloned.1.call-done.up_ref.down_ref, bf16[4096,1024]{1,0:T(8,128)(2,1)} %all-reduce.3.cloned.1.call-done.up_ref.down_ref), custom_call_target="tpu_custom_call" | custom-call | tf_op jit(solution)/shard_map/widen/pallas_call | solution.py:641
  (72 shorter events, 24.9 us)
Async XLA Ops:
  7.2 144.7 %all-gather.2.cloned.1.call-start = ((), (), s32[]{:S(2)}) async-start(), calls=%async_computation | async-start | bytes 8912896 | tf_op jit(solution)/shard_map/all_gather | solution.py:1089
  7.2 48.8 %collective-permute-start = (bf16[1024,1024]{1,0:T(8,128)(2,1)}, bf16[1024,1024]{1,0:T(8,128)(2,1)S(1)}, u32[]{:S(2)}, u32[]{:S(2)}) collective-permute-start(bf16[1024,1024]{1,0:T(8,128)(2,1)} %bitcast.22), channel_id=1, source_target_pairs={{1,0},{0,1},{3,2},{2,3},{5,4},{4,5},{7,6},{6,7},{9,8},{8,9},{11,10... | collective-permute-start | bytes 6291464 | tf_op jit(solution)/shard_map/ppermute | solution.py:1017
  18.1 39.7 %copy-start.7 = (bf16[2048]{0:T(1024)(128)(2,1)S(1)}, bf16[2048]{0:T(1024)(128)(2,1)}, u32[]{:S(2)}) copy-start(bf16[2048]{0:T(1024)(128)(2,1)} %param.21) | copy-start | bytes 12292
  56.1 2.0 copy-start.2
  56.1 13.2 %collective-permute-start.1 = (bf16[2,128,1024]{2,1,0:T(8,128)(2,1)S(1)}, bf16[2,128,1024]{2,1,0:T(8,128)(2,1)S(1)}, u32[]{:S(2)}, u32[]{:S(2)}) collective-permute-start(bf16[2,128,1024]{2,1,0:T(8,128)(2,1)S(1)} %pad_maximum_fusion.2), channel_id=1, source_target_pairs={{1,0},{0,1},{3,2},{2,3},{5,4},{4,5},{7,6},{6,7},{9,8},{8,9},{11,10... | collective-permute-start | bytes 1572872 | tf_op jit(solution)/shard_map/ppermute | solution.py:1017
  57.8 11.5 %collective-permute-start.2 = (bf16[2048]{0:T(1024)(128)(2,1)S(1)}, bf16[2048]{0:T(1024)(128)(2,1)S(1)}, u32[]{:S(2)}, u32[]{:S(2)}) collective-permute-start(bf16[2048]{0:T(1024)(128)(2,1)S(1)} %copy-done.7), channel_id=1, source_target_pairs={{1,0},{0,1},{3,2},{2,3},{5,4},{4,5},{7,6},{6,7},{9,8},{8,9},{11,10... | collective-permute-start | bytes 12296 | tf_op jit(solution)/shard_map/ppermute | solution.py:1017
  69.3 0.8 copy-start.5
  70.1 418.5 %all-reduce.3.cloned.1.call-start = ((), (), s32[]{:S(2)}) async-start(), calls=%async_computation.1 | async-start | bytes 16777216 | tf_op jit(solution)/shard_map/psum | solution.py:1114
  87.3 32.5 %collective-permute-start.3 = (bf16[512,1024]{1,0:T(8,128)(2,1)}, bf16[512,1024]{1,0:T(8,128)(2,1)S(1)}, u32[]{:S(2)}, u32[]{:S(2)}) collective-permute-start(bf16[512,1024]{1,0:T(8,128)(2,1)} %get-tuple-element.76), channel_id=1, source_target_pairs={{1,0},{0,1},{3,2},{2,3},{5,4},{4,5},{7,6},{6,7},{9,8},{8,9},{11,10... | collective-permute-start | bytes 3145736 | tf_op jit(solution)/shard_map/ppermute | solution.py:1017
  95.5 22.4 %copy-start.11 = (bf16[1024]{0:T(1024)(128)(2,1)S(1)}, bf16[1024]{0:T(1024)(128)(2,1)}, u32[]{:S(2)}) copy-start(bf16[1024]{0:T(1024)(128)(2,1)} %param.23) | copy-start | bytes 6148
  115.8 23.8 %collective-permute-start.4 = (bf16[512,1024]{1,0:T(8,128)(2,1)}, bf16[512,1024]{1,0:T(8,128)(2,1)S(1)}, u32[]{:S(2)}, u32[]{:S(2)}) collective-permute-start(bf16[512,1024]{1,0:T(8,128)(2,1)} %get-tuple-element.84), channel_id=1, source_target_pairs={{1,0},{0,1},{3,2},{2,3},{5,4},{4,5},{7,6},{6,7},{9,8},{8,9},{11,10... | collective-permute-start | bytes 3145736 | tf_op jit(solution)/shard_map/ppermute | solution.py:1017
  119.8 12.5 %copy-start.3 = (bf16[512,1024]{1,0:T(8,128)(2,1)}, bf16[512,1024]{1,0:T(8,128)(2,1)S(1)}, u32[]{:S(2)}) copy-start(bf16[512,1024]{1,0:T(8,128)(2,1)S(1)} %collective-permute-done.3.refs_2_) | copy-start | bytes 3145732
  139.6 1.0 copy-start.4
  149.4 74.6 %collective-permute-start.5 = (bf16[1024,1024]{1,0:T(8,128)(2,1)}, bf16[1024,1024]{1,0:T(8,128)(2,1)S(1)}, u32[]{:S(2)}, u32[]{:S(2)}) collective-permute-start(bf16[1024,1024]{1,0:T(8,128)(2,1)} %get-tuple-element.85.refs_0_.refs_5_), channel_id=1, source_target_pairs={{1,0},{0,1},{3,2},{2,3},{5,4},{4,5},{7,6},{6,7},{9,8},{8,9},{11,10... | collective-permute-start | bytes 6291464 | tf_op jit(solution)/shard_map/ppermute | solution.py:1017
  189.2 54.1 %collective-permute-start.7 = (bf16[1024,1024]{1,0:T(8,128)(2,1)}, bf16[1024,1024]{1,0:T(8,128)(2,1)}, u32[]{:S(2)}, u32[]{:S(2)}) collective-permute-start(bf16[1024,1024]{1,0:T(8,128)(2,1)} %get-tuple-element.91.refs_0_.refs_7_), channel_id=1, source_target_pairs={{1,0},{0,1},{3,2},{2,3},{5,4},{4,5},{7,6},{6,7},{9,8},{8,9},{11,10... | collective-permute-start | bytes 6291464 | tf_op jit(solution)/shard_map/ppermute | solution.py:1017
  224.1 1.3 copy-start.12
  225.4 59.1 %collective-permute-start.6 = (bf16[1024,1024]{1,0:T(8,128)(2,1)}, bf16[1024,1024]{1,0:T(8,128)(2,1)S(1)}, u32[]{:S(2)}, u32[]{:S(2)}) collective-permute-start(bf16[1024,1024]{1,0:T(8,128)(2,1)} %get-tuple-element.96.x_ref.refs_2_), channel_id=1, source_target_pairs={{1,0},{0,1},{3,2},{2,3},{5,4},{4,5},{7,6},{6,7},{9,8},{8,9},{11,10... | collective-permute-start | bytes 6291464 | tf_op jit(solution)/shard_map/ppermute | solution.py:1017
  284.5 1.3 copy-start
  284.5 1.3 copy-start.9
  284.5 1.3 copy-start.8
  284.5 1.4 copy-start.10
  484.3 1.8 copy-start.6
  488.6 9.9 %copy-start.1 = (bf16[1024,1024]{1,0:T(8,128)(2,1)S(1)}, bf16[1024,1024]{1,0:T(8,128)(2,1)}, u32[]{:S(2)}) copy-start(bf16[1024,1024]{1,0:T(8,128)(2,1)} %get-tuple-element.114) | copy-start | bytes 6291460
Sparse Core Ops, SparseCore 0:
  70.2 76.1 all-gather.1
  284.7 203.8 all-reduce.2
